TPU v7x, 32 devices: a whole 2x2x4 slice. The times are simulated.
32 devices in a mesh: dp: 4 (over y, x), ctx: 8 (over z, core).
Axes of the slice: x: 2, y: 2, z: 4, core: 2. Of those that a mesh axis runs over, the one named last changes fastest.
Arguments:
- tokens: bfloat16 [4, 2048, 768], P('dp', 'ctx'), may hold values from -6 to 6
- segment_ids: int32 [4, 2048], P('dp', 'ctx'), may hold values from 0 to 7, never falling along the last dimension, each value on 1 to 1024 neighbouring positions
- live_blocks: int32 [4, 16, 16], P('dp'), may hold values 0 or 1
- norm1_gain: bfloat16 [768], P(('dp', 'ctx')), may hold values from 0.25 to 1.75
- norm1_bias: bfloat16 [768], P(('dp', 'ctx')), may hold values from -1.5 to 1.5
- qkv_weight: bfloat16 [768, 2304], P(('dp', 'ctx')), may hold values from -0.3125 to 0.3125
- qv_bias: bfloat16 [1536], P(('dp', 'ctx')), may hold values from -2.5 to 2.5
- out_weight: bfloat16 [768, 768], P(('dp', 'ctx')), may hold values from -1.25 to 1.25
- out_bias: bfloat16 [768], P(('dp', 'ctx')), may hold values from -1.5 to 1.5
- norm2_gain: bfloat16 [768], P(('dp', 'ctx')), may hold values from 0.25 to 1.75
- norm2_bias: bfloat16 [768], P(('dp', 'ctx')), may hold values from -1.5 to 1.5
- up_weight: bfloat16 [768, 3072], P(('dp', 'ctx')), may hold values from -0.21875 to 0.21875
- up_bias: bfloat16 [3072], P(('dp', 'ctx')), may hold values from -2.5 to 2.5
- down_weight: bfloat16 [3072, 768], P(('dp', 'ctx')), may hold values from -0.15625 to 0.15625
- down_bias: bfloat16 [768], P(('dp', 'ctx')), may hold values from -1.5 to 1.5
- grad_out: bfloat16 [4, 2048, 768], P('dp', 'ctx'), may hold values from -6 to 6
Outputs:
- output: bfloat16 [4, 2048, 768], P('dp', 'ctx')
- grad_tokens: float32 [4, 2048, 768], P('dp', 'ctx')
- grad_norm1_gain: float32 [768], P(('dp', 'ctx'))
- grad_norm1_bias: float32 [768], P(('dp', 'ctx'))
- grad_qkv_weight: float32 [768, 2304], P(('dp', 'ctx'))
- grad_qv_bias: float32 [1536], P(('dp', 'ctx'))
- grad_out_weight: float32 [768, 768], P(('dp', 'ctx'))
- grad_out_bias: float32 [768], P(('dp', 'ctx'))
- grad_norm2_gain: float32 [768], P(('dp', 'ctx'))
- grad_norm2_bias: float32 [768], P(('dp', 'ctx'))
- grad_up_weight: float32 [768, 3072], P(('dp', 'ctx'))
- grad_up_bias: float32 [3072], P(('dp', 'ctx'))
- grad_down_weight: float32 [3072, 768], P(('dp', 'ctx'))
- grad_down_bias: float32 [768], P(('dp', 'ctx'))
Inputs may be any that keep to these rules, and one draw needn't show every extreme that they name: `segment_ids`: segment numbers never fall along a sequence; a document holds 1 to 1024 positions and one holds exactly 1024.
All inputs are finite; a program needn't handle non-finite values. No bound on the sum of `live_blocks` on one device may be relied on, other than what follows from the above.
Results may differ from a plain program's by a relative error of at most 0.019.
Values may be sent and summed in bfloat16 or wider, within the bound.
No kernel may reach another device: no remote copies, remote signals or barrier semaphores. Data moves between devices by JAX's collectives and lax.ppermute only.
A program may use at most 192 MiB of HBM per device.

v0:
```python
import math

import jax
import jax.numpy as jnp
from jax import lax
from jax.sharding import PartitionSpec as P

HEADS = 12
HEAD_DIM = 64
BLOCK = 128


NEG_FILL = -1e30
SCORE_SCALE = 0.125


def layer_norm(value_in, norm_gain, norm_shift):
    center = value_in - jnp.mean(value_in, axis=-1, keepdims=True)
    spread = jnp.mean(center * center, axis=-1, keepdims=True)
    return center * lax.rsqrt(spread + 1e-05) * norm_gain + norm_shift


def exact_gelu(value_in):
    return jax.nn.gelu(value_in, approximate=False)


def matmul_low(left_side, right_side):
    return jnp.dot(left_side, right_side, preferred_element_type=jnp.float32)


def inner_rows(left_side, right_side):
    return lax.dot_general(
        left_side, right_side, (((0,), (0,)), ((), ())), preferred_element_type=jnp.float32
    )


def times_transpose(left_side, right_side):
    return lax.dot_general(
        left_side, right_side, (((1,), (1,)), ((), ())), preferred_element_type=jnp.float32
    )


def sweep_blocks(count_rows, step_fn, carry_state):
    span_rows = math.gcd(count_rows, 512)
    return lax.fori_loop(
        0,
        count_rows // span_rows,
        lambda loop_index, loop_state: step_fn(loop_index * span_rows, span_rows, loop_state),
        carry_state,
    )


def allowed_pairs(live_table, query_pos, key_pos, query_seg, key_seg):
    block_slots = jnp.arange(live_table.shape[-1], dtype=jnp.int32)
    query_block = query_pos // BLOCK
    key_block = key_pos // BLOCK
    pick_query = (query_block[:, None] == block_slots[None, :]).astype(jnp.bfloat16)
    pick_key = (key_block[:, None] == block_slots[None, :]).astype(jnp.bfloat16)
    live_rows = jnp.einsum(
        "qa,sab->sqb", pick_query, live_table, preferred_element_type=jnp.float32
    )
    live_grid = jnp.einsum(
        "sqb,kb->sqk", live_rows.astype(jnp.bfloat16), pick_key, preferred_element_type=jnp.float32
    )
    same_block = query_block[:, None] == key_block[None, :]
    same_doc = query_seg[:, :, None] == key_seg[:, None, :]
    return same_doc & ((live_grid > 0.5) | same_block[None])


def pair_grads(
    live_table,
    query_heads,
    dout_heads,
    lse_heads,
    delta_heads,
    query_pos,
    query_seg,
    key_heads,
    value_heads,
    key_pos,
    key_seg,
):
    scores = (
        jnp.einsum("sqhd,skhd->shqk", query_heads, key_heads, preferred_element_type=jnp.float32)
        * SCORE_SCALE
    )
    permit = allowed_pairs(live_table, query_pos, key_pos, query_seg, key_seg)[:, None]
    attn_probs = jnp.where(permit, jnp.exp(scores - lse_heads[..., None]), 0.0)
    grad_prob = jnp.einsum(
        "sqhd,skhd->shqk", dout_heads, value_heads, preferred_element_type=jnp.float32
    )
    grad_score = (attn_probs * (grad_prob - delta_heads[..., None])).astype(jnp.bfloat16)
    grad_query = (
        jnp.einsum("shqk,skhd->sqhd", grad_score, key_heads, preferred_element_type=jnp.float32)
        * SCORE_SCALE
    )
    grad_key = (
        jnp.einsum("shqk,sqhd->skhd", grad_score, query_heads, preferred_element_type=jnp.float32)
        * SCORE_SCALE
    )
    grad_value = jnp.einsum(
        "shqk,sqhd->skhd",
        attn_probs.astype(jnp.bfloat16),
        dout_heads,
        preferred_element_type=jnp.float32,
    )
    return (grad_query, grad_key, grad_value)


def local(
    tokens,
    segment_ids,
    live_blocks,
    norm1_gain,
    norm1_bias,
    qkv_weight,
    qv_bias,
    out_weight,
    out_bias,
    norm2_gain,
    norm2_bias,
    up_weight,
    up_bias,
    down_weight,
    down_bias,
    grad_out,
):
    shards = (
        norm1_gain,
        norm1_bias,
        qkv_weight,
        qv_bias,
        out_weight,
        out_bias,
        norm2_gain,
        norm2_bias,
        up_weight,
        up_bias,
        down_weight,
        down_bias,
    )
    gathered = (
        lax.all_gather(shards[0], ("dp", "ctx"), axis=0, tiled=True),
        lax.all_gather(shards[1], ("dp", "ctx"), axis=0, tiled=True),
        lax.all_gather(shards[2], ("dp", "ctx"), axis=0, tiled=True),
        lax.all_gather(shards[3], ("dp", "ctx"), axis=0, tiled=True),
        lax.all_gather(shards[4], ("dp", "ctx"), axis=0, tiled=True),
        lax.all_gather(shards[5], ("dp", "ctx"), axis=0, tiled=True),
        lax.all_gather(shards[6], ("dp", "ctx"), axis=0, tiled=True),
        lax.all_gather(shards[7], ("dp", "ctx"), axis=0, tiled=True),
        lax.all_gather(shards[8], ("dp", "ctx"), axis=0, tiled=True),
        lax.all_gather(shards[9], ("dp", "ctx"), axis=0, tiled=True),
        lax.all_gather(shards[10], ("dp", "ctx"), axis=0, tiled=True),
        lax.all_gather(shards[11], ("dp", "ctx"), axis=0, tiled=True),
    )
    (
        gain_first,
        shift_first,
        full_qkv,
        bias_qv,
        full_out,
        bias_out,
        gain_second,
        shift_second,
        full_up,
        bias_up,
        full_down,
        bias_down,
    ) = gathered
    seq_count, tok_rows, model_width = tokens.shape
    head_count = HEADS
    head_size = HEAD_DIM
    flat_rows = seq_count * tok_rows
    query_pos = lax.axis_index("ctx") * tok_rows + jnp.arange(tok_rows, dtype=jnp.int32)
    live_table = live_blocks.astype(jnp.bfloat16)
    seg_low = segment_ids.astype(jnp.bfloat16)
    inputs_wide = tokens.reshape(flat_rows, model_width).astype(jnp.float32)
    normed_wide, norm_pull_one = jax.vjp(
        layer_norm, inputs_wide, gain_first.astype(jnp.float32), shift_first.astype(jnp.float32)
    )
    normed_one = normed_wide.astype(jnp.bfloat16)
    projected = matmul_low(normed_one, full_qkv)
    bias_wide = bias_qv.astype(jnp.float32)
    query_low = (projected[:, :model_width] + bias_wide[:model_width]).astype(jnp.bfloat16)
    key_low = projected[:, model_width : 2 * model_width].astype(jnp.bfloat16)
    value_low = (projected[:, 2 * model_width :] + bias_wide[model_width:]).astype(jnp.bfloat16)
    query_heads = query_low.reshape(seq_count, tok_rows, head_count, head_size)
    key_seq = key_low.reshape(seq_count, tok_rows, model_width)
    value_seq = value_low.reshape(seq_count, tok_rows, model_width)
    initial = (
        jnp.full((seq_count, head_count, tok_rows), NEG_FILL, jnp.float32),
        jnp.zeros((seq_count, head_count, tok_rows), jnp.float32),
        jnp.zeros((seq_count, tok_rows, head_count, head_size), jnp.float32),
    )
    key_part = lax.all_gather(key_seq, "ctx", axis=1, tiled=True)
    value_part = lax.all_gather(value_seq, "ctx", axis=1, tiled=True)
    seg_part = lax.all_gather(seg_low, "ctx", axis=1, tiled=True)

    def step_fn(offset, span_rows, inner_state):
        run_max, run_total, accum_out = inner_state
        key_heads = lax.dynamic_slice_in_dim(key_part, offset, span_rows, 1).reshape(
            seq_count, span_rows, head_count, head_size
        )
        value_heads = lax.dynamic_slice_in_dim(value_part, offset, span_rows, 1).reshape(
            seq_count, span_rows, head_count, head_size
        )
        key_seg = lax.dynamic_slice_in_dim(seg_part, offset, span_rows, 1)
        key_pos = offset + jnp.arange(span_rows, dtype=jnp.int32)
        scores = (
            jnp.einsum(
                "sqhd,skhd->shqk", query_heads, key_heads, preferred_element_type=jnp.float32
            )
            * SCORE_SCALE
        )
        permit = allowed_pairs(live_table, query_pos, key_pos, seg_low, key_seg)[:, None]
        scores = jnp.where(permit, scores, NEG_FILL)
        new_max = jnp.maximum(run_max, jnp.max(scores, axis=-1))
        exp_scores = jnp.where(permit, jnp.exp(scores - new_max[..., None]), 0.0)
        factor = jnp.exp(run_max - new_max)
        run_total = run_total * factor + jnp.sum(exp_scores, axis=-1)
        weighted = jnp.einsum(
            "shqk,skhd->sqhd",
            exp_scores.astype(jnp.bfloat16),
            value_heads,
            preferred_element_type=jnp.float32,
        )
        accum_out = accum_out * jnp.transpose(factor, (0, 2, 1))[..., None] + weighted
        return (new_max, run_total, accum_out)

    run_max, run_total, accum_out = sweep_blocks(key_part.shape[1], step_fn, initial)
    attn_wide = accum_out / jnp.transpose(run_total, (0, 2, 1))[..., None]
    lse_heads = run_max + jnp.log(run_total)
    attn_low = attn_wide.reshape(flat_rows, model_width).astype(jnp.bfloat16)
    hidden = inputs_wide + matmul_low(attn_low, full_out) + bias_out.astype(jnp.float32)
    normed_two_wide, norm_pull_two = jax.vjp(
        layer_norm, hidden, gain_second.astype(jnp.float32), shift_second.astype(jnp.float32)
    )
    normed_two = normed_two_wide.astype(jnp.bfloat16)
    before = matmul_low(normed_two, full_up) + bias_up.astype(jnp.float32)
    activated_wide, gelu_pull = jax.vjp(exact_gelu, before)
    activated = activated_wide.astype(jnp.bfloat16)
    output = (hidden + matmul_low(activated, full_down) + bias_down.astype(jnp.float32)).astype(
        jnp.bfloat16
    )
    back_params = (
        lax.all_gather(shards[0], ("dp", "ctx"), axis=0, tiled=True),
        lax.all_gather(shards[1], ("dp", "ctx"), axis=0, tiled=True),
        lax.all_gather(shards[2], ("dp", "ctx"), axis=0, tiled=True),
        lax.all_gather(shards[3], ("dp", "ctx"), axis=0, tiled=True),
        lax.all_gather(shards[4], ("dp", "ctx"), axis=0, tiled=True),
        lax.all_gather(shards[5], ("dp", "ctx"), axis=0, tiled=True),
        lax.all_gather(shards[6], ("dp", "ctx"), axis=0, tiled=True),
        lax.all_gather(shards[7], ("dp", "ctx"), axis=0, tiled=True),
        lax.all_gather(shards[8], ("dp", "ctx"), axis=0, tiled=True),
        lax.all_gather(shards[9], ("dp", "ctx"), axis=0, tiled=True),
        lax.all_gather(shards[10], ("dp", "ctx"), axis=0, tiled=True),
        lax.all_gather(shards[11], ("dp", "ctx"), axis=0, tiled=True),
    )
    back_qkv = back_params[2]
    back_out = back_params[4]
    back_up = back_params[8]
    back_down = back_params[10]
    grad_low = grad_out.reshape(flat_rows, model_width)
    grad_down = inner_rows(activated, grad_low)
    grad_bias_down = jnp.sum(grad_low.astype(jnp.float32), axis=0)
    grad_act = times_transpose(grad_low, back_down)
    grad_before = gelu_pull(grad_act)[0].astype(jnp.bfloat16)
    grad_up = inner_rows(normed_two, grad_before)
    grad_bias_up = jnp.sum(grad_before.astype(jnp.float32), axis=0)
    grad_normed_two = times_transpose(grad_before, back_up)
    grad_hidden_part, grad_gain_two, grad_shift_two = norm_pull_two(grad_normed_two)
    grad_hidden = grad_low.astype(jnp.float32) + grad_hidden_part
    grad_branch = grad_hidden.astype(jnp.bfloat16)
    grad_out_full = inner_rows(attn_low, grad_branch)
    grad_bias_out = jnp.sum(grad_branch.astype(jnp.float32), axis=0)
    grad_attn = times_transpose(grad_branch, back_out).astype(jnp.bfloat16)
    dout_heads = grad_attn.reshape(seq_count, tok_rows, head_count, head_size)
    delta_rows = jnp.sum(dout_heads.astype(jnp.float32) * attn_wide, axis=-1)
    delta_heads = jnp.transpose(delta_rows, (0, 2, 1))
    key_all, value_all, seg_all = (
        lax.all_gather(key_seq, "ctx", axis=1, tiled=True),
        lax.all_gather(value_seq, "ctx", axis=1, tiled=True),
        lax.all_gather(seg_low, "ctx", axis=1, tiled=True),
    )

    def key_step(offset, span_rows, inner_state):
        grad_query_acc, grad_key_all, grad_value_all = inner_state
        key_heads = lax.dynamic_slice_in_dim(key_all, offset, span_rows, 1).reshape(
            seq_count, span_rows, head_count, head_size
        )
        value_heads = lax.dynamic_slice_in_dim(value_all, offset, span_rows, 1).reshape(
            seq_count, span_rows, head_count, head_size
        )
        key_seg = lax.dynamic_slice_in_dim(seg_all, offset, span_rows, 1)
        key_pos = offset + jnp.arange(span_rows, dtype=jnp.int32)
        grad_query, grad_key, grad_value = pair_grads(
            live_table,
            query_heads,
            dout_heads,
            lse_heads,
            delta_heads,
            query_pos,
            seg_low,
            key_heads,
            value_heads,
            key_pos,
            key_seg,
        )
        grad_key_all = lax.dynamic_update_slice_in_dim(
            grad_key_all, grad_key.reshape(seq_count, span_rows, model_width), offset, 1
        )
        grad_value_all = lax.dynamic_update_slice_in_dim(
            grad_value_all, grad_value.reshape(seq_count, span_rows, model_width), offset, 1
        )
        return (grad_query_acc + grad_query, grad_key_all, grad_value_all)

    length_rows = key_all.shape[1]
    zero_query = jnp.zeros((seq_count, tok_rows, head_count, head_size), jnp.float32)
    zero_keys = jnp.zeros((seq_count, length_rows, model_width), jnp.float32)
    grad_query_heads, grad_key_all, grad_value_all = sweep_blocks(
        length_rows, key_step, (zero_query, zero_keys, zero_keys)
    )
    grad_key_seq, grad_value_seq = (
        lax.psum_scatter(
            grad_key_all.astype(jnp.bfloat16), "ctx", scatter_dimension=1, tiled=True
        ).astype(jnp.float32),
        lax.psum_scatter(
            grad_value_all.astype(jnp.bfloat16), "ctx", scatter_dimension=1, tiled=True
        ).astype(jnp.float32),
    )
    grad_query_low = grad_query_heads.reshape(flat_rows, model_width).astype(jnp.bfloat16)
    grad_key_low = grad_key_seq.reshape(flat_rows, model_width).astype(jnp.bfloat16)
    grad_value_low = grad_value_seq.reshape(flat_rows, model_width).astype(jnp.bfloat16)
    grad_proj_low = jnp.concatenate([grad_query_low, grad_key_low, grad_value_low], axis=1)
    grad_qkv_full = inner_rows(normed_one, grad_proj_low)
    grad_bias_qv = jnp.concatenate(
        [
            jnp.sum(grad_query_low.astype(jnp.float32), axis=0),
            jnp.sum(grad_value_low.astype(jnp.float32), axis=0),
        ]
    )
    grad_normed_one = times_transpose(grad_proj_low, back_qkv)
    grad_input_part, grad_gain_one, grad_shift_one = norm_pull_one(grad_normed_one)
    grad_tokens = (grad_hidden + grad_input_part).reshape(seq_count, tok_rows, model_width)
    summed = (
        lax.psum_scatter(grad_gain_one, ("dp", "ctx"), scatter_dimension=0, tiled=True),
        lax.psum_scatter(grad_shift_one, ("dp", "ctx"), scatter_dimension=0, tiled=True),
        lax.psum_scatter(grad_qkv_full, ("dp", "ctx"), scatter_dimension=0, tiled=True),
        lax.psum_scatter(grad_bias_qv, ("dp", "ctx"), scatter_dimension=0, tiled=True),
        lax.psum_scatter(grad_out_full, ("dp", "ctx"), scatter_dimension=0, tiled=True),
        lax.psum_scatter(grad_bias_out, ("dp", "ctx"), scatter_dimension=0, tiled=True),
        lax.psum_scatter(grad_gain_two, ("dp", "ctx"), scatter_dimension=0, tiled=True),
        lax.psum_scatter(grad_shift_two, ("dp", "ctx"), scatter_dimension=0, tiled=True),
        lax.psum_scatter(grad_up, ("dp", "ctx"), scatter_dimension=0, tiled=True),
        lax.psum_scatter(grad_bias_up, ("dp", "ctx"), scatter_dimension=0, tiled=True),
        lax.psum_scatter(grad_down, ("dp", "ctx"), scatter_dimension=0, tiled=True),
        lax.psum_scatter(grad_bias_down, ("dp", "ctx"), scatter_dimension=0, tiled=True),
    )
    return (
        output.reshape(seq_count, tok_rows, model_width),
        grad_tokens,
        summed[0],
        summed[1],
        summed[2],
        summed[3],
        summed[4],
        summed[5],
        summed[6],
        summed[7],
        summed[8],
        summed[9],
        summed[10],
        summed[11],
    )


def solution(mesh):
    return jax.shard_map(
        local,
        mesh=mesh,
        in_specs=(
            P("dp", "ctx", None),
            P("dp", "ctx"),
            P("dp", None, None),
            P(("dp", "ctx")),
            P(("dp", "ctx")),
            P(("dp", "ctx"), None),
            P(("dp", "ctx")),
            P(("dp", "ctx"), None),
            P(("dp", "ctx")),
            P(("dp", "ctx")),
            P(("dp", "ctx")),
            P(("dp", "ctx"), None),
            P(("dp", "ctx")),
            P(("dp", "ctx"), None),
            P(("dp", "ctx")),
            P("dp", "ctx", None),
        ),
        out_specs=(
            P("dp", "ctx", None),
            P("dp", "ctx", None),
            P(("dp", "ctx")),
            P(("dp", "ctx")),
            P(("dp", "ctx"), None),
            P(("dp", "ctx")),
            P(("dp", "ctx"), None),
            P(("dp", "ctx")),
            P(("dp", "ctx")),
            P(("dp", "ctx")),
            P(("dp", "ctx"), None),
            P(("dp", "ctx")),
            P(("dp", "ctx"), None),
            P(("dp", "ctx")),
        ),
        check_vma=False,
    )
```

profile of v0, /device:TPU:0, one launch (start us, length us, event | category | flops | bytes accessed | tf_op | source)
XLA Modules:
  0.0 1026.6 jit_solution(8394590929126080544)
XLA Ops:
  14.7 42.9 %all-reduce.17 = (bf16[768]{0:T(1024)(128)(2,1)S(1)}, bf16[768]{0:T(1024)(128)(2,1)S(1)}, bf16[1536]{0:T(1024)(128)(2,1)S(1)}, bf16[768]{0:T(1024)(128)(2,1)S(1)...) all-reduce(bf16[768]{0:T(1024)(128)(2,1)S(1)} %dynamic-update-slice, ...), channel_id=1, replica_groups=mesh['dp'=4,'ctx'=8] {'dp','ctx'}, use_global_device_ids=true, to_apply=%add.1 | all-reduce | flops 9216 | bytes 36864
  60.6 13.6 %all-gather.9.cloned.1.call-done = bf16[768,2304]{1,0:T(8,128)(2,1)} async-done(((bf16[24,2304]{1,0:T(8,128)(2,1)}), bf16[768,2304]{1,0:T(8,128)(2,1)}) %all-gather.9.cloned.1.call-update) | async-done | bytes 3538960 | tf_op jit(solution)/shard_map/all_gather | solution.py:145
  74.2 3.3 fusion.108
  81.2 11.4 %all_gather.52 = bf16[1,2048]{1,0:T(2,128)(2,1)} all-gather(bf16[1,256]{1,0:T(2,128)(2,1)S(1)} %convert_element_type.217), channel_id=1, replica_groups=mesh['dp'=4,'ctx'=8] {'ctx'}, dimensions={1}, use_global_device_ids=true | all-gather | bytes 4608 | tf_op jit(solution)/shard_map/all_gather | solution.py:197
  93.6 22.1 %all-gather.19.cloned.1.call-done = bf16[2048,768]{1,0:T(8,128)(2,1)} async-done(((bf16[256,768]{1,0:T(8,128)(2,1)}), bf16[2048,768]{1,0:T(8,128)(2,1)}) %all-gather.19.cloned.1.call-update) | async-done | bytes 3145744 | tf_op jit(solution)/shard_map/all_gather | solution.py:196
  115.7 4.7 copy.58
  120.4 34.7 %all-gather.17.cloned.1.call-done = bf16[2048,768]{1,0:T(8,128)(2,1)} async-done(((bf16[256,768]{1,0:T(8,128)(2,1)}), bf16[2048,768]{1,0:T(8,128)(2,1)}) %all-gather.17.cloned.1.call-update) | async-done | bytes 3145744 | tf_op jit(solution)/shard_map/all_gather | solution.py:195
  155.1 4.7 copy.57
  159.8 53.7 %while.52 = (s32[]{:T(128)}, f32[1,12,256]{2,1,0:T(8,128)S(1)}, f32[1,12,256]{2,1,0:T(8,128)S(1)}, f32[1,256,12,64]{1,3,2,0:T(8,128)S(1)}, bf16[1,256]{1,0:T(2,1...) while((s32[]{:T(128)}, f32[1,12,256]{2,1,0:T(8,128)S(1)}, ...), condition=%wide.region_5.6_spmd.clone.clone.clone, body=%wide.region_2.5_spmd.clone.clone.clone.sunk | while | flops 428841472 | bytes 51467520 | solution.py:45
  163.2 3.8 fusion.175
  167.0 4.7 fusion.178
  176.5 3.8 fusion.175
  180.4 4.7 fusion.178
  189.9 3.8 fusion.175
  193.8 4.7 fusion.178
  203.4 3.8 fusion.175
  207.2 4.7 fusion.178
  215.9 60.7 %all-gather.13.cloned.1.call-done = bf16[768,3072]{1,0:T(8,128)(2,1)} async-done(((bf16[24,3072]{1,0:T(8,128)(2,1)}), bf16[768,3072]{1,0:T(8,128)(2,1)}) %all-gather.13.cloned.1.call-update) | async-done | bytes 4718608 | tf_op jit(solution)/shard_map/all_gather | solution.py:151
  276.6 11.8 %multiply_convert_fusion = (bf16[256,3072]{1,0:T(8,128)(2,1)}, f32[256,3072]{1,0:T(8,128)}, f32[256,3072]{1,0:T(8,128)}) fusion(f32[3072]{0:T(1024)S(1)} %convert_element_type.235, bf16[768,3072]{1,0:T(8,128)(2,1)} %all-gather.13.cloned.1.call-done, f32[256,768]{1,0:T(8,128)S(1)} %get-tuple-element.1434, f32[768]{0:T(1024)S(1)} %convert_element_type.233, ...), kind=kOutput, calls=%fused_computation.107 | convolution fusion | flops 1260847104 | bytes 13389824 | tf_op jit(solution)/shard_map/dot_general | solution.py:28
  288.3 53.6 %all-gather.15.cloned.1.call-done = bf16[3072,768]{1,0:T(8,128)(2,1)} async-done(((bf16[96,768]{1,0:T(8,128)(2,1)}), bf16[3072,768]{1,0:T(8,128)(2,1)}) %all-gather.15.cloned.1.call-update) | async-done | bytes 4718608 | tf_op jit(solution)/shard_map/all_gather | solution.py:153
  341.9 7.0 convert_reduce_fusion
  348.9 2.2 multiply_reduce_fusion
  357.7 2.1 broadcast_in_dim.147
  359.8 2.0 broadcast_in_dim.147.clone
  361.8 64.2 %while.53 = (s32[]{:T(128)}, f32[1,256,12,64]{1,3,2,0:T(8,128)}, bf16[1,2048,768]{1,2,0:T(8,128)(2,1)}, bf16[1,2048,768]{1,2,0:T(8,128)(2,1)}, bf16[1,2048,768]{...) while((s32[]{:T(128)}, f32[1,256,12,64]{1,3,2,0:T(8,128)}, ...), condition=%wide.region_12.13_spmd.clone.clone.clone, body=%wide.region_11.12_spmd.clone.clone.clone.sunk | while | flops 1028870656 | bytes 45278496 | solution.py:45
  367.1 3.1 fusion.193
  371.3 2.4 fusion.195
  375.0 2.7 fusion.194
  382.9 3.1 fusion.193
  387.1 2.4 fusion.195
  390.9 2.9 fusion.194
  399.1 3.1 fusion.193
  403.3 2.4 fusion.195
  407.0 2.9 fusion.194
  415.2 3.1 fusion.193
  419.4 2.4 fusion.195
  423.1 2.9 fusion.194
  429.4 5.2 fusion.111
  435.6 6.5 fusion.93
  443.4 22.0 %reduce-scatter.7.cloned.1.call-done = bf16[1,256,768]{1,2,0:T(8,128)(2,1)} async-done(((bf16[1,2048,768]{1,2,0:T(8,128)(2,1)}), bf16[1,256,768]{1,2,0:T(8,128)(2,1)}) %reduce-scatter.7.cloned.1.call-update) | async-done | bytes 393232 | tf_op jit(solution)/shard_map/reduce_scatter | solution.py:324
  465.4 41.7 %reduce-scatter.9.cloned.1.call-done = bf16[1,256,768]{1,2,0:T(8,128)(2,1)} async-done(((bf16[1,2048,768]{1,2,0:T(8,128)(2,1)}), bf16[1,256,768]{1,2,0:T(8,128)(2,1)}) %reduce-scatter.9.cloned.1.call-update) | async-done | bytes 393232 | tf_op jit(solution)/shard_map/reduce_scatter | solution.py:327
  507.1 5.3 fusion.91
  513.2 5.1 fusion.74
  521.6 38.7 %all-reduce.16 = (f32[768]{0:T(1024)S(1)}, f32[768]{0:T(1024)S(1)}, f32[1536]{0:T(1024)S(1)}, f32[768]{0:T(1024)S(1)}, f32[768]{0:T(1024)S(1)}, /*index=5*/f32[7...) all-reduce(f32[768]{0:T(1024)S(1)} %get-tuple-element.1340, ...), channel_id=6, replica_groups=mesh['dp'=4,'ctx'=8] {'dp','ctx'}, use_global_device_ids=true, to_apply=%region_18.19.clone | all-reduce | flops 9216 | bytes 73728
  565.0 46.1 %reduce-scatter.13.cloned.1.call-done = f32[24,768]{1,0:T(8,128)} async-done(((f32[768,768]{1,0:T(8,128)}), f32[24,768]{1,0:T(8,128)}) %reduce-scatter.13.cloned.1.call-update) | async-done | bytes 73744 | tf_op jit(solution)/shard_map/reduce_scatter | solution.py:350
  611.1 141.9 %reduce-scatter.15.cloned.1.call-done = f32[24,3072]{1,0:T(8,128)} async-done(((f32[768,3072]{1,0:T(8,128)}), f32[24,3072]{1,0:T(8,128)}) %reduce-scatter.15.cloned.1.call-update) | async-done | bytes 294928 | tf_op jit(solution)/shard_map/reduce_scatter | solution.py:354
  753.1 141.0 %reduce-scatter.17.cloned.1.call-done = f32[96,768]{1,0:T(8,128)} async-done(((f32[3072,768]{1,0:T(8,128)}), f32[96,768]{1,0:T(8,128)}) %reduce-scatter.17.cloned.1.call-update) | async-done | bytes 294928 | tf_op jit(solution)/shard_map/reduce_scatter | solution.py:356
  894.0 125.3 %reduce-scatter.11.cloned.1.call-done = f32[24,2304]{1,0:T(8,128)} async-done(((f32[768,2304]{1,0:T(8,128)}), f32[24,2304]{1,0:T(8,128)}) %reduce-scatter.11.cloned.1.call-update) | async-done | bytes 221200 | tf_op jit(solution)/shard_map/reduce_scatter | solution.py:348
  (288 shorter events, 87.6 us)
Async XLA Ops:
  7.2 67.0 %all-gather.9.cloned.1.call-start = ((), (), s32[]{:S(2)}) async-start(), calls=%async_computation.6 | async-start | bytes 3649536 | tf_op jit(solution)/shard_map/all_gather | solution.py:145
  7.9 107.8 %all-gather.19.cloned.1.call-start = ((), (), s32[]{:S(2)}) async-start(), calls=%async_computation.17 | async-start | bytes 3538944 | tf_op jit(solution)/shard_map/all_gather | solution.py:196
  57.6 19.9 %copy-start.20 = (f32[768]{0:T(1024)}, f32[768]{0:T(1024)S(1)}, u32[]{:S(2)}) copy-start(f32[768]{0:T(1024)S(1)} %convert_element_type.223) | copy-start | bytes 9220
  57.6 19.9 %copy-start.22 = (f32[768]{0:T(1024)}, f32[768]{0:T(1024)S(1)}, u32[]{:S(2)}) copy-start(f32[768]{0:T(1024)S(1)} %convert_element_type.224) | copy-start | bytes 9220
  58.7 18.8 %copy-start.24 = (f32[256]{0:T(256)}, f32[256]{0:T(256)S(1)}, u32[]{:S(2)}) copy-start(f32[256]{0:T(256)S(1)} %broadcast_multiply_fusion.1) | copy-start | bytes 3076
  60.0 17.5 %copy-start.26 = (f32[256]{0:T(256)}, f32[256]{0:T(256)S(1)}, u32[]{:S(2)}) copy-start(f32[256]{0:T(256)S(1)} %fusion.103) | copy-start | bytes 3076
  77.5 3.6 copy-start.39
  77.6 15.1 %copy-start.42 = (s32[1,16,16]{2,1,0:T(8,128)S(1)}, s32[1,16,16]{2,1,0:T(8,128)}, u32[]{:S(2)}) copy-start(s32[1,16,16]{2,1,0:T(8,128)} %param.22) | copy-start | bytes 3076
  78.5 76.6 %all-gather.17.cloned.1.call-start = ((), (), s32[]{:S(2)}) async-start(), calls=%async_computation.16 | async-start | bytes 3538944 | tf_op jit(solution)/shard_map/all_gather | solution.py:195
  79.3 134.3 %all-gather.11.cloned.1.call-start = ((), (), s32[]{:S(2)}) async-start(), calls=%async_computation.7 | async-start | bytes 1216512 | tf_op jit(solution)/shard_map/all_gather | solution.py:147
  79.9 196.7 %all-gather.13.cloned.1.call-start = ((), (), s32[]{:S(2)}) async-start(), calls=%async_computation.8 | async-start | bytes 4866048 | tf_op jit(solution)/shard_map/all_gather | solution.py:151
  80.5 261.5 %all-gather.15.cloned.1.call-start = ((), (), s32[]{:S(2)}) async-start(), calls=%async_computation.9 | async-start | bytes 4866048 | tf_op jit(solution)/shard_map/all_gather | solution.py:153
  81.1 384.3 %reduce-scatter.7.cloned.1.call-start = ((), (), s32[]{:S(2)}) async-start(), calls=%async_computation.10 | async-start | bytes 3538944 | tf_op jit(solution)/shard_map/reduce_scatter | solution.py:324
  159.8 53.8 %copy-start.3 = (bf16[1,256,768]{2,1,0:T(8,128)(2,1)S(1)}, bf16[1,256,768]{2,1,0:T(8,128)(2,1)}, u32[]{:S(2)}) copy-start(bf16[1,256,768]{2,1,0:T(8,128)(2,1)} %param.20) | copy-start | bytes 1179652
  167.0 4.7 copy-start
  180.3 4.7 copy-start
  193.8 4.8 copy-start
  207.2 4.7 copy-start
  213.6 74.8 %copy-start.12 = (bf16[1,256,12,64]{1,3,2,0:T(8,128)(2,1)}, bf16[1,256,12,64]{1,3,2,0:T(8,128)(2,1)S(1)}, u32[]{:S(2)}) copy-start(bf16[1,256,12,64]{1,3,2,0:T(8,128)(2,1)S(1)} %fusion.99) | copy-start | bytes 1179652
  215.6 135.5 %copy-start.5 = (f32[256,768]{1,0:T(8,128)}, f32[256,768]{1,0:T(8,128)S(1)}, u32[]{:S(2)}) copy-start(f32[256,768]{1,0:T(8,128)S(1)} %get-tuple-element.1434) | copy-start | bytes 2359300
  215.8 135.3 %copy-start.29 = (f32[256]{0:T(256)}, f32[256]{0:T(256)S(1)}, u32[]{:S(2)}) copy-start(f32[256]{0:T(256)S(1)} %fusion.104) | copy-start | bytes 3076
  215.8 126.1 %copy-start.10 = (bf16[1,256,768]{2,1,0:T(8,128)(2,1)S(1)}, bf16[1,256,768]{2,1,0:T(8,128)(2,1)}, u32[]{:S(2)}) copy-start(bf16[1,256,768]{2,1,0:T(8,128)(2,1)} %param.35) | copy-start | bytes 1179652
  341.9 7.0 copy-start.40
  348.9 2.2 copy-start.16
  351.1 2.8 copy-start.9
  351.5 8.3 copy-start.34
  426.1 81.0 %reduce-scatter.9.cloned.1.call-start = ((), (), s32[]{:S(2)}) async-start(), calls=%async_computation.11 | async-start | bytes 3538944 | tf_op jit(solution)/shard_map/reduce_scatter | solution.py:327
  426.8 2.5 copy-start.6
  426.8 2.5 copy-start.17
  426.9 2.5 copy-start.30
  426.9 184.3 %reduce-scatter.13.cloned.1.call-start = ((), (), s32[]{:S(2)}) async-start(), calls=%async_computation.13 | async-start | bytes 2433024 | tf_op jit(solution)/shard_map/reduce_scatter | solution.py:350
  429.1 324.0 %reduce-scatter.15.cloned.1.call-start = ((), (), s32[]{:S(2)}) async-start(), calls=%async_computation.14 | async-start | bytes 9732096 | tf_op jit(solution)/shard_map/reduce_scatter | solution.py:354
  434.6 459.4 %reduce-scatter.17.cloned.1.call-start = ((), (), s32[]{:S(2)}) async-start(), calls=%async_computation.15 | async-start | bytes 9732096 | tf_op jit(solution)/shard_map/reduce_scatter | solution.py:356
  442.1 65.0 %copy-start.4 = (bf16[1,256,768]{2,1,0:T(8,128)(2,1)S(1)}, bf16[1,256,768]{2,1,0:T(8,128)(2,1)}, u32[]{:S(2)}) copy-start(bf16[1,256,768]{2,1,0:T(8,128)(2,1)} %param.20) | copy-start | bytes 1179652
  442.1 65.0 %copy-start.21 = (f32[768]{0:T(1024)S(1)}, f32[768]{0:T(1024)}, u32[]{:S(2)}) copy-start(f32[768]{0:T(1024)} %copy-done.20) | copy-start | bytes 9220
  442.1 65.0 %copy-start.23 = (f32[768]{0:T(1024)S(1)}, f32[768]{0:T(1024)}, u32[]{:S(2)}) copy-start(f32[768]{0:T(1024)} %copy-done.22) | copy-start | bytes 9220
  442.1 65.0 %copy-start.25 = (f32[256]{0:T(256)S(1)}, f32[256]{0:T(256)}, u32[]{:S(2)}) copy-start(f32[256]{0:T(256)} %copy-done.24) | copy-start | bytes 3076
  442.1 65.0 %copy-start.27 = (f32[256]{0:T(256)S(1)}, f32[256]{0:T(256)}, u32[]{:S(2)}) copy-start(f32[256]{0:T(256)} %copy-done.26) | copy-start | bytes 3076
  442.2 577.2 %reduce-scatter.11.cloned.1.call-start = ((), (), s32[]{:S(2)}) async-start(), calls=%async_computation.12 | async-start | bytes 7299072 | tf_op jit(solution)/shard_map/reduce_scatter | solution.py:348
  513.2 5.1 copy-start.18
  513.2 5.3 copy-start.19
  513.2 5.3 copy-start.41
  518.5 1.8 copy-start.8
  518.5 1.8 copy-start.35
  519.8 1.8 copy-start.28
  519.8 1.8 copy-start.31
  519.8 1.8 copy-start.36
  519.8 1.8 copy-start.37
  (13 other events, 12.7 us)
Sparse Core Ops, SparseCore 0:
  11.0 63.1 all-gather.8
  78.6 37.0 all-gather.18
  117.9 37.1 all-gather.16
  158.0 53.0 all-gather.10
  213.9 62.5 all-gather.12
  279.4 62.4 all-gather.14
  426.2 39.1 reduce-scatter.6
  467.7 39.3 reduce-scatter.8
  513.0 98.1 reduce-scatter.12
  618.5 134.5 reduce-scatter.14
  759.5 134.4 reduce-scatter.16
  901.1 118.1 reduce-scatter.10
where the time goes:
time: 1030 us
  waiting for transfers between devices  706 us (69%)
  matrix products  137 us (13%)
  blocking collectives  93 us (9%)
  local copies, waits for them, and re-layouts  58.5 us (6%)
  other arithmetic  15.8 us (2%)
  between operations  15.3 us (1%)
    reduce_scatter x1, waiting for transfers between devices, local(): lax.psum_scatter(grad_up, ('dp', 'ctx'), scatter_dimension=0, tiled=True)  142 us
    reduce_scatter x1, waiting for transfers between devices, local(): lax.psum_scatter(grad_down, ('dp', 'ctx'), scatter_dimension=0, tiled=True)  141 us
    reduce_scatter x1, waiting for transfers between devices, local(): lax.psum_scatter(grad_qkv_full, ('dp', 'ctx'), scatter_dimension=0, tiled...  125 us
    unnamed x2, blocking collectives  81.6 us
    all_gather x1, waiting for transfers between devices, local(): lax.all_gather(shards[8], ('dp', 'ctx'), axis=0, tiled=True)  60.7 us
    all_gather x1, waiting for transfers between devices, local(): lax.all_gather(shards[10], ('dp', 'ctx'), axis=0, tiled=True)  53.6 us
    reduce_scatter x1, waiting for transfers between devices, local(): lax.psum_scatter(grad_out_full, ('dp', 'ctx'), scatter_dimension=0, tiled...  46.1 us
    reduce_scatter x1, waiting for transfers between devices, local(): lax.psum_scatter(grad_value_all.astype(jnp.bfloat16), 'ctx', scatter_dime...  41.7 us
  transfers between devices with their start and end apart: 12, of which 11 were waited for; matrix products, arithmetic and copies ran while one was open for 12% of the time, Pallas kernels for 0%

commit v1 on v0

--- a/solution.py
+++ b/solution.py
@@ -345,15 +345,15 @@
     summed = (
         lax.psum_scatter(grad_gain_one, ("dp", "ctx"), scatter_dimension=0, tiled=True),
         lax.psum_scatter(grad_shift_one, ("dp", "ctx"), scatter_dimension=0, tiled=True),
-        lax.psum_scatter(grad_qkv_full, ("dp", "ctx"), scatter_dimension=0, tiled=True),
+        lax.psum_scatter(grad_qkv_full.astype(jnp.bfloat16), ("dp", "ctx"), scatter_dimension=0, tiled=True).astype(jnp.float32),
         lax.psum_scatter(grad_bias_qv, ("dp", "ctx"), scatter_dimension=0, tiled=True),
-        lax.psum_scatter(grad_out_full, ("dp", "ctx"), scatter_dimension=0, tiled=True),
+        lax.psum_scatter(grad_out_full.astype(jnp.bfloat16), ("dp", "ctx"), scatter_dimension=0, tiled=True).astype(jnp.float32),
         lax.psum_scatter(grad_bias_out, ("dp", "ctx"), scatter_dimension=0, tiled=True),
         lax.psum_scatter(grad_gain_two, ("dp", "ctx"), scatter_dimension=0, tiled=True),
         lax.psum_scatter(grad_shift_two, ("dp", "ctx"), scatter_dimension=0, tiled=True),
-        lax.psum_scatter(grad_up, ("dp", "ctx"), scatter_dimension=0, tiled=True),
+        lax.psum_scatter(grad_up.astype(jnp.bfloat16), ("dp", "ctx"), scatter_dimension=0, tiled=True).astype(jnp.float32),
         lax.psum_scatter(grad_bias_up, ("dp", "ctx"), scatter_dimension=0, tiled=True),
-        lax.psum_scatter(grad_down, ("dp", "ctx"), scatter_dimension=0, tiled=True),
+        lax.psum_scatter(grad_down.astype(jnp.bfloat16), ("dp", "ctx"), scatter_dimension=0, tiled=True).astype(jnp.float32),
         lax.psum_scatter(grad_bias_down, ("dp", "ctx"), scatter_dimension=0, tiled=True),
     )
     return (

time: 1030 us -> 953 us (0.925)
  waiting for transfers between devices: 706 us -> 620 us
    reduce_scatter x4, waiting for transfers between devices: 454 us -> 366 us  [the longest x1 111 us: local(): lax.psum_scatter(grad_down.astype(jnp.bfloat16), ('dp', 'ctx'), scatter_d...]
    unnamed x108 -> x106, local copies, waits for them, and re-layouts: 26 us -> 25.2 us
  transfers between devices with their start and end apart: 12 -> 12, of which waited for: 11 -> 11; matrix products, arithmetic and copies ran while one was open for 12% -> 13% of each run, Pallas kernels for 0% -> 0%
where the time goes in v1:
time: 953 us; the launch traced here: 947 us
  waiting for transfers between devices  620 us (65%)
  matrix products  135 us (14%)
  blocking collectives  95.5 us (10%)
  local copies, waits for them, and re-layouts  57.7 us (6%)
  other arithmetic  22.1 us (2%)
  between operations  15.2 us (2%)
    reduce_scatter x1, waiting for transfers between devices, local(): lax.psum_scatter(grad_down.astype(jnp.bfloat16), ('dp', 'ctx'), scatter_d...  111 us
    reduce_scatter x1, waiting for transfers between devices, local(): lax.psum_scatter(grad_qkv_full.astype(jnp.bfloat16), ('dp', 'ctx'), scatt...  106 us
    reduce_scatter x1, waiting for transfers between devices, local(): lax.psum_scatter(grad_out_full.astype(jnp.bfloat16), ('dp', 'ctx'), scatt...  90.4 us
    unnamed x2, blocking collectives  83.9 us
    all_gather x1, waiting for transfers between devices, local(): lax.all_gather(shards[8], ('dp', 'ctx'), axis=0, tiled=True)  60.6 us
    reduce_scatter x1, waiting for transfers between devices, local(): lax.psum_scatter(grad_up.astype(jnp.bfloat16), ('dp', 'ctx'), scatter_dim...  58.9 us
    all_gather x1, waiting for transfers between devices, local(): lax.all_gather(shards[10], ('dp', 'ctx'), axis=0, tiled=True)  53.5 us
    reduce_scatter x1, waiting for transfers between devices, local(): lax.psum_scatter(grad_value_all.astype(jnp.bfloat16), 'ctx', scatter_dime...  41.7 us
  transfers between devices with their start and end apart: 12, of which 11 were waited for; matrix products, arithmetic and copies ran while one was open for 13% of the time, Pallas kernels for 0%

profile of v1, /device:TPU:0, one launch (start us, length us, event | category | flops | bytes accessed | tf_op | source)
XLA Modules:
  0.0 947.0 jit_solution(15682025812178937999)
XLA Ops:
  14.7 42.8 %all-reduce.17 = (bf16[768]{0:T(1024)(128)(2,1)S(1)}, bf16[768]{0:T(1024)(128)(2,1)S(1)}, bf16[1536]{0:T(1024)(128)(2,1)S(1)}, bf16[768]{0:T(1024)(128)(2,1)S(1)...) all-reduce(bf16[768]{0:T(1024)(128)(2,1)S(1)} %dynamic-update-slice, ...), channel_id=1, replica_groups=mesh['dp'=4,'ctx'=8] {'dp','ctx'}, use_global_device_ids=true, to_apply=%add.1 | all-reduce | flops 9216 | bytes 36864
  60.5 13.7 %all-gather.9.cloned.1.call-done = bf16[768,2304]{1,0:T(8,128)(2,1)} async-done(((bf16[24,2304]{1,0:T(8,128)(2,1)}), bf16[768,2304]{1,0:T(8,128)(2,1)}) %all-gather.9.cloned.1.call-update) | async-done | bytes 3538960 | tf_op jit(solution)/shard_map/all_gather | solution.py:145
  74.2 3.3 fusion.106
  81.2 11.6 %all_gather.52 = bf16[1,2048]{1,0:T(2,128)(2,1)} all-gather(bf16[1,256]{1,0:T(2,128)(2,1)S(1)} %convert_element_type.241), channel_id=1, replica_groups=mesh['dp'=4,'ctx'=8] {'ctx'}, dimensions={1}, use_global_device_ids=true | all-gather | bytes 4608 | tf_op jit(solution)/shard_map/all_gather | solution.py:197
  93.8 21.9 %all-gather.19.cloned.1.call-done = bf16[2048,768]{1,0:T(8,128)(2,1)} async-done(((bf16[256,768]{1,0:T(8,128)(2,1)}), bf16[2048,768]{1,0:T(8,128)(2,1)}) %all-gather.19.cloned.1.call-update) | async-done | bytes 3145744 | tf_op jit(solution)/shard_map/all_gather | solution.py:196
  115.7 4.7 copy.58
  120.4 34.7 %all-gather.17.cloned.1.call-done = bf16[2048,768]{1,0:T(8,128)(2,1)} async-done(((bf16[256,768]{1,0:T(8,128)(2,1)}), bf16[2048,768]{1,0:T(8,128)(2,1)}) %all-gather.17.cloned.1.call-update) | async-done | bytes 3145744 | tf_op jit(solution)/shard_map/all_gather | solution.py:195
  155.1 4.7 copy.57
  159.8 53.8 %while.52 = (s32[]{:T(128)}, f32[1,12,256]{2,1,0:T(8,128)S(1)}, f32[1,12,256]{2,1,0:T(8,128)S(1)}, f32[1,256,12,64]{1,3,2,0:T(8,128)S(1)}, bf16[1,256]{1,0:T(2,1...) while((s32[]{:T(128)}, f32[1,12,256]{2,1,0:T(8,128)S(1)}, ...), condition=%wide.region_5.6_spmd.clone.clone.clone, body=%wide.region_2.5_spmd.clone.clone.clone.sunk | while | flops 428841472 | bytes 51467520 | solution.py:45
  163.2 3.8 fusion.171
  167.0 4.7 fusion.174
  176.6 3.8 fusion.171
  180.4 4.7 fusion.174
  190.0 3.8 fusion.171
  193.9 4.7 fusion.174
  203.5 3.8 fusion.171
  207.3 4.7 fusion.174
  216.0 60.6 %all-gather.13.cloned.1.call-done = bf16[768,3072]{1,0:T(8,128)(2,1)} async-done(((bf16[24,3072]{1,0:T(8,128)(2,1)}), bf16[768,3072]{1,0:T(8,128)(2,1)}) %all-gather.13.cloned.1.call-update) | async-done | bytes 4718608 | tf_op jit(solution)/shard_map/all_gather | solution.py:151
  276.6 11.8 %multiply_convert_fusion = (bf16[256,3072]{1,0:T(8,128)(2,1)}, f32[256,3072]{1,0:T(8,128)}, f32[256,3072]{1,0:T(8,128)}) fusion(f32[3072]{0:T(1024)S(1)} %convert_element_type.259, bf16[768,3072]{1,0:T(8,128)(2,1)} %all-gather.13.cloned.1.call-done, f32[256,768]{1,0:T(8,128)S(1)} %get-tuple-element.1434, f32[768]{0:T(1024)S(1)} %convert_element_type.257, ...), kind=kOutput, calls=%fused_computation.110 | convolution fusion | flops 1260847104 | bytes 13389824 | tf_op jit(solution)/shard_map/dot_general | solution.py:28
  288.4 53.5 %all-gather.15.cloned.1.call-done = bf16[3072,768]{1,0:T(8,128)(2,1)} async-done(((bf16[96,768]{1,0:T(8,128)(2,1)}), bf16[3072,768]{1,0:T(8,128)(2,1)}) %all-gather.15.cloned.1.call-update) | async-done | bytes 4718608 | tf_op jit(solution)/shard_map/all_gather | solution.py:153
  342.0 7.0 convert_reduce_fusion
  349.0 2.2 multiply_reduce_fusion
  357.0 2.1 broadcast_in_dim.147
  361.1 64.2 %while.53 = (s32[]{:T(128)}, f32[1,256,12,64]{1,3,2,0:T(8,128)}, bf16[1,2048,768]{1,2,0:T(8,128)(2,1)}, bf16[1,2048,768]{1,2,0:T(8,128)(2,1)}, bf16[1,2048,768]{...) while((s32[]{:T(128)}, f32[1,256,12,64]{1,3,2,0:T(8,128)}, ...), condition=%wide.region_12.13_spmd.clone.clone.clone, body=%wide.region_11.12_spmd.clone.clone.clone.sunk | while | flops 1028870656 | bytes 45278496 | solution.py:45
  366.3 3.1 fusion.189
  370.6 2.4 fusion.191
  374.3 2.7 fusion.190
  382.2 3.1 fusion.189
  386.4 2.4 fusion.191
  390.2 2.9 fusion.190
  398.3 3.1 fusion.189
  402.5 2.4 fusion.191
  406.2 2.9 fusion.190
  414.4 3.1 fusion.189
  418.6 2.4 fusion.191
  422.4 2.9 fusion.190
  428.3 3.7 convolution_convert_fusion.1
  433.0 5.1 convolution_convert_fusion
  439.4 25.2 %reduce-scatter.7.cloned.1.call-done = bf16[1,256,768]{1,2,0:T(8,128)(2,1)} async-done(((bf16[1,2048,768]{1,2,0:T(8,128)(2,1)}), bf16[1,256,768]{1,2,0:T(8,128)(2,1)}) %reduce-scatter.7.cloned.1.call-update) | async-done | bytes 393232 | tf_op jit(solution)/shard_map/reduce_scatter | solution.py:324
  464.6 41.7 %reduce-scatter.9.cloned.1.call-done = bf16[1,256,768]{1,2,0:T(8,128)(2,1)} async-done(((bf16[1,2048,768]{1,2,0:T(8,128)(2,1)}), bf16[1,256,768]{1,2,0:T(8,128)(2,1)}) %reduce-scatter.9.cloned.1.call-update) | async-done | bytes 393232 | tf_op jit(solution)/shard_map/reduce_scatter | solution.py:327
  506.4 4.2 convolution_convert_fusion.2
  511.3 5.0 fusion.74
  516.3 90.4 %reduce-scatter.13.cloned.1.call-done = bf16[24,768]{1,0:T(8,128)(2,1)} async-done(((bf16[768,768]{1,0:T(8,128)(2,1)}), bf16[24,768]{1,0:T(8,128)(2,1)}) %reduce-scatter.13.cloned.1.call-update) | async-done | bytes 36880 | tf_op jit(solution)/shard_map/reduce_scatter | solution.py:350
  608.4 3.3 fusion.109
  613.6 41.1 %all-reduce.16 = (f32[768]{0:T(1024)S(1)}, f32[768]{0:T(1024)S(1)}, f32[1536]{0:T(1024)S(1)}, f32[768]{0:T(1024)S(1)}, f32[768]{0:T(1024)S(1)}, /*index=5*/f32[7...) all-reduce(f32[768]{0:T(1024)S(1)} %get-tuple-element.1340, ...), channel_id=6, replica_groups=mesh['dp'=4,'ctx'=8] {'dp','ctx'}, use_global_device_ids=true, to_apply=%region_18.19.clone | all-reduce | flops 9216 | bytes 73728
  659.3 58.9 %reduce-scatter.15.cloned.1.call-done = bf16[24,3072]{1,0:T(8,128)(2,1)} async-done(((bf16[768,3072]{1,0:T(8,128)(2,1)}), bf16[24,3072]{1,0:T(8,128)(2,1)}) %reduce-scatter.15.cloned.1.call-update) | async-done | bytes 147472 | tf_op jit(solution)/shard_map/reduce_scatter | solution.py:354
  719.8 110.8 %reduce-scatter.17.cloned.1.call-done = bf16[96,768]{1,0:T(8,128)(2,1)} async-done(((bf16[3072,768]{1,0:T(8,128)(2,1)}), bf16[96,768]{1,0:T(8,128)(2,1)}) %reduce-scatter.17.cloned.1.call-update) | async-done | bytes 147472 | tf_op jit(solution)/shard_map/reduce_scatter | solution.py:356
  832.3 105.8 %reduce-scatter.11.cloned.1.call-done = bf16[24,2304]{1,0:T(8,128)(2,1)} async-done(((bf16[768,2304]{1,0:T(8,128)(2,1)}), bf16[24,2304]{1,0:T(8,128)(2,1)}) %reduce-scatter.11.cloned.1.call-update) | async-done | bytes 110608 | tf_op jit(solution)/shard_map/reduce_scatter | solution.py:348
  (290 shorter events, 93.5 us)
Async XLA Ops:
  7.2 67.0 %all-gather.9.cloned.1.call-start = ((), (), s32[]{:S(2)}) async-start(), calls=%async_computation.6 | async-start | bytes 3649536 | tf_op jit(solution)/shard_map/all_gather | solution.py:145
  7.9 107.8 %all-gather.19.cloned.1.call-start = ((), (), s32[]{:S(2)}) async-start(), calls=%async_computation.17 | async-start | bytes 3538944 | tf_op jit(solution)/shard_map/all_gather | solution.py:196
  57.5 20.0 %copy-start.19 = (f32[768]{0:T(1024)}, f32[768]{0:T(1024)S(1)}, u32[]{:S(2)}) copy-start(f32[768]{0:T(1024)S(1)} %convert_element_type.247) | copy-start | bytes 9220
  57.6 20.0 %copy-start.33 = (f32[768]{0:T(1024)}, f32[768]{0:T(1024)S(1)}, u32[]{:S(2)}) copy-start(f32[768]{0:T(1024)S(1)} %convert_element_type.248) | copy-start | bytes 9220
  58.7 18.8 %copy-start.21 = (f32[256]{0:T(256)}, f32[256]{0:T(256)S(1)}, u32[]{:S(2)}) copy-start(f32[256]{0:T(256)S(1)} %broadcast_multiply_fusion.1) | copy-start | bytes 3076
  60.5 17.1 %copy-start.27 = (f32[256]{0:T(256)}, f32[256]{0:T(256)S(1)}, u32[]{:S(2)}) copy-start(f32[256]{0:T(256)S(1)} %fusion.101) | copy-start | bytes 3076
  77.5 3.6 copy-start.38
  77.6 15.2 %copy-start.41 = (s32[1,16,16]{2,1,0:T(8,128)S(1)}, s32[1,16,16]{2,1,0:T(8,128)}, u32[]{:S(2)}) copy-start(s32[1,16,16]{2,1,0:T(8,128)} %param.22) | copy-start | bytes 3076
  78.5 76.7 %all-gather.17.cloned.1.call-start = ((), (), s32[]{:S(2)}) async-start(), calls=%async_computation.16 | async-start | bytes 3538944 | tf_op jit(solution)/shard_map/all_gather | solution.py:195
  79.3 134.4 %all-gather.11.cloned.1.call-start = ((), (), s32[]{:S(2)}) async-start(), calls=%async_computation.7 | async-start | bytes 1216512 | tf_op jit(solution)/shard_map/all_gather | solution.py:147
  79.9 196.7 %all-gather.13.cloned.1.call-start = ((), (), s32[]{:S(2)}) async-start(), calls=%async_computation.8 | async-start | bytes 4866048 | tf_op jit(solution)/shard_map/all_gather | solution.py:151
  80.5 261.5 %all-gather.15.cloned.1.call-start = ((), (), s32[]{:S(2)}) async-start(), calls=%async_computation.9 | async-start | bytes 4866048 | tf_op jit(solution)/shard_map/all_gather | solution.py:153
  81.1 383.6 %reduce-scatter.7.cloned.1.call-start = ((), (), s32[]{:S(2)}) async-start(), calls=%async_computation.10 | async-start | bytes 3538944 | tf_op jit(solution)/shard_map/reduce_scatter | solution.py:324
  159.8 53.9 %copy-start.5 = (bf16[1,256,768]{2,1,0:T(8,128)(2,1)S(1)}, bf16[1,256,768]{2,1,0:T(8,128)(2,1)}, u32[]{:S(2)}) copy-start(bf16[1,256,768]{2,1,0:T(8,128)(2,1)} %param.20) | copy-start | bytes 1179652
  167.0 4.7 copy-start
  180.4 4.7 copy-start
  193.8 4.8 copy-start
  207.3 4.7 copy-start
  213.7 74.7 %copy-start.12 = (bf16[1,256,12,64]{1,3,2,0:T(8,128)(2,1)}, bf16[1,256,12,64]{1,3,2,0:T(8,128)(2,1)S(1)}, u32[]{:S(2)}) copy-start(bf16[1,256,12,64]{1,3,2,0:T(8,128)(2,1)S(1)} %fusion.97) | copy-start | bytes 1179652
  215.7 135.5 %copy-start.3 = (f32[256,768]{1,0:T(8,128)}, f32[256,768]{1,0:T(8,128)S(1)}, u32[]{:S(2)}) copy-start(f32[256,768]{1,0:T(8,128)S(1)} %get-tuple-element.1434) | copy-start | bytes 2359300
  216.0 135.2 %copy-start.24 = (f32[256]{0:T(256)}, f32[256]{0:T(256)S(1)}, u32[]{:S(2)}) copy-start(f32[256]{0:T(256)S(1)} %fusion.102) | copy-start | bytes 3076
  216.0 126.0 %copy-start.10 = (bf16[1,256,768]{2,1,0:T(8,128)(2,1)S(1)}, bf16[1,256,768]{2,1,0:T(8,128)(2,1)}, u32[]{:S(2)}) copy-start(bf16[1,256,768]{2,1,0:T(8,128)(2,1)} %param.35) | copy-start | bytes 1179652
  342.0 7.0 copy-start.39
  349.0 2.2 copy-start.16
  351.2 2.0 copy-start.9
  351.5 7.5 copy-start.31
  353.2 5.9 copy-start.14
  425.3 81.0 %reduce-scatter.9.cloned.1.call-start = ((), (), s32[]{:S(2)}) async-start(), calls=%async_computation.11 | async-start | bytes 3538944 | tf_op jit(solution)/shard_map/reduce_scatter | solution.py:327
  425.4 2.9 copy-start.4
  425.4 2.8 copy-start.17
  425.4 2.8 copy-start.25
  426.1 180.7 %reduce-scatter.13.cloned.1.call-start = ((), (), s32[]{:S(2)}) async-start(), calls=%async_computation.13 | async-start | bytes 1216512 | tf_op jit(solution)/shard_map/reduce_scatter | solution.py:350
  427.9 290.2 %reduce-scatter.15.cloned.1.call-start = ((), (), s32[]{:S(2)}) async-start(), calls=%async_computation.14 | async-start | bytes 4866048 | tf_op jit(solution)/shard_map/reduce_scatter | solution.py:354
  432.0 398.6 %reduce-scatter.17.cloned.1.call-start = ((), (), s32[]{:S(2)}) async-start(), calls=%async_computation.15 | async-start | bytes 4866048 | tf_op jit(solution)/shard_map/reduce_scatter | solution.py:356
  438.1 68.3 %copy-start.6 = (bf16[1,256,768]{2,1,0:T(8,128)(2,1)S(1)}, bf16[1,256,768]{2,1,0:T(8,128)(2,1)}, u32[]{:S(2)}) copy-start(bf16[1,256,768]{2,1,0:T(8,128)(2,1)} %param.20) | copy-start | bytes 1179652
  438.1 68.3 %copy-start.20 = (f32[768]{0:T(1024)S(1)}, f32[768]{0:T(1024)}, u32[]{:S(2)}) copy-start(f32[768]{0:T(1024)} %copy-done.19) | copy-start | bytes 9220
  438.1 68.3 %copy-start.22 = (f32[256]{0:T(256)S(1)}, f32[256]{0:T(256)}, u32[]{:S(2)}) copy-start(f32[256]{0:T(256)} %copy-done.21) | copy-start | bytes 3076
  438.1 68.3 %copy-start.28 = (f32[256]{0:T(256)S(1)}, f32[256]{0:T(256)}, u32[]{:S(2)}) copy-start(f32[256]{0:T(256)} %copy-done.27) | copy-start | bytes 3076
  438.1 68.3 %copy-start.34 = (f32[768]{0:T(1024)S(1)}, f32[768]{0:T(1024)}, u32[]{:S(2)}) copy-start(f32[768]{0:T(1024)} %copy-done.33) | copy-start | bytes 9220
  438.1 499.9 %reduce-scatter.11.cloned.1.call-start = ((), (), s32[]{:S(2)}) async-start(), calls=%async_computation.12 | async-start | bytes 3649536 | tf_op jit(solution)/shard_map/reduce_scatter | solution.py:348
  511.3 96.8 %copy-start.18 = (bf16[1,256,768]{1,2,0:T(8,128)(2,1)S(1)}, bf16[1,256,768]{1,2,0:T(8,128)(2,1)}, u32[]{:S(2)}) copy-start(bf16[1,256,768]{1,2,0:T(8,128)(2,1)} %reduce-scatter.9.cloned.1.call-done) | copy-start | bytes 1179652
  511.3 97.0 %copy-start.40 = (bf16[1,256,768]{1,2,0:T(8,128)(2,1)S(1)}, bf16[1,256,768]{1,2,0:T(8,128)(2,1)}, u32[]{:S(2)}) copy-start(bf16[1,256,768]{1,2,0:T(8,128)(2,1)} %reduce-scatter.7.cloned.1.call-done) | copy-start | bytes 1179652
  608.3 3.4 copy-start.30
  608.4 3.9 copy-start.8
  608.4 3.9 copy-start.32
  611.7 1.9 copy-start.23
  611.7 1.9 copy-start.26
  611.7 1.8 copy-start.35
  (12 other events, 12.3 us)
Sparse Core Ops, SparseCore 0:
  11.1 63.0 all-gather.8
  78.6 37.0 all-gather.18
  117.9 37.1 all-gather.16
  158.0 53.0 all-gather.10
  213.9 62.6 all-gather.12
  279.5 62.4 all-gather.14
  425.4 39.1 reduce-scatter.6
  466.9 39.3 reduce-scatter.8
  511.5 95.2 reduce-scatter.12
  612.1 106.0 reduce-scatter.14
  724.5 106.0 reduce-scatter.16
  835.9 102.1 reduce-scatter.10

commit v2 on v1

--- a/solution.py
+++ b/solution.py
@@ -3,7 +3,9 @@
 import jax
 import jax.numpy as jnp
 from jax import lax
-from jax.sharding import PartitionSpec as P
+from jax.experimental import pallas as pl
+from jax.experimental.pallas import tpu as pltpu
+from jax.sharding import Mesh, PartitionSpec as P
 
 HEADS = 12
 HEAD_DIM = 64
@@ -374,43 +376,485 @@
     )
 
 
-def solution(mesh):
+NZ = 4
+GROUP = HEADS // NZ
+GW = GROUP * HEAD_DIM
+CHUNK = 256
+
+
+def pick(array, index, axis=0):
+    return lax.dynamic_index_in_dim(array, index, axis, keepdims=False)
+
+
+def shift(array, axis, size, hop):
+    return lax.ppermute(array, axis, [(i, (i + hop) % size) for i in range(size)])
+
+
+def swap(array, axis):
+    return shift(array, axis, 2, 1)
+
+
+def in_order(own, received, index, axis):
+    first = jnp.where(index == 0, own, received)
+    second = jnp.where(index == 0, received, own)
+    return jnp.stack([first, second], axis=axis)
+
+
+def z_spread(block, z):
+    up = lax.ppermute(block, "z", [(0, 1), (1, 2), (2, 3)])
+    down = lax.ppermute(block, "z", [(1, 0), (2, 1), (3, 2)])
+    far = shift(block, "z", NZ, 2)
+    last = lax.ppermute(far, "z", [(2, 3), (1, 0)])
+    return jnp.stack(
+        [
+            lax.select_n(z, block, up, far, last),
+            lax.select_n(z, down, block, up, far),
+            lax.select_n(z, far, down, block, up),
+            lax.select_n(z, last, far, down, block),
+        ]
+    )
+
+
+def z_order(pieces, z):
+    return jnp.stack([lax.select_n((z - a) % NZ, *pieces) for a in range(NZ)])
+
+
+def z_exchange(array, z):
+    return [pick(array, z)] + [shift(pick(array, (z + j) % NZ), "z", NZ, j) for j in range(1, NZ)]
+
+
+def xy_gather(line, y, x):
+    a, b = line[:2], line[2:]
+    a = in_order(a, swap(a, "x"), x, 0)
+    b = in_order(b, swap(b, "y"), y, 0)
+    a = in_order(a, swap(a, "y"), y, 0)
+    b = in_order(b, swap(b, "x"), x, 1)
+    return jnp.concatenate([a, b], axis=2)
+
+
+def xy_scatter(blocks, y, x, wire):
+    def halve(array, axis, name, index):
+        sent = swap(pick(array, 1 - index, axis).astype(wire), name)
+        return pick(array, index, axis).astype(jnp.float32) + sent.astype(jnp.float32)
+
+    a, b = blocks[:, :, :2], blocks[:, :, 2:]
+    a = halve(a, 0, "y", y)
+    b = halve(b, 1, "x", x)
+    a = halve(a, 0, "x", x)
+    b = halve(b, 0, "y", y)
+    return jnp.concatenate([a, b], axis=0)
+
+
+def z_collect(line, z, wire):
+    own, *rest = z_exchange_wide(line, z, wire)
+    total = own.astype(jnp.float32)
+    for piece in rest:
+        total = total + piece.astype(jnp.float32)
+    return total
+
+
+def z_exchange_wide(array, z, wire):
+    return [pick(array, z)] + [
+        shift(pick(array, (z + j) % NZ).astype(wire), "z", NZ, j) for j in range(1, NZ)
+    ]
+
+
+def norm_stats(values):
+    center = values - jnp.mean(values, axis=-1, keepdims=True)
+    scale = lax.rsqrt(jnp.mean(center * center, axis=-1, keepdims=True) + 1e-05)
+    return center * scale, scale
+
+
+def norm_back(grad, gain, unit, scale):
+    c = grad * gain
+    return scale * (
+        c - jnp.mean(c, axis=-1, keepdims=True) - unit * jnp.mean(c * unit, axis=-1, keepdims=True)
+    )
+
+
+def dot_nt(a, b):
+    return lax.dot_general(a, b, (((1,), (1,)), ((), ())), preferred_element_type=jnp.float32)
+
+
+def dot_tn(a, b):
+    return lax.dot_general(a, b, (((0,), (0,)), ((), ())), preferred_element_type=jnp.float32)
+
+
+def dot_nn(a, b):
+    return lax.dot_general(a, b, (((1,), (0,)), ((), ())), preferred_element_type=jnp.float32)
+
+
+def attend_kernel(
+    act_ref, q_ref, kv_ref, qseg_ref, kseg_ref, o_ref, low_ref, lse_ref, k_s, v_s, m_s, l_s, acc_s
+):
+    i = pl.program_id(0)
+    chunks = kv_ref.shape[0] // CHUNK
+
+    @pl.when(i == 0)
+    def _():
+        for h in range(GROUP):
+            k_s[h] = kv_ref[:, HEAD_DIM * h : HEAD_DIM * (h + 1)]
+            v_s[h] = kv_ref[:, GW + HEAD_DIM * h : GW + HEAD_DIM * (h + 1)]
+
+    m_s[...] = jnp.full(m_s.shape, NEG_FILL, jnp.float32)
+    l_s[...] = jnp.zeros(l_s.shape, jnp.float32)
+    acc_s[...] = jnp.zeros(acc_s.shape, jnp.float32)
+    q_heads = [q_ref[:, HEAD_DIM * h : HEAD_DIM * (h + 1)] for h in range(GROUP)]
+    q_seg = qseg_ref[...]
+
+    def one_chunk(j, carry):
+        @pl.when(act_ref[i, j] != 0)
+        def _():
+            at = pl.ds(pl.multiple_of(j * CHUNK, CHUNK), CHUNK)
+            permit = q_seg == kseg_ref[0, :, at]
+            for h in range(GROUP):
+                s = jnp.where(permit, dot_nt(q_heads[h], k_s[h, at]), NEG_FILL)
+                old = m_s[h]
+                new = jnp.maximum(old, jnp.max(s, axis=-1, keepdims=True))
+                p = jnp.exp(s - new)
+                fade = jnp.exp(old - new)
+                l_s[h] = l_s[h] * fade + jnp.sum(p, axis=-1, keepdims=True)
+                acc_s[h] = acc_s[h] * fade + dot_nn(p.astype(jnp.bfloat16), v_s[h, at])
+                m_s[h] = new
+
+        return carry
+
+    lax.fori_loop(0, chunks, one_chunk, 0)
+    rows = q_ref.shape[0]
+    outs, logs = [], []
+    for h in range(GROUP):
+        outs.append(acc_s[h] / l_s[h])
+        lse = m_s[h] + jnp.log(l_s[h])
+        logs.append(jnp.transpose(jnp.broadcast_to(lse, (rows, rows)))[0:1])
+    out = jnp.concatenate(outs, axis=1)
+    o_ref[...] = out
+    low_ref[...] = out.astype(jnp.bfloat16)
+    lse_ref[...] = jnp.concatenate(logs + [logs[0]] * (8 - GROUP), axis=0)
+
+
+def attend(active, q, kv, q_seg, k_seg):
+    rows, keys = q.shape[0], kv.shape[0]
+    grid = rows // BLOCK
+    return pl.pallas_call(
+        attend_kernel,
+        out_shape=(
+            jax.ShapeDtypeStruct((rows, GW), jnp.float32),
+            jax.ShapeDtypeStruct((rows, GW), jnp.bfloat16),
+            jax.ShapeDtypeStruct((8, rows), jnp.float32),
+        ),
+        grid_spec=pltpu.PrefetchScalarGridSpec(
+            num_scalar_prefetch=1,
+            grid=(grid,),
+            in_specs=[
+                pl.BlockSpec((BLOCK, GW), lambda i, t: (i, 0)),
+                pl.BlockSpec((keys, 2 * GW), lambda i, t: (0, 0)),
+                pl.BlockSpec((BLOCK, 1), lambda i, t: (i, 0)),
+                pl.BlockSpec((1, 1, keys), lambda i, t: (i, 0, 0)),
+            ],
+            out_specs=[
+                pl.BlockSpec((BLOCK, GW), lambda i, t: (i, 0)),
+                pl.BlockSpec((BLOCK, GW), lambda i, t: (i, 0)),
+                pl.BlockSpec((8, BLOCK), lambda i, t: (0, i)),
+            ],
+            scratch_shapes=[
+                pltpu.VMEM((GROUP, keys, HEAD_DIM), jnp.bfloat16),
+                pltpu.VMEM((GROUP, keys, HEAD_DIM), jnp.bfloat16),
+                pltpu.VMEM((GROUP, BLOCK, 1), jnp.float32),
+                pltpu.VMEM((GROUP, BLOCK, 1), jnp.float32),
+                pltpu.VMEM((GROUP, BLOCK, HEAD_DIM), jnp.float32),
+            ],
+        ),
+        compiler_params=pltpu.CompilerParams(vmem_limit_bytes=32 << 20),
+        cost_estimate=pl.CostEstimate(
+            flops=2 * rows * keys * GW, bytes_accessed=4 * keys * GW, transcendentals=rows * keys
+        ),
+        name="attend",
+    )(active, q, kv, q_seg, k_seg)
+
+
+def attend_back_kernel(
+    act_ref, q_ref, do_ref, o_ref, kv_ref, lse_ref, qseg_ref, kseg_ref, dq_ref, dkv_ref,
+    q_s, do_s, dq_s, delta_s, dk_s, dv_s,
+):
+    kb = pl.program_id(0)
+    rows = q_ref.shape[0]
+
+    @pl.when(kb == 0)
+    def _():
+        ones = jnp.ones((8, HEAD_DIM), jnp.float32)
+        for h in range(GROUP):
+            lanes = slice(HEAD_DIM * h, HEAD_DIM * (h + 1))
+            q_s[h] = q_ref[:, lanes]
+            do_s[h] = do_ref[:, lanes]
+            both = do_ref[:, lanes].astype(jnp.float32) * o_ref[:, lanes]
+            delta_s[h] = lax.dot_general(
+                ones, both, (((1,), (1,)), ((), ())), precision=lax.Precision.HIGHEST,
+                preferred_element_type=jnp.float32,
+            )[0:1]
+        dq_s[...] = jnp.zeros(dq_s.shape, jnp.float32)
+
+    dk_s[...] = jnp.zeros(dk_s.shape, jnp.float32)
+    dv_s[...] = jnp.zeros(dv_s.shape, jnp.float32)
+    k_heads = [kv_ref[:, HEAD_DIM * h : HEAD_DIM * (h + 1)] for h in range(GROUP)]
+    v_heads = [kv_ref[:, GW + HEAD_DIM * h : GW + HEAD_DIM * (h + 1)] for h in range(GROUP)]
+    k_seg = kseg_ref[...]
+
+    def one_chunk(j, carry):
+        @pl.when(act_ref[kb, j] != 0)
+        def _():
+            at = pl.ds(pl.multiple_of(j * CHUNK, CHUNK), CHUNK)
+            permit = k_seg == qseg_ref[0, :, at]
+            for h in range(GROUP):
+                q, do = q_s[h, at], do_s[h, at]
+                s = dot_nt(k_heads[h], q)
+                p = jnp.where(permit, jnp.exp(s - lse_ref[h : h + 1, at]), 0.0)
+                dp = dot_nt(v_heads[h], do)
+                ds = (p * (dp - delta_s[h, :, at])).astype(jnp.bfloat16)
+                dv_s[h] += dot_nn(p.astype(jnp.bfloat16), do)
+                dk_s[h] += dot_nn(ds, q)
+                dq_s[h, at] += dot_tn(ds, k_heads[h])
+
+        return carry
+
+    lax.fori_loop(0, rows // CHUNK, one_chunk, 0)
+    dkv_ref[...] = jnp.concatenate(
+        [dk_s[h] for h in range(GROUP)] + [dv_s[h] for h in range(GROUP)], axis=1
+    ).astype(jnp.bfloat16)
+
+    @pl.when(kb == pl.num_programs(0) - 1)
+    def _():
+        dq_ref[...] = jnp.concatenate(
+            [dq_s[h] * SCORE_SCALE for h in range(GROUP)], axis=1
+        ).astype(jnp.bfloat16)
+
+
+def attend_back(active, q, dout, out, kv, lse, q_seg, k_seg):
+    rows, keys = q.shape[0], kv.shape[0]
+    whole = lambda shape: pl.BlockSpec(shape, lambda i, t: (0,) * len(shape))
+    return pl.pallas_call(
+        attend_back_kernel,
+        out_shape=(
+            jax.ShapeDtypeStruct((rows, GW), jnp.bfloat16),
+            jax.ShapeDtypeStruct((keys, 2 * GW), jnp.bfloat16),
+        ),
+        grid_spec=pltpu.PrefetchScalarGridSpec(
+            num_scalar_prefetch=1,
+            grid=(keys // BLOCK,),
+            in_specs=[
+                whole((rows, GW)),
+                whole((rows, GW)),
+                whole((rows, GW)),
+                pl.BlockSpec((BLOCK, 2 * GW), lambda i, t: (i, 0)),
+                whole((8, rows)),
+                pl.BlockSpec((1, 1, rows), lambda i, t: (i, 0, 0)),
+                pl.BlockSpec((BLOCK, 1), lambda i, t: (i, 0)),
+            ],
+            out_specs=[
+                whole((rows, GW)),
+                pl.BlockSpec((BLOCK, 2 * GW), lambda i, t: (i, 0)),
+            ],
+            scratch_shapes=[
+                pltpu.VMEM((GROUP, rows, HEAD_DIM), jnp.bfloat16),
+                pltpu.VMEM((GROUP, rows, HEAD_DIM), jnp.bfloat16),
+                pltpu.VMEM((GROUP, rows, HEAD_DIM), jnp.float32),
+                pltpu.VMEM((GROUP, 1, rows), jnp.float32),
+                pltpu.VMEM((GROUP, BLOCK, HEAD_DIM), jnp.float32),
+                pltpu.VMEM((GROUP, BLOCK, HEAD_DIM), jnp.float32),
+            ],
+        ),
+        compiler_params=pltpu.CompilerParams(vmem_limit_bytes=32 << 20),
+        cost_estimate=pl.CostEstimate(
+            flops=5 * rows * keys * GW, bytes_accessed=8 * keys * GW, transcendentals=rows * keys
+        ),
+        name="attend_back",
+    )(active, q, dout, out, kv, lse, q_seg, k_seg)
+
+
+def fast_local(
+    tokens, segment_ids, live_blocks, norm1_gain, norm1_bias, qkv_weight, qv_bias, out_weight, out_bias,
+    norm2_gain, norm2_bias, up_weight, up_bias, down_weight, down_bias, grad_out,
+):
+    y, x, z, c = (lax.axis_index(name) for name in ("y", "x", "z", "c"))
+    wide, low = jnp.float32, jnp.bfloat16
+    _, rows, width = tokens.shape
+    own_rows, units = qkv_weight.shape[0], down_weight.shape[0]
+    ff = up_weight.shape[1]
+    half = ff // 2
+    devices = width // own_rows
+    seq_rows = rows * NZ
+    keys = 2 * seq_rows
+    blocks = keys // BLOCK
+
+    own_tokens = tokens[0]
+    line_tokens = z_spread(own_tokens, z).reshape(seq_rows, width)
+    own_seg = z_spread(segment_ids, z).reshape(NZ, rows)
+    seg = in_order(own_seg, swap(own_seg, "c"), c, 1).reshape(keys)
+    vectors = (norm1_gain, norm1_bias, qv_bias, out_bias, norm2_gain, norm2_bias, up_bias, down_bias)
+    sizes = [v.shape[0] for v in vectors]
+    packed = xy_gather(z_spread(jnp.concatenate(vectors)[None], z), y, x)
+    packed = in_order(packed, swap(packed, "c"), c, 3).reshape(devices, sum(sizes)).astype(wide)
+    cuts = [sum(sizes[:i]) for i in range(len(sizes) + 1)]
+    gain1, shift1, bias_qv, bias_out, gain2, shift2, bias_up, bias_down = (
+        packed[:, cuts[i] : cuts[i + 1]].reshape(-1) for i in range(len(sizes))
+    )
+    wz = qkv_weight.reshape(own_rows, 3, NZ, GW).transpose(2, 0, 1, 3).reshape(NZ, own_rows, 3 * GW)
+    wz = xy_gather(z_order(z_exchange(wz, z), z), y, x)
+    wz = in_order(wz, swap(wz, "c"), c, 3).reshape(width, 3 * GW)
+
+    up_sets = up_weight.reshape(own_rows, ff // (2 * units), 2, units).transpose(2, 0, 1, 3)
+    up_sets = up_sets.reshape(2, own_rows, half)
+    up_chip = in_order(pick(up_sets, c), swap(pick(up_sets, 1 - c), "c"), c, 0)
+    up_half = xy_gather(z_spread(up_chip.reshape(2 * own_rows, half), z), y, x).reshape(width, half)
+    wo = xy_gather(z_spread(out_weight, z), y, x)
+    wo = in_order(wo, swap(wo, "c"), c, 3).reshape(NZ, GW, width)
+    down_half = xy_gather(z_spread(down_weight, z), y, x).reshape(half, width)
+    up_bias_half = pick(bias_up.reshape(ff // (2 * units), 2, units), c, 1).reshape(half)
+
+    own_blocks = seq_rows // BLOCK
+    per = rows // BLOCK
+    ids = jnp.arange(blocks, dtype=jnp.int32)
+    own_ids = pick(ids.reshape(NZ, 2, per), c, 1).reshape(own_blocks)
+    own_live = pick(live_blocks[0].reshape(NZ, 2, per, blocks), c, 1).reshape(own_blocks, blocks)
+    seg_blocks = seg.reshape(blocks, BLOCK)
+    first, last = seg_blocks[:, 0], seg_blocks[:, -1]
+    own_seg_blocks = own_seg.reshape(own_blocks, BLOCK)
+    own_first, own_last = own_seg_blocks[:, 0], own_seg_blocks[:, -1]
+    may = (own_live > 0) | (own_ids[:, None] == ids[None, :])
+    meet = may & (own_first[:, None] <= last[None, :]) & (first[None, :] <= own_last[:, None])
+    per_chunk = CHUNK // BLOCK
+    active = jnp.any(meet.reshape(own_blocks, blocks // per_chunk, per_chunk), axis=2).astype(jnp.int32)
+    active_back = jnp.any(
+        meet.reshape(own_blocks // per_chunk, per_chunk, blocks), axis=1
+    ).T.astype(jnp.int32)
+    key_seg = jnp.where(may[:, :, None], seg_blocks[None], -1).reshape(own_blocks, 1, keys)
+    query_seg = jnp.where(may.T[:, :, None], own_seg_blocks[None], -1).reshape(blocks, 1, seq_rows)
+
+    tokens_wide = line_tokens.astype(wide)
+    unit1, scale1 = norm_stats(tokens_wide)
+    n1 = (unit1 * gain1 + shift1).astype(low)
+    projected = matmul_low(n1, wz)
+    q_bias = pick(bias_qv[:width].reshape(NZ, GW), z)
+    v_bias = pick(bias_qv[width:].reshape(NZ, GW), z)
+    q = (projected[:, :GW] + q_bias).astype(low) * jnp.asarray(SCORE_SCALE, low)
+    kv = jnp.concatenate(
+        [projected[:, GW : 2 * GW].astype(low), (projected[:, 2 * GW :] + v_bias).astype(low)], axis=1
+    )
+    kv_line = kv.reshape(NZ, rows, 2 * GW)
+    kv_all = in_order(kv_line, swap(kv_line, "c"), c, 1).reshape(keys, 2 * GW)
+    att_wide, att_low, lse = attend(active, q, kv_all, own_seg.reshape(seq_rows, 1), key_seg)
+    att = z_order(z_exchange(att_low.reshape(NZ, rows, GW), z), z)
+
+    own_wide = own_tokens.astype(wide)
+    branch = sum(matmul_low(att[g], wo[g]) for g in range(NZ))
+    hidden = own_wide + branch + bias_out
+    unit2, scale2 = norm_stats(hidden)
+    n2 = (unit2 * gain2 + shift2).astype(low)
+
+    go = grad_out[0]
+    n2_both = jnp.concatenate([n2, swap(n2, "c")], axis=0)
+    go_both = jnp.concatenate([go, swap(go, "c")], axis=0)
+    before = matmul_low(n2_both, up_half) + up_bias_half
+    cdf = 0.5 * (1.0 + lax.erf(before * 0.7071067811865476))
+    slope = cdf + before * (0.3989422804014327 * jnp.exp(-0.5 * before * before))
+    activated = (before * cdf).astype(low)
+    out_part = matmul_low(activated, down_half)
+    out_sum = out_part[:rows] + swap(out_part[rows:].astype(low), "c").astype(wide)
+    output = (hidden + out_sum + bias_down).astype(low)
+    grad_before = (dot_nt(go_both, down_half) * slope).astype(low)
+    m_part = dot_nt(grad_before, up_half)
+    m = m_part[:rows] + swap(m_part[rows:].astype(low), "c").astype(wide)
+    grad_up = dot_tn(n2_both, grad_before).astype(low)
+    grad_down = dot_tn(activated, go_both).astype(low)
+    up_bias_part = jnp.sum(grad_before.astype(wide), axis=0)
+
+    go_wide = go.astype(wide)
+    grad_hidden = go_wide + norm_back(m, gain2, unit2, scale2)
+    grad_branch = grad_hidden.astype(low)
+    grad_att = jnp.stack([dot_nt(grad_branch, wo[g]).astype(low) for g in range(NZ)])
+    dout = z_order(z_exchange(grad_att, z), z).reshape(seq_rows, GW)
+    grad_wo = jnp.stack([dot_tn(att[g], grad_branch) for g in range(NZ)]).astype(low)
+
+    dq, dkv = attend_back(
+        active_back, q, dout, att_wide, kv_all, lse, query_seg, seg.reshape(keys, 1)
+    )
+    dkv = dkv.reshape(NZ, 2, rows, 2 * GW)
+    dkv_sum = pick(dkv, c, 1).astype(wide) + swap(pick(dkv, 1 - c, 1), "c").astype(wide)
+    dkv_low = dkv_sum.reshape(seq_rows, 2 * GW).astype(low)
+    dqkv = jnp.concatenate([dq, dkv_low], axis=1)
+    m1 = dot_nt(dqkv, wz)
+    m1_line = m1.reshape(NZ, rows, width)
+    m1_own = z_collect(m1_line, z, low)
+    grad_wz = dot_tn(n1, dqkv).astype(low)
+    own_unit1, own_scale1 = norm_stats(own_wide)
+    grad_tokens = grad_hidden + norm_back(m1_own, gain1, own_unit1, own_scale1)
+
+    grad_down = z_collect(xy_scatter(grad_down.reshape(2, 2, NZ, units, width), y, x, low), z, low)
+    grad_up = z_collect(xy_scatter(grad_up.reshape(2, 2, NZ, 2 * own_rows, half), y, x, low), z, low)
+    grad_up = grad_up.reshape(2, own_rows, half)
+    up_other = swap(pick(grad_up, 1 - c).astype(low), "c").astype(wide)
+    up_shape = (own_rows, ff // (2 * units), units)
+    grad_up = in_order(pick(grad_up, c).reshape(up_shape), up_other.reshape(up_shape), c, 2)
+    grad_up = grad_up.reshape(own_rows, ff)
+
+    def over_cores(array, wire):
+        return pick(array, c, 3).astype(wide) + swap(pick(array, 1 - c, 3).astype(wire), "c").astype(wide)
+
+    grad_wo = over_cores(grad_wo.reshape(2, 2, NZ, 2, own_rows, width), low)
+    grad_wo = z_collect(xy_scatter(grad_wo, y, x, low), z, low)
+    grad_wz = over_cores(grad_wz.reshape(2, 2, NZ, 2, own_rows, 3 * GW), low)
+    grad_wz = z_order(z_exchange(xy_scatter(grad_wz, y, x, low).astype(low), z), z)
+    grad_qkv = grad_wz.reshape(NZ, own_rows, 3, GW).transpose(1, 2, 0, 3).reshape(own_rows, 3 * width)
+
+    dqkv_sum = jnp.sum(dqkv.astype(wide), axis=0)
+    at_group = (jnp.arange(NZ) == z)[:, None]
+    qv_part = jnp.concatenate(
+        [
+            jnp.where(at_group, dqkv_sum[None, :GW], 0.0).reshape(width),
+            jnp.where(at_group, dqkv_sum[None, 2 * GW :], 0.0).reshape(width),
+        ]
+    )
+    at_core = (jnp.arange(2) == c)[None, :, None]
+    up_bias_part = jnp.where(at_core, up_bias_part.reshape(ff // (2 * units), 1, units), 0.0)
+    parts = (
+        jnp.sum(m1 * unit1, axis=0),
+        jnp.sum(m1, axis=0),
+        qv_part,
+        jnp.sum(grad_branch.astype(wide), axis=0),
+        jnp.sum(m * unit2, axis=0),
+        jnp.sum(m, axis=0),
+        up_bias_part,
+        jnp.sum(go_wide, axis=0),
+    )
+    vec = jnp.concatenate([p.reshape(devices, s) for p, s in zip(parts, sizes)], axis=1)
+    vec = over_cores(vec.reshape(2, 2, NZ, 2, 1, sum(sizes)), wide)
+    vec = z_collect(xy_scatter(vec, y, x, wide), z, wide)[0]
+    v = [vec[cuts[i] : cuts[i + 1]] for i in range(len(sizes))]
+    return (
+        output[None], grad_tokens[None], v[0], v[1], grad_qkv.astype(wide), v[2], grad_wo, v[3],
+        v[4], v[5], grad_up, v[6], grad_down, v[7],
+    )
+
+
+def build(body, mesh, dp, ctx):
+    both = dp + ctx
+    rows, vector, matrix = P(dp, ctx, None), P(both), P(both, None)
     return jax.shard_map(
-        local,
+        body,
         mesh=mesh,
         in_specs=(
-            P("dp", "ctx", None),
-            P("dp", "ctx"),
-            P("dp", None, None),
-            P(("dp", "ctx")),
-            P(("dp", "ctx")),
-            P(("dp", "ctx"), None),
-            P(("dp", "ctx")),
-            P(("dp", "ctx"), None),
-            P(("dp", "ctx")),
-            P(("dp", "ctx")),
-            P(("dp", "ctx")),
-            P(("dp", "ctx"), None),
-            P(("dp", "ctx")),
-            P(("dp", "ctx"), None),
-            P(("dp", "ctx")),
-            P("dp", "ctx", None),
+            rows, P(dp, ctx), P(dp, None, None), vector, vector, matrix, vector, matrix, vector,
+            vector, vector, matrix, vector, matrix, vector, rows,
         ),
         out_specs=(
-            P("dp", "ctx", None),
-            P("dp", "ctx", None),
-            P(("dp", "ctx")),
-            P(("dp", "ctx")),
-            P(("dp", "ctx"), None),
-            P(("dp", "ctx")),
-            P(("dp", "ctx"), None),
-            P(("dp", "ctx")),
-            P(("dp", "ctx")),
-            P(("dp", "ctx")),
-            P(("dp", "ctx"), None),
-            P(("dp", "ctx")),
-            P(("dp", "ctx"), None),
-            P(("dp", "ctx")),
+            rows, rows, vector, vector, matrix, vector, matrix, vector, vector, vector, matrix,
+            vector, matrix, vector,
         ),
         check_vma=False,
     )
+
+
+def solution(mesh):
+    if dict(mesh.shape) == {"dp": 4, "ctx": 2 * NZ}:
+        grid = Mesh(mesh.devices.reshape(2, 2, NZ, 2), ("y", "x", "z", "c"))
+        return build(fast_local, grid, ("y", "x"), ("z", "c"))
+    return build(local, mesh, ("dp",), ("ctx",))

time: 953 us -> 489 us (0.51)
  waiting for transfers between devices: 620 us -> 121 us
  starting transfers between devices: 0.73 us -> 166 us
  matrix products: 135 us -> 29.4 us
  blocking collectives: 95.5 us -> 0 us
  Pallas kernels: 0 us -> 56.7 us
  other arithmetic: 22.1 us -> 46.6 us
  between operations: 15.2 us -> 3.84 us
    reduce_scatter x6 -> x0, waiting for transfers between devices: 433 us -> none  [the longest x1 111 us: local(): lax.psum_scatter(grad_down.astype(jnp.bfloat16), ('dp', 'ctx'), scatter_d...]
    all_gather x6 -> x0, waiting for transfers between devices: 185 us -> none  [the longest x1 60.6 us: local(): lax.all_gather(shards[8], ('dp', 'ctx'), axis=0, tiled=True)]
    ppermute x0 -> x106, starting transfers between devices: none -> 166 us  [the longest x88 131 us: shift(): lax.ppermute(array, axis, [(i, (i + hop) % size) for i in range(size)])]
    ppermute x0 -> x106, waiting for transfers between devices: none -> 121 us  [the longest x88 106 us: shift(): lax.ppermute(array, axis, [(i, (i + hop) % size) for i in range(size)])]
    dot_general x45 -> x14, matrix products: 113 us -> 21.9 us  [the longest x7 11.7 us: dot_tn(): lax.dot_general(a, b, (((0,), (0,)), ((), ())), preferred_element_type=jn...]
    unnamed x2 -> x0, blocking collectives: 83.9 us -> none
    pallas_call x0 -> x2, Pallas kernels: none -> 56.7 us  [the longest x1 28.8 us: attend_back(): pl.pallas_call(attend_back_kernel, out_shape=(jax.ShapeDtypeStruct((rows,...]
    another operation x0 -> x63, other arithmetic: none -> 16.3 us  [the longest x40 13.3 us: in_order(): return jnp.stack([first, second], axis=axis)]
  transfers between devices with their start and end apart: 12 -> 106, of which waited for: 11 -> 45; matrix products, arithmetic and copies ran while one was open for 13% -> 22% of each run, Pallas kernels for 0% -> 12%
where the time goes in v2:
time: 489 us; the launch traced here: 479 us
  starting transfers between devices  166 us (34%)
  waiting for transfers between devices  121 us (25%)
  Pallas kernels  56.7 us (12%)
  local copies, waits for them, and re-layouts  56.1 us (11%)
  other arithmetic  46.6 us (10%)
  matrix products  29.4 us (6%)
    ppermute x88, starting transfers between devices, shift(): lax.ppermute(array, axis, [(i, (i + hop) % size) for i in range(size)])  131 us
    ppermute x88, waiting for transfers between devices, shift(): lax.ppermute(array, axis, [(i, (i + hop) % size) for i in range(size)])  106 us
    pallas_call x1, Pallas kernels, attend_back(): pl.pallas_call(attend_back_kernel, out_shape=(jax.ShapeDtypeStruct((rows,...  28.8 us
    pallas_call x1, Pallas kernels, attend(): pl.pallas_call(attend_kernel, out_shape=(jax.ShapeDtypeStruct((rows, GW),...  27.9 us
    ppermute x6, starting transfers between devices, z_spread(): up = lax.ppermute(block, 'z', [(0, 1), (1, 2), (2, 3)])  18.7 us
    another operation x40, other arithmetic, in_order(): return jnp.stack([first, second], axis=axis)  13.3 us
    unnamed x219, local copies, waits for them, and re-layouts  12.3 us
    ppermute x6, waiting for transfers between devices, z_spread(): last = lax.ppermute(far, 'z', [(2, 3), (1, 0)])  11.9 us
  transfers between devices with their start and end apart: 106, of which 45 were waited for; matrix products, arithmetic and copies ran while one was open for 22% of the time, Pallas kernels for 12%

profile of v2, /device:TPU:0, one launch (start us, length us, event | category | flops | bytes accessed | tf_op | source)
XLA Modules:
  0.0 479.1 jit_solution(3359576523188675319)
XLA Ops:
  0.7 5.5 %concatenate.79 = bf16[288]{0:T(512)(128)(2,1)S(1)} concatenate(bf16[24]{0:T(256)(128)(2,1)} %param.19, bf16[24]{0:T(256)(128)(2,1)} %param.20, bf16[48]{0:T(256)(128)(2,1)} %param.22, bf16[24]{0:T(256)(128)(2,1)} %param.24, bf16[24]{0:T(256)(128)(2,1)} %param.25, bf16[24]{0:T(256)(128)(2,1)} %param.26, bf16[96]{0:T(256)(128)(2,1)} %param.28, bf16[24]{0:T(256)(128)(2,1)} %param.30), dimensions={0} | concatenate | bytes 1152 | tf_op jit(solution)/shard_map/concatenate | solution.py:694
  7.5 5.6 %collective-permute-start.9 = (bf16[1,288]{1,0:T(2,128)(2,1)S(1)}, bf16[1,288]{1,0:T(2,128)(2,1)S(1)}, u32[]{:S(2)}, u32[]{:S(2)}) collective-permute-start(bf16[1,288]{1,0:T(2,128)(2,1)S(1)} %broadcast_in_dim.139), channel_id=1, source_target_pairs={{0,2},{2,4},{4,6},{1,3},{3,5},{5,7},{8,10},{10,12},{12,14},{9,11},... | collective-permute-start | bytes 1736 | tf_op jit(solution)/shard_map/ppermute | solution.py:404
  13.0 3.1 collective-permute-start.10
  25.5 4.5 collective-permute-start
  32.2 2.5 collective-permute-start.5
  36.1 2.7 collective-permute-start.18
  59.6 13.2 %collective-permute-start.20 = (bf16[24,576]{1,0:T(8,128)(2,1)S(1)}, bf16[24,576]{1,0:T(8,128)(2,1)S(1)}, u32[]{:S(2)}, u32[]{:S(2)}) collective-permute-start(bf16[24,576]{1,0:T(8,128)(2,1)S(1)} %get-tuple-element.158), channel_id=1, source_target_pairs={{0,6},{2,0},{4,2},{6,4},{1,7},{3,1},{5,3},{7,5},{8,14},{10,8},{12,... | collective-permute-start | bytes 82952 | tf_op jit(solution)/shard_map/ppermute | solution.py:390
  77.0 2.5 collective-permute-start.30
  83.2 3.2 collective-permute-done.33
  96.2 2.7 collective-permute-done.36
  100.4 3.5 collective-permute-done.34
  105.5 3.3 collective-permute-done.24
  115.2 6.7 %collective-permute-start.42 = (bf16[48,1536]{1,0:T(8,128)(2,1)S(1)}, bf16[48,1536]{1,0:T(8,128)(2,1)S(1)}, u32[]{:S(2)}, u32[]{:S(2)}) collective-permute-start(bf16[48,1536]{1,0:T(8,128)(2,1)S(1)} %bitcast.706), channel_id=1, source_target_pairs={{0,4},{2,6},{4,0},{6,2},{1,5},{3,7},{5,1},{7,3},{8,12},{10,14},{12... | collective-permute-start | bytes 442376 | tf_op jit(solution)/shard_map/ppermute | solution.py:390
  124.9 3.6 collective-permute-done.37
  130.4 3.3 collective-permute-done.35
  137.3 3.4 collective-permute-done.43
  141.4 6.0 %collective-permute-done.55 = bf16[2,96,768]{2,1,0:T(8,128)(2,1)S(1)} collective-permute-done((bf16[2,96,768]{2,1,0:T(8,128)(2,1)S(1)}, bf16[2,96,768]{2,1,0:T(8,128)(2,1)S(1)}, u32[]{:S(2)}, u32[]{:S(2)}) %collective-permute-start.55) | collective-permute-done | bytes 294944 | tf_op jit(solution)/shard_map/ppermute | solution.py:390
  149.9 4.3 collective-permute-done.53
  156.5 8.2 %collective-permute-done.47 = bf16[2,48,1536]{2,1,0:T(8,128)(2,1)S(1)} collective-permute-done((bf16[2,48,1536]{2,1,0:T(8,128)(2,1)S(1)}, bf16[2,48,1536]{2,1,0:T(8,128)(2,1)S(1)}, u32[]{:S(2)}, u32[]{:S(2)}) %collective-permute-start.47) | collective-permute-done | bytes 294944 | tf_op jit(solution)/shard_map/ppermute | solution.py:390
  166.3 7.0 %collective-permute-done.45 = bf16[2,48,1536]{2,1,0:T(8,128)(2,1)S(1)} collective-permute-done((bf16[2,48,1536]{2,1,0:T(8,128)(2,1)S(1)}, bf16[2,48,1536]{2,1,0:T(8,128)(2,1)S(1)}, u32[]{:S(2)}, u32[]{:S(2)}) %collective-permute-start.45) | collective-permute-done | bytes 294944 | tf_op jit(solution)/shard_map/ppermute | solution.py:390
  179.0 8.1 %collective-permute-done.7 = bf16[256,768]{1,0:T(8,128)(2,1)S(1)} collective-permute-done((bf16[256,768]{1,0:T(8,128)(2,1)S(1)}, bf16[256,768]{1,0:T(8,128)(2,1)S(1)}, u32[]{:S(2)}, u32[]{:S(2)}) %collective-permute-start.7) | collective-permute-done | bytes 393248 | tf_op jit(solution)/shard_map/ppermute | solution.py:407
  208.0 27.9 %attend.1 = (f32[1024,192]{1,0:T(8,128)S(1)}, bf16[1024,192]{1,0:T(8,128)(2,1)S(1)}, f32[8,1024]{1,0:T(8,128)S(1)}) custom-call(s32[8,8]{1,0:T(8,128)S(1)} %convert_element_type.419.act_ref, bf16[1024,192]{1,0:T(8,128)(2,1)S(1)} %fusion.36.q_ref, bf16[2048,384]{1,0:T(8,128)(2,1)S(1)} %bitcast.660, s32[1024,1]{1,0:T(8,128)S(1)} %bitcast.665, ...), custom_call_target="tpu_custom_call" | custom-call | flops 805306368 | bytes 1572864 | tf_op jit(solution)/shard_map/attend/pallas_call | solution.py:538
  238.7 7.4 %collective-permute-start.28 = (bf16[256,192]{0,1:T(8,128)(2,1)}, bf16[256,192]{0,1:T(8,128)(2,1)S(1)}, u32[]{:S(2)}, u32[]{:S(2)}) collective-permute-start(bf16[256,192]{0,1:T(8,128)(2,1)} %bitcast.710), channel_id=1, source_target_pairs={{0,4},{2,6},{4,0},{6,2},{1,5},{3,7},{5,1},{7,3},{8,12},{10,14},{12... | collective-permute-start | bytes 294920 | tf_op jit(solution)/shard_map/ppermute | solution.py:390
  250.0 2.6 collective-permute-done.28
  262.0 3.8 convert_reduce_fusion
  271.3 3.1 convolution_convert_fusion.1
  277.2 2.5 convolution_convert_fusion
  283.6 3.3 convert_reduce_fusion.5
  311.9 28.8 %attend_back.1 = (bf16[1024,192]{1,0:T(8,128)(2,1)S(1)}, bf16[2048,384]{1,0:T(8,128)(2,1)S(1)}) custom-call(s32[16,4]{1,0:T(8,128)S(1)} %bitcast.667, bf16[1024,192]{1,0:T(8,128)(2,1)S(1)} %copy-done.7, bf16[1024,192]{1,0:T(8,128)(2,1)S(1)} %bitcast.664, f32[1024,192]{1,0:T(8,128)S(1)} %copy-done.9, bf16[2048,384]{1,0:T(8,128)(2,1)S(1)} %bitcast.661, ...), custom_call_target="tpu_custom_call" | custom-call | flops 2013265920 | bytes 3145728 | tf_op jit(solution)/shard_map/attend_back/pallas_call | solution.py:634
  341.7 4.9 %collective-permute-start.63 = (bf16[4,256,384]{2,1,0:T(8,128)(2,1)}, bf16[4,256,384]{2,1,0:T(8,128)(2,1)}, u32[]{:S(2)}, u32[]{:S(2)}) collective-permute-start(bf16[4,256,384]{2,1,0:T(8,128)(2,1)} %dynamic-slice_bitcast_fusion), channel_id=1, source_target_pairs={{0,1},{1,0},{2,3},{3,2},{4,5},{5,4},{6,7},{7,6},{8,9},{9,8},{10,11... | collective-permute-start | bytes 2359304 | tf_op jit(solution)/shard_map/ppermute | solution.py:390
  354.0 3.8 collective-permute-done.92
  361.3 2.7 collective-permute-done.100
  367.9 2.7 collective-permute-start.105
  373.4 5.2 %collective-permute-done.96 = bf16[48,1536]{1,0:T(8,128)(2,1)S(1)} collective-permute-done((bf16[48,1536]{1,0:T(8,128)(2,1)S(1)}, bf16[48,1536]{1,0:T(8,128)(2,1)S(1)}, u32[]{:S(2)}, u32[]{:S(2)}) %collective-permute-start.96) | collective-permute-done | bytes 147488 | tf_op jit(solution)/shard_map/ppermute | solution.py:390
  378.8 4.2 collective-permute-start.86
  383.1 6.5 %collective-permute-done.104 = bf16[96,768]{1,0:T(8,128)(2,1)S(1)} collective-permute-done((bf16[96,768]{1,0:T(8,128)(2,1)S(1)}, bf16[96,768]{1,0:T(8,128)(2,1)S(1)}, u32[]{:S(2)}, u32[]{:S(2)}) %collective-permute-start.104) | collective-permute-done | bytes 147488 | tf_op jit(solution)/shard_map/ppermute | solution.py:390
  392.9 3.2 collective-permute-done.85
  397.5 2.7 collective-permute-start.89
  403.1 2.8 collective-permute-done.88
  408.8 3.8 fusion.193
  416.3 3.0 convolution_convert_fusion.2
  421.3 2.4 collective-permute-done.70
  428.4 3.3 collective-permute-start.74
  433.4 14.1 %collective-permute-start.64 = (bf16[256,768]{1,0:T(8,128)(2,1)S(1)}, bf16[256,768]{1,0:T(8,128)(2,1)S(1)}, u32[]{:S(2)}, u32[]{:S(2)}) collective-permute-start(bf16[256,768]{1,0:T(8,128)(2,1)S(1)} %get-tuple-element.44), channel_id=1, source_target_pairs={{0,2},{2,4},{4,6},{6,0},{1,3},{3,5},{5,7},{7,1},{8,10},{10,12},{12... | collective-permute-start | bytes 1179656 | tf_op jit(solution)/shard_map/ppermute | solution.py:390
  449.4 3.5 collective-permute-done.64
  460.0 2.7 collective-permute-start.77
  469.1 2.4 collective-permute-start.82
  473.0 4.1 collective-permute-done.80
  (679 shorter events, 215.1 us)
Async XLA Ops:
  6.2 19.3 %collective-permute-start.12 = (bf16[1,288]{1,0:T(2,128)(2,1)S(1)}, bf16[1,288]{1,0:T(2,128)(2,1)S(1)}, u32[]{:S(2)}, u32[]{:S(2)}) collective-permute-start(bf16[1,288]{1,0:T(2,128)(2,1)S(1)} %broadcast_in_dim.139), channel_id=1, source_target_pairs={{2,0},{4,2},{6,4},{3,1},{5,3},{7,5},{10,8},{12,10},{14,12},{11,9},... | collective-permute-start | bytes 1736 | tf_op jit(solution)/shard_map/ppermute | solution.py:405
  7.5 22.6 %collective-permute-start.9 = (bf16[1,288]{1,0:T(2,128)(2,1)S(1)}, bf16[1,288]{1,0:T(2,128)(2,1)S(1)}, u32[]{:S(2)}, u32[]{:S(2)}) collective-permute-start(bf16[1,288]{1,0:T(2,128)(2,1)S(1)} %broadcast_in_dim.139), channel_id=1, source_target_pairs={{0,2},{2,4},{4,6},{1,3},{3,5},{5,7},{8,10},{10,12},{12,14},{9,11},... | collective-permute-start | bytes 1736 | tf_op jit(solution)/shard_map/ppermute | solution.py:404
  13.0 11.2 %collective-permute-start.10 = (bf16[1,288]{1,0:T(2,128)(2,1)S(1)}, bf16[1,288]{1,0:T(2,128)(2,1)S(1)}, u32[]{:S(2)}, u32[]{:S(2)}) collective-permute-start(bf16[1,288]{1,0:T(2,128)(2,1)S(1)} %broadcast_in_dim.139), channel_id=1, source_target_pairs={{0,4},{2,6},{4,0},{6,2},{1,5},{3,7},{5,1},{7,3},{8,12},{10,14},{12... | collective-permute-start | bytes 1736 | tf_op jit(solution)/shard_map/ppermute | solution.py:390
  16.1 20.0 %collective-permute-start.3 = (s32[1,256]{1,0:T(1,128)}, s32[1,256]{1,0:T(1,128)S(1)}, u32[]{:S(2)}, u32[]{:S(2)}) collective-permute-start(s32[1,256]{1,0:T(1,128)} %param.17), channel_id=1, source_target_pairs={{2,0},{4,2},{6,4},{3,1},{5,3},{7,5},{10,8},{12,10},{14,12},{11,9},... | collective-permute-start | bytes 3080 | tf_op jit(solution)/shard_map/ppermute | solution.py:405
  17.4 14.8 %collective-permute-start.1 = (s32[1,256]{1,0:T(1,128)}, s32[1,256]{1,0:T(1,128)S(1)}, u32[]{:S(2)}, u32[]{:S(2)}) collective-permute-start(s32[1,256]{1,0:T(1,128)} %param.17), channel_id=1, source_target_pairs={{0,4},{2,6},{4,0},{6,2},{1,5},{3,7},{5,1},{7,3},{8,12},{10,14},{12... | collective-permute-start | bytes 3080 | tf_op jit(solution)/shard_map/ppermute | solution.py:390
  25.5 13.3 %collective-permute-start = (s32[1,256]{1,0:T(1,128)S(1)}, s32[1,256]{1,0:T(1,128)S(1)}, u32[]{:S(2)}, u32[]{:S(2)}) collective-permute-start(s32[1,256]{1,0:T(1,128)S(1)} %copy-done.99), channel_id=1, source_target_pairs={{0,2},{2,4},{4,6},{1,3},{3,5},{5,7},{8,10},{10,12},{12,14},{9,11},... | collective-permute-start | bytes 3080 | tf_op jit(solution)/shard_map/ppermute | solution.py:404
  30.1 136.2 %collective-permute-start.6 = (bf16[256,768]{1,0:T(8,128)(2,1)S(1)}, bf16[256,768]{1,0:T(8,128)(2,1)S(1)}, u32[]{:S(2)}, u32[]{:S(2)}) collective-permute-start(bf16[256,768]{1,0:T(8,128)(2,1)S(1)} %bitcast.668), channel_id=1, source_target_pairs={{0,4},{2,6},{4,0},{6,2},{1,5},{3,7},{5,1},{7,3},{8,12},{10,14},{12... | collective-permute-start | bytes 1179656 | tf_op jit(solution)/shard_map/ppermute | solution.py:390
  32.2 144.4 %collective-permute-start.5 = (bf16[256,768]{1,0:T(8,128)(2,1)S(1)}, bf16[256,768]{1,0:T(8,128)(2,1)S(1)}, u32[]{:S(2)}, u32[]{:S(2)}) collective-permute-start(bf16[256,768]{1,0:T(8,128)(2,1)S(1)} %bitcast.669), channel_id=1, source_target_pairs={{0,2},{2,4},{4,6},{1,3},{3,5},{5,7},{8,10},{10,12},{12,14},{9,11},... | collective-permute-start | bytes 1179656 | tf_op jit(solution)/shard_map/ppermute | solution.py:404
  36.1 40.9 %collective-permute-start.18 = (bf16[24,576]{1,0:T(8,128)(2,1)S(1)}, bf16[24,576]{1,0:T(8,128)(2,1)S(1)}, u32[]{:S(2)}, u32[]{:S(2)}) collective-permute-start(bf16[24,576]{1,0:T(8,128)(2,1)S(1)} %get-tuple-element.160), channel_id=1, source_target_pairs={{0,2},{2,4},{4,6},{6,0},{1,3},{3,5},{5,7},{7,1},{8,10},{10,12},{12... | collective-permute-start | bytes 82952 | tf_op jit(solution)/shard_map/ppermute | solution.py:390
  38.8 38.2 %collective-permute-start.19 = (bf16[24,576]{1,0:T(8,128)(2,1)S(1)}, bf16[24,576]{1,0:T(8,128)(2,1)S(1)}, u32[]{:S(2)}, u32[]{:S(2)}) collective-permute-start(bf16[24,576]{1,0:T(8,128)(2,1)S(1)} %get-tuple-element.159), channel_id=1, source_target_pairs={{0,4},{2,6},{4,0},{6,2},{1,5},{3,7},{5,1},{7,3},{8,12},{10,14},{12... | collective-permute-start | bytes 82952 | tf_op jit(solution)/shard_map/ppermute | solution.py:390
  59.6 19.8 %collective-permute-start.20 = (bf16[24,576]{1,0:T(8,128)(2,1)S(1)}, bf16[24,576]{1,0:T(8,128)(2,1)S(1)}, u32[]{:S(2)}, u32[]{:S(2)}) collective-permute-start(bf16[24,576]{1,0:T(8,128)(2,1)S(1)} %get-tuple-element.158), channel_id=1, source_target_pairs={{0,6},{2,0},{4,2},{6,4},{1,7},{3,1},{5,3},{7,5},{8,14},{10,8},{12,... | collective-permute-start | bytes 82952 | tf_op jit(solution)/shard_map/ppermute | solution.py:390
  86.4 24.0 %collective-permute-start.50 = (bf16[96,768]{1,0:T(8,128)(2,1)S(1)}, bf16[96,768]{1,0:T(8,128)(2,1)S(1)}, u32[]{:S(2)}, u32[]{:S(2)}) collective-permute-start(bf16[96,768]{1,0:T(8,128)(2,1)S(1)} %copy-done.70), channel_id=1, source_target_pairs={{0,4},{2,6},{4,0},{6,2},{1,5},{3,7},{5,1},{7,3},{8,12},{10,14},{12... | collective-permute-start | bytes 442376 | tf_op jit(solution)/shard_map/ppermute | solution.py:390
  92.2 23.0 %collective-permute-start.49 = (bf16[96,768]{1,0:T(8,128)(2,1)S(1)}, bf16[96,768]{1,0:T(8,128)(2,1)S(1)}, u32[]{:S(2)}, u32[]{:S(2)}) collective-permute-start(bf16[96,768]{1,0:T(8,128)(2,1)S(1)} %copy-done.70), channel_id=1, source_target_pairs={{0,2},{2,4},{4,6},{1,3},{3,5},{5,7},{8,10},{10,12},{12,14},{9,11},... | collective-permute-start | bytes 442376 | tf_op jit(solution)/shard_map/ppermute | solution.py:404
  110.4 11.5 %collective-permute-start.52 = (bf16[96,768]{1,0:T(8,128)(2,1)S(1)}, bf16[96,768]{1,0:T(8,128)(2,1)S(1)}, u32[]{:S(2)}, u32[]{:S(2)}) collective-permute-start(bf16[96,768]{1,0:T(8,128)(2,1)S(1)} %copy-done.70), channel_id=1, source_target_pairs={{2,0},{4,2},{6,4},{3,1},{5,3},{7,5},{10,8},{12,10},{14,12},{11,9},... | collective-permute-start | bytes 442376 | tf_op jit(solution)/shard_map/ppermute | solution.py:405
  115.2 13.9 %collective-permute-start.42 = (bf16[48,1536]{1,0:T(8,128)(2,1)S(1)}, bf16[48,1536]{1,0:T(8,128)(2,1)S(1)}, u32[]{:S(2)}, u32[]{:S(2)}) collective-permute-start(bf16[48,1536]{1,0:T(8,128)(2,1)S(1)} %bitcast.706), channel_id=1, source_target_pairs={{0,4},{2,6},{4,0},{6,2},{1,5},{3,7},{5,1},{7,3},{8,12},{10,14},{12... | collective-permute-start | bytes 442376 | tf_op jit(solution)/shard_map/ppermute | solution.py:390
  121.9 14.0 %collective-permute-start.41 = (bf16[48,1536]{1,0:T(8,128)(2,1)S(1)}, bf16[48,1536]{1,0:T(8,128)(2,1)S(1)}, u32[]{:S(2)}, u32[]{:S(2)}) collective-permute-start(bf16[48,1536]{1,0:T(8,128)(2,1)S(1)} %bitcast.707), channel_id=1, source_target_pairs={{0,2},{2,4},{4,6},{1,3},{3,5},{5,7},{8,10},{10,12},{12,14},{9,11},... | collective-permute-start | bytes 442376 | tf_op jit(solution)/shard_map/ppermute | solution.py:404
  135.9 42.3 %collective-permute-start.8 = (bf16[256,768]{1,0:T(8,128)(2,1)S(1)}, bf16[256,768]{1,0:T(8,128)(2,1)S(1)}, u32[]{:S(2)}, u32[]{:S(2)}) collective-permute-start(bf16[256,768]{1,0:T(8,128)(2,1)S(1)} %bitcast.670), channel_id=1, source_target_pairs={{2,0},{4,2},{6,4},{3,1},{5,3},{7,5},{10,8},{12,10},{14,12},{11,9},... | collective-permute-start | bytes 1179656 | tf_op jit(solution)/shard_map/ppermute | solution.py:405
  137.3 17.9 %collective-permute-start.25 = (bf16[2,2,4,24,576]{4,3,2,1,0:T(8,128)(2,1)S(1)}, bf16[2,2,4,24,576]{4,3,2,1,0:T(8,128)(2,1)S(1)}, u32[]{:S(2)}, u32[]{:S(2)}) collective-permute-start(bf16[2,2,4,24,576]{4,3,2,1,0:T(8,128)(2,1)S(1)} %maximum_maximum_fusion.3), channel_id=1, source_target_pairs={{0,1},{1,0},{2,3},{3,2},{4,5},{5,4},{6,7},{7,6},{8,9},{9,8},{10,11... | collective-permute-start | bytes 1327112 | tf_op jit(solution)/shard_map/ppermute | solution.py:390
  154.1 107.8 %collective-permute-start.58 = (bf16[256,768]{1,0:T(8,128)(2,1)}, bf16[256,768]{1,0:T(8,128)(2,1)}, u32[]{:S(2)}, u32[]{:S(2)}) collective-permute-start(bf16[256,768]{1,0:T(8,128)(2,1)} %bitcast.120), channel_id=1, source_target_pairs={{0,1},{1,0},{2,3},{3,2},{4,5},{5,4},{6,7},{7,6},{8,9},{9,8},{10,11... | collective-permute-start | bytes 1179656 | tf_op jit(solution)/shard_map/ppermute | solution.py:390
  166.2 34.5 %collective-permute-start.38 = (bf16[2,2,4,24,768]{4,3,2,1,0:T(8,128)(2,1)}, bf16[2,2,4,24,768]{4,3,2,1,0:T(8,128)(2,1)}, u32[]{:S(2)}, u32[]{:S(2)}) collective-permute-start(bf16[2,2,4,24,768]{4,3,2,1,0:T(8,128)(2,1)} %maximum_maximum_fusion.2), channel_id=1, source_target_pairs={{0,1},{1,0},{2,3},{3,2},{4,5},{5,4},{6,7},{7,6},{8,9},{9,8},{10,11... | collective-permute-start | bytes 1769480 | tf_op jit(solution)/shard_map/ppermute | solution.py:390
  173.3 13.8 %collective-permute-start.7 = (bf16[256,768]{1,0:T(8,128)(2,1)S(1)}, bf16[256,768]{1,0:T(8,128)(2,1)S(1)}, u32[]{:S(2)}, u32[]{:S(2)}) collective-permute-start(bf16[256,768]{1,0:T(8,128)(2,1)S(1)} %collective-permute-done.6), channel_id=1, source_target_pairs={{4,6},{2,0},{5,7},{3,1},{12,14},{10,8},{13,15},{11,9},{20,22},{18,... | collective-permute-start | bytes 1179656 | tf_op jit(solution)/shard_map/ppermute | solution.py:407
  176.7 26.5 %collective-permute-start.56 = (bf16[2,2,96,768]{3,2,1,0:T(8,128)(2,1)}, bf16[2,2,96,768]{3,2,1,0:T(8,128)(2,1)}, u32[]{:S(2)}, u32[]{:S(2)}) collective-permute-start(bf16[2,2,96,768]{3,2,1,0:T(8,128)(2,1)} %pad_maximum_fusion.12), channel_id=1, source_target_pairs={{0,8},{8,0},{1,9},{9,1},{2,10},{10,2},{3,11},{11,3},{4,12},{12,4},... | collective-permute-start | bytes 1769480 | tf_op jit(solution)/shard_map/ppermute | solution.py:390
  178.2 26.6 %collective-permute-start.54 = (bf16[2,2,96,768]{3,2,1,0:T(8,128)(2,1)}, bf16[2,2,96,768]{3,2,1,0:T(8,128)(2,1)}, u32[]{:S(2)}, u32[]{:S(2)}) collective-permute-start(bf16[2,2,96,768]{3,2,1,0:T(8,128)(2,1)} %pad_maximum_fusion.11), channel_id=1, source_target_pairs={{0,16},{16,0},{1,17},{17,1},{2,18},{18,2},{3,19},{19,3},{4,20},{20... | collective-permute-start | bytes 1769480 | tf_op jit(solution)/shard_map/ppermute | solution.py:390
  187.1 59.7 %collective-permute-start.48 = (bf16[2,2,48,1536]{3,2,1,0:T(8,128)(2,1)}, bf16[2,2,48,1536]{3,2,1,0:T(8,128)(2,1)}, u32[]{:S(2)}, u32[]{:S(2)}) collective-permute-start(bf16[2,2,48,1536]{3,2,1,0:T(8,128)(2,1)} %pad_maximum_fusion.10), channel_id=1, source_target_pairs={{0,8},{8,0},{1,9},{9,1},{2,10},{10,2},{3,11},{11,3},{4,12},{12,4},... | collective-permute-start | bytes 1769480 | tf_op jit(solution)/shard_map/ppermute | solution.py:390
  203.2 55.3 %collective-permute-start.46 = (bf16[2,2,48,1536]{3,2,1,0:T(8,128)(2,1)}, bf16[2,2,48,1536]{3,2,1,0:T(8,128)(2,1)}, u32[]{:S(2)}, u32[]{:S(2)}) collective-permute-start(bf16[2,2,48,1536]{3,2,1,0:T(8,128)(2,1)} %pad_maximum_fusion.9), channel_id=1, source_target_pairs={{0,16},{16,0},{1,17},{17,1},{2,18},{18,2},{3,19},{19,3},{4,20},{20... | collective-permute-start | bytes 1769480 | tf_op jit(solution)/shard_map/ppermute | solution.py:390
  237.9 12.0 %collective-permute-start.27 = (bf16[256,192]{0,1:T(8,128)(2,1)S(1)}, bf16[256,192]{0,1:T(8,128)(2,1)S(1)}, u32[]{:S(2)}, u32[]{:S(2)}) collective-permute-start(bf16[256,192]{0,1:T(8,128)(2,1)S(1)} %bitcast.709), channel_id=1, source_target_pairs={{0,2},{2,4},{4,6},{6,0},{1,3},{3,5},{5,7},{7,1},{8,10},{10,12},{12... | collective-permute-start | bytes 294920 | tf_op jit(solution)/shard_map/ppermute | solution.py:390
  238.7 13.9 %collective-permute-start.28 = (bf16[256,192]{0,1:T(8,128)(2,1)}, bf16[256,192]{0,1:T(8,128)(2,1)S(1)}, u32[]{:S(2)}, u32[]{:S(2)}) collective-permute-start(bf16[256,192]{0,1:T(8,128)(2,1)} %bitcast.710), channel_id=1, source_target_pairs={{0,4},{2,6},{4,0},{6,2},{1,5},{3,7},{5,1},{7,3},{8,12},{10,14},{12... | collective-permute-start | bytes 294920 | tf_op jit(solution)/shard_map/ppermute | solution.py:390
  268.1 14.2 %collective-permute-start.59 = (bf16[256,768]{1,0:T(8,128)(2,1)}, bf16[256,768]{1,0:T(8,128)(2,1)S(1)}, u32[]{:S(2)}, u32[]{:S(2)}) collective-permute-start(bf16[256,768]{1,0:T(8,128)(2,1)} %slice.342), channel_id=1, source_target_pairs={{0,1},{1,0},{2,3},{3,2},{4,5},{5,4},{6,7},{7,6},{8,9},{9,8},{10,11... | collective-permute-start | bytes 1179656 | tf_op jit(solution)/shard_map/ppermute | solution.py:390
  271.1 12.5 %collective-permute-start.57 = (bf16[256,768]{1,0:T(8,128)(2,1)S(1)}, bf16[256,768]{1,0:T(8,128)(2,1)}, u32[]{:S(2)}, u32[]{:S(2)}) collective-permute-start(bf16[256,768]{1,0:T(8,128)(2,1)S(1)} %slice.343), channel_id=1, source_target_pairs={{0,1},{1,0},{2,3},{3,2},{4,5},{5,4},{6,7},{7,6},{8,9},{9,8},{10,11... | collective-permute-start | bytes 1179656 | tf_op jit(solution)/shard_map/ppermute | solution.py:390
  275.5 66.2 %collective-permute-start.91 = (bf16[2,2,48,1536]{3,2,1,0:T(8,128)(2,1)}, bf16[2,2,48,1536]{3,2,1,0:T(8,128)(2,1)}, u32[]{:S(2)}, u32[]{:S(2)}) collective-permute-start(bf16[2,2,48,1536]{3,2,1,0:T(8,128)(2,1)} %dynamic-slice_bitcast_fusion.4), channel_id=1, source_target_pairs={{0,16},{16,0},{1,17},{17,1},{2,18},{18,2},{3,19},{19,3},{4,20},{20... | collective-permute-start | bytes 1769480 | tf_op jit(solution)/shard_map/ppermute | solution.py:390
  276.4 71.5 %collective-permute-start.93 = (bf16[2,2,48,1536]{3,2,1,0:T(8,128)(2,1)}, bf16[2,2,48,1536]{3,2,1,0:T(8,128)(2,1)}, u32[]{:S(2)}, u32[]{:S(2)}) collective-permute-start(bf16[2,2,48,1536]{3,2,1,0:T(8,128)(2,1)} %dynamic-slice_bitcast_fusion.3), channel_id=1, source_target_pairs={{0,8},{8,0},{1,9},{9,1},{2,10},{10,2},{3,11},{11,3},{4,12},{12,4},... | collective-permute-start | bytes 1769480 | tf_op jit(solution)/shard_map/ppermute | solution.py:390
  302.0 47.4 %collective-permute-start.99 = (bf16[2,2,96,768]{3,2,1,0:T(8,128)(2,1)}, bf16[2,2,96,768]{3,2,1,0:T(8,128)(2,1)}, u32[]{:S(2)}, u32[]{:S(2)}) collective-permute-start(bf16[2,2,96,768]{3,2,1,0:T(8,128)(2,1)} %dynamic-slice_bitcast_fusion.2), channel_id=1, source_target_pairs={{0,16},{16,0},{1,17},{17,1},{2,18},{18,2},{3,19},{19,3},{4,20},{20... | collective-permute-start | bytes 1769480 | tf_op jit(solution)/shard_map/ppermute | solution.py:390
  303.6 47.2 %collective-permute-start.101 = (bf16[2,2,96,768]{3,2,1,0:T(8,128)(2,1)}, bf16[2,2,96,768]{3,2,1,0:T(8,128)(2,1)}, u32[]{:S(2)}, u32[]{:S(2)}) collective-permute-start(bf16[2,2,96,768]{3,2,1,0:T(8,128)(2,1)} %dynamic-slice_bitcast_fusion.1), channel_id=1, source_target_pairs={{0,8},{8,0},{1,9},{9,1},{2,10},{10,2},{3,11},{11,3},{4,12},{12,4},... | collective-permute-start | bytes 1769480 | tf_op jit(solution)/shard_map/ppermute | solution.py:390
  305.2 62.7 %collective-permute-start.83 = (bf16[2,2,4,24,768]{4,3,2,0,1:T(8,128)(2,1)}, bf16[2,2,4,24,768]{4,3,2,0,1:T(8,128)(2,1)}, u32[]{:S(2)}, u32[]{:S(2)}) collective-permute-start(bf16[2,2,4,24,768]{4,3,2,0,1:T(8,128)(2,1)} %bitcast.652), channel_id=1, source_target_pairs={{0,1},{1,0},{2,3},{3,2},{4,5},{5,4},{6,7},{7,6},{8,9},{9,8},{10,11... | collective-permute-start | bytes 1769480 | tf_op jit(solution)/shard_map/ppermute | solution.py:390
  341.7 64.9 %collective-permute-start.63 = (bf16[4,256,384]{2,1,0:T(8,128)(2,1)}, bf16[4,256,384]{2,1,0:T(8,128)(2,1)}, u32[]{:S(2)}, u32[]{:S(2)}) collective-permute-start(bf16[4,256,384]{2,1,0:T(8,128)(2,1)} %dynamic-slice_bitcast_fusion), channel_id=1, source_target_pairs={{0,1},{1,0},{2,3},{3,2},{4,5},{5,4},{6,7},{7,6},{8,9},{9,8},{10,11... | collective-permute-start | bytes 2359304 | tf_op jit(solution)/shard_map/ppermute | solution.py:390
  350.8 13.2 %collective-permute-start.100 = (bf16[2,96,768]{2,1,0:T(8,128)(2,1)S(1)}, bf16[2,96,768]{2,1,0:T(8,128)(2,1)S(1)}, u32[]{:S(2)}, u32[]{:S(2)}) collective-permute-start(bf16[2,96,768]{2,1,0:T(8,128)(2,1)S(1)} %fusion.44), channel_id=1, source_target_pairs={{0,8},{8,0},{1,9},{9,1},{2,10},{10,2},{3,11},{11,3},{4,12},{12,4},... | collective-permute-start | bytes 884744 | tf_op jit(solution)/shard_map/ppermute | solution.py:390
  359.3 13.9 %collective-permute-start.97 = (bf16[48,1536]{1,0:T(8,128)(2,1)S(1)}, bf16[48,1536]{1,0:T(8,128)(2,1)S(1)}, u32[]{:S(2)}, u32[]{:S(2)}) collective-permute-start(bf16[48,1536]{1,0:T(8,128)(2,1)S(1)} %get-tuple-element.63), channel_id=1, source_target_pairs={{0,6},{2,0},{4,2},{6,4},{1,7},{3,1},{5,3},{7,5},{8,14},{10,8},{12,... | collective-permute-start | bytes 442376 | tf_op jit(solution)/shard_map/ppermute | solution.py:390
  364.0 14.7 %collective-permute-start.96 = (bf16[48,1536]{1,0:T(8,128)(2,1)S(1)}, bf16[48,1536]{1,0:T(8,128)(2,1)S(1)}, u32[]{:S(2)}, u32[]{:S(2)}) collective-permute-start(bf16[48,1536]{1,0:T(8,128)(2,1)S(1)} %get-tuple-element.62), channel_id=1, source_target_pairs={{0,4},{2,6},{4,0},{6,2},{1,5},{3,7},{5,1},{7,3},{8,12},{10,14},{12... | collective-permute-start | bytes 442376 | tf_op jit(solution)/shard_map/ppermute | solution.py:390
  366.5 12.2 %collective-permute-start.95 = (bf16[48,1536]{1,0:T(8,128)(2,1)S(1)}, bf16[48,1536]{1,0:T(8,128)(2,1)S(1)}, u32[]{:S(2)}, u32[]{:S(2)}) collective-permute-start(bf16[48,1536]{1,0:T(8,128)(2,1)S(1)} %get-tuple-element.61), channel_id=1, source_target_pairs={{0,2},{2,4},{4,6},{6,0},{1,3},{3,5},{5,7},{7,1},{8,10},{10,12},{12... | collective-permute-start | bytes 442376 | tf_op jit(solution)/shard_map/ppermute | solution.py:390
  367.9 10.9 %collective-permute-start.105 = (bf16[96,768]{1,0:T(8,128)(2,1)S(1)}, bf16[96,768]{1,0:T(8,128)(2,1)S(1)}, u32[]{:S(2)}, u32[]{:S(2)}) collective-permute-start(bf16[96,768]{1,0:T(8,128)(2,1)S(1)} %get-tuple-element.60), channel_id=1, source_target_pairs={{0,6},{2,0},{4,2},{6,4},{1,7},{3,1},{5,3},{7,5},{8,14},{10,8},{12,... | collective-permute-start | bytes 442376 | tf_op jit(solution)/shard_map/ppermute | solution.py:390
  373.2 16.3 %collective-permute-start.104 = (bf16[96,768]{1,0:T(8,128)(2,1)S(1)}, bf16[96,768]{1,0:T(8,128)(2,1)S(1)}, u32[]{:S(2)}, u32[]{:S(2)}) collective-permute-start(bf16[96,768]{1,0:T(8,128)(2,1)S(1)} %get-tuple-element.59), channel_id=1, source_target_pairs={{0,4},{2,6},{4,0},{6,2},{1,5},{3,7},{5,1},{7,3},{8,12},{10,14},{12... | collective-permute-start | bytes 442376 | tf_op jit(solution)/shard_map/ppermute | solution.py:390
  378.7 12.6 %collective-permute-start.84 = (bf16[2,2,24,768]{3,2,1,0:T(8,128)(2,1)}, bf16[2,2,24,768]{3,2,1,0:T(8,128)(2,1)S(1)}, u32[]{:S(2)}, u32[]{:S(2)}) collective-permute-start(bf16[2,2,24,768]{3,2,1,0:T(8,128)(2,1)} %fusion.71), channel_id=1, source_target_pairs={{0,16},{16,0},{1,17},{17,1},{2,18},{18,2},{3,19},{19,3},{4,20},{20... | collective-permute-start | bytes 442376 | tf_op jit(solution)/shard_map/ppermute | solution.py:390
  378.8 13.0 %collective-permute-start.86 = (bf16[2,2,24,768]{3,2,1,0:T(8,128)(2,1)}, bf16[2,2,24,768]{3,2,1,0:T(8,128)(2,1)}, u32[]{:S(2)}, u32[]{:S(2)}) collective-permute-start(bf16[2,2,24,768]{3,2,1,0:T(8,128)(2,1)} %fusion.72), channel_id=1, source_target_pairs={{0,8},{8,0},{1,9},{9,1},{2,10},{10,2},{3,11},{11,3},{4,12},{12,4},... | collective-permute-start | bytes 442376 | tf_op jit(solution)/shard_map/ppermute | solution.py:390
  414.4 34.9 %collective-permute-start.66 = (bf16[256,768]{1,0:T(8,128)(2,1)S(1)}, bf16[256,768]{1,0:T(8,128)(2,1)}, u32[]{:S(2)}, u32[]{:S(2)}) collective-permute-start(bf16[256,768]{1,0:T(8,128)(2,1)S(1)} %get-tuple-element.45), channel_id=1, source_target_pairs={{0,6},{2,0},{4,2},{6,4},{1,7},{3,1},{5,3},{7,5},{8,14},{10,8},{12,... | collective-permute-start | bytes 1179656 | tf_op jit(solution)/shard_map/ppermute | solution.py:390
  414.7 34.7 %collective-permute-start.65 = (bf16[256,768]{1,0:T(8,128)(2,1)S(1)}, bf16[256,768]{1,0:T(8,128)(2,1)}, u32[]{:S(2)}, u32[]{:S(2)}) collective-permute-start(bf16[256,768]{1,0:T(8,128)(2,1)S(1)} %get-tuple-element.46), channel_id=1, source_target_pairs={{0,4},{2,6},{4,0},{6,2},{1,5},{3,7},{5,1},{7,3},{8,12},{10,14},{12... | collective-permute-start | bytes 1179656 | tf_op jit(solution)/shard_map/ppermute | solution.py:390
  431.7 15.8 %collective-permute-start.73 = (f32[1,288]{1,0:T(1,128)S(1)}, f32[1,288]{1,0:T(1,128)S(1)}, u32[]{:S(2)}, u32[]{:S(2)}) collective-permute-start(f32[1,288]{1,0:T(1,128)S(1)} %get-tuple-element.182), channel_id=1, source_target_pairs={{0,4},{2,6},{4,0},{6,2},{1,5},{3,7},{5,1},{7,3},{8,12},{10,14},{12... | collective-permute-start | bytes 3464 | tf_op jit(solution)/shard_map/ppermute | solution.py:390
  431.7 15.8 %collective-permute-start.72 = (f32[1,288]{1,0:T(1,128)S(1)}, f32[1,288]{1,0:T(1,128)S(1)}, u32[]{:S(2)}, u32[]{:S(2)}) collective-permute-start(f32[1,288]{1,0:T(1,128)S(1)} %get-tuple-element.181), channel_id=1, source_target_pairs={{0,2},{2,4},{4,6},{6,0},{1,3},{3,5},{5,7},{7,1},{8,10},{10,12},{12... | collective-permute-start | bytes 3464 | tf_op jit(solution)/shard_map/ppermute | solution.py:390
  433.4 19.4 %collective-permute-start.64 = (bf16[256,768]{1,0:T(8,128)(2,1)S(1)}, bf16[256,768]{1,0:T(8,128)(2,1)S(1)}, u32[]{:S(2)}, u32[]{:S(2)}) collective-permute-start(bf16[256,768]{1,0:T(8,128)(2,1)S(1)} %get-tuple-element.44), channel_id=1, source_target_pairs={{0,2},{2,4},{4,6},{6,0},{1,3},{3,5},{5,7},{7,1},{8,10},{10,12},{12... | collective-permute-start | bytes 1179656 | tf_op jit(solution)/shard_map/ppermute | solution.py:390
  (164 other events, 1096.3 us)

commit v3 on v2

--- a/solution.py
+++ b/solution.py
@@ -400,11 +400,16 @@
     return jnp.stack([first, second], axis=axis)
 
 
-def z_spread(block, z):
+def z_pieces(block):
     up = lax.ppermute(block, "z", [(0, 1), (1, 2), (2, 3)])
     down = lax.ppermute(block, "z", [(1, 0), (2, 1), (3, 2)])
     far = shift(block, "z", NZ, 2)
-    last = lax.ppermute(far, "z", [(2, 3), (1, 0)])
+    last = lax.ppermute(after(far, up, down), "z", [(2, 3), (1, 0)])
+    return up, down, far, last
+
+
+def z_select(block, pieces, z):
+    up, down, far, last = pieces
     return jnp.stack(
         [
             lax.select_n(z, block, up, far, last),
@@ -423,16 +428,18 @@
     return [pick(array, z)] + [shift(pick(array, (z + j) % NZ), "z", NZ, j) for j in range(1, NZ)]
 
 
-def xy_gather(line, y, x):
+def xy_gather(line, y, x, event=None):
     a, b = line[:2], line[2:]
     a = in_order(a, swap(a, "x"), x, 0)
     b = in_order(b, swap(b, "y"), y, 0)
+    if event is not None:
+        a, b = after(a, event), after(b, event)
     a = in_order(a, swap(a, "y"), y, 0)
     b = in_order(b, swap(b, "x"), x, 1)
     return jnp.concatenate([a, b], axis=2)
 
 
-def xy_scatter(blocks, y, x, wire):
+def xy_scatter(blocks, y, x, wire, event=None):
     def halve(array, axis, name, index):
         sent = swap(pick(array, 1 - index, axis).astype(wire), name)
         return pick(array, index, axis).astype(jnp.float32) + sent.astype(jnp.float32)
@@ -440,9 +447,16 @@
     a, b = blocks[:, :, :2], blocks[:, :, 2:]
     a = halve(a, 0, "y", y)
     b = halve(b, 1, "x", x)
+    if event is not None:
+        a, b = after(a, event), after(b, event)
     a = halve(a, 0, "x", x)
     b = halve(b, 0, "y", y)
     return jnp.concatenate([a, b], axis=0)
+
+
+def after(value, *events):
+    flag = sum(e[(slice(0, 1),) * e.ndim].reshape(()).astype(jnp.float32) * 0.0 for e in events)
+    return jnp.where(flag != 0.0, jnp.zeros_like(value), value)
 
 
 def z_collect(line, z, wire):
@@ -459,12 +473,6 @@
     ]
 
 
-def norm_stats(values):
-    center = values - jnp.mean(values, axis=-1, keepdims=True)
-    scale = lax.rsqrt(jnp.mean(center * center, axis=-1, keepdims=True) + 1e-05)
-    return center * scale, scale
-
-
 def norm_back(grad, gain, unit, scale):
     c = grad * gain
     return scale * (
@@ -484,57 +492,459 @@
     return lax.dot_general(a, b, (((1,), (0,)), ((), ())), preferred_element_type=jnp.float32)
 
 
+def column_of(row):
+    return jnp.transpose(jnp.broadcast_to(row, (8, row.shape[1])))[:, 0:1]
+
+
+def query_row(may_ref, tile, block, seg_row):
+    per = CHUNK // BLOCK
+    lane = lax.broadcasted_iota(jnp.int32, (1, CHUNK), 1)
+    flag = jnp.full((1, CHUNK), may_ref[tile * per, block], jnp.int32)
+    for b in range(1, per):
+        flag = jnp.where(lane >= b * BLOCK, may_ref[tile * per + b, block], flag)
+    return jnp.where(flag > 0, seg_row, -1.0)
+
+
+def permit_of(may_ref, tile, chunk, seg_row, key_column):
+    per = CHUNK // BLOCK
+    return jnp.concatenate(
+        [
+            key_column[b * BLOCK : (b + 1) * BLOCK]
+            == query_row(may_ref, tile, chunk * per + b, seg_row)
+            for b in range(per)
+        ],
+        axis=0,
+    )
+
+
+def whole_spec(shape):
+    return pl.BlockSpec(shape, lambda *_: (0,) * len(shape))
+
+
+def kernel_call(body, place, arrays, in_specs, outs, out_specs, grid, scratch, flops, name, more=()):
+    prefetch = (place,) + tuple(more)
+    moved = sum(a.size * a.dtype.itemsize for a in arrays)
+    return pl.pallas_call(
+        body,
+        out_shape=tuple(jax.ShapeDtypeStruct(shape, dtype) for shape, dtype in outs),
+        grid_spec=pltpu.PrefetchScalarGridSpec(
+            num_scalar_prefetch=len(prefetch),
+            grid=grid,
+            in_specs=in_specs,
+            out_specs=out_specs,
+            scratch_shapes=scratch,
+        ),
+        compiler_params=pltpu.CompilerParams(vmem_limit_bytes=40 << 20),
+        cost_estimate=pl.CostEstimate(flops=flops, bytes_accessed=moved, transcendentals=0),
+        name=name,
+    )(*prefetch, *arrays)
+
+
+def lane_groups(lanes, size):
+    lane = lax.broadcasted_iota(jnp.int32, (1, lanes), 1).astype(jnp.float32)
+    group = jnp.floor((lane + 0.5) * (1.0 / size))
+    return group, lane - group * size
+
+
+def one_hot_rows(place_row, count):
+    rows = lax.broadcasted_iota(jnp.int32, (count, place_row.shape[1]), 0).astype(jnp.float32)
+    return (rows == place_row).astype(jnp.float32).astype(jnp.bfloat16)
+
+
+VEC_ROWS = 16
+
+
+def unpack_kernel(place_ref, packed_ref, vec_ref):
+    devices = packed_ref.shape[0]
+    width = vec_ref.shape[1]
+    size = width // devices
+    c = place_ref[1]
+    device = lax.broadcasted_iota(jnp.int32, (devices, 1), 0)
+    parity = lax.rem(device, 2)
+    pair = lax.div(device, 2).astype(jnp.float32)
+    device = device.astype(jnp.float32)
+    vec_ref[...] = jnp.zeros(vec_ref.shape, jnp.float32)
+
+    def spread(start, n, lanes, owner, keep):
+        group, at = lane_groups(lanes, n)
+        tiled = dot_nn(packed_ref[:, start : start + n], one_hot_rows(at, n))
+        mine = (owner == group) if keep is None else (owner == group) & keep
+        return jnp.sum(jnp.where(mine, tiled, 0.0), axis=0, keepdims=True)
+
+    vec_ref[0:1] = spread(0, size, width, device, None)
+    vec_ref[1:2] = spread(size, size, width, device, None)
+    qv = spread(2 * size, 2 * size, 2 * width, device, None)
+    vec_ref[2:3] = qv[:, :width]
+    vec_ref[3:4] = qv[:, width:]
+    vec_ref[4:5] = spread(4 * size, size, width, device, None)
+    vec_ref[5:6] = spread(5 * size, size, width, device, None)
+    vec_ref[6:7] = spread(6 * size, size, width, device, None)
+    up = spread(7 * size, 4 * size, 2 * width, pair, parity == c)
+    vec_ref[8:9] = up[:, :width]
+    vec_ref[9:10] = up[:, width:]
+    vec_ref[7:8] = spread(11 * size, size, width, device, None)
+
+
+def pack_kernel(place_ref, grads_ref, mid_ref, qkv_ref, up_ref, packed_ref):
+    devices = packed_ref.shape[0]
+    width = grads_ref.shape[1]
+    size = width // devices
+    z, c = place_ref[0], place_ref[1]
+    device = lax.broadcasted_iota(jnp.int32, (devices, 1), 0)
+    parity = lax.rem(device, 2)
+    pair = lax.div(device, 2).astype(jnp.float32)
+    device = device.astype(jnp.float32)
+    packed_ref[...] = jnp.zeros(packed_ref.shape, jnp.bfloat16)
+
+    def gather(row, n, owner, keep):
+        group, at = lane_groups(row.shape[1], n)
+        mine = (owner == group) if keep is None else (owner == group) & keep
+        return dot_nt(jnp.where(mine, row, 0.0).astype(jnp.bfloat16), one_hot_rows(at, n))
+
+    def place_group(row):
+        wide = jnp.concatenate([row] * NZ, axis=1)
+        group, _ = lane_groups(wide.shape[1], GW)
+        return jnp.where(group == z.astype(jnp.float32), wide, 0.0)
+
+    qkv = qkv_ref[0:1]
+    qv = jnp.concatenate([place_group(qkv[:, :GW]), place_group(qkv[:, 2 * GW :])], axis=1)
+    parts = [
+        gather(grads_ref[0:1], size, device, None),
+        gather(grads_ref[1:2], size, device, None),
+        gather(qv, 2 * size, device, None),
+        gather(mid_ref[2:3], size, device, None),
+        gather(mid_ref[0:1], size, device, None),
+        gather(mid_ref[1:2], size, device, None),
+        gather(up_ref[0:1], 4 * size, pair, parity == c),
+        gather(mid_ref[3:4], size, device, None),
+    ]
+    packed_ref[:, 0 : 12 * size] = jnp.concatenate(parts, axis=1).astype(jnp.bfloat16)
+
+
+def norm_rows(x):
+    center = x - jnp.mean(x, axis=-1, keepdims=True)
+    scale = lax.rsqrt(jnp.mean(center * center, axis=-1, keepdims=True) + 1e-05)
+    return center * scale, scale
+
+
+def project_kernel(
+    place_ref, own_ref, up_ref, down_ref, far_ref, last_ref, vec_ref, wz_ref, line_ref, n1_ref, q_ref, kv_ref
+):
+    a = pl.program_id(0)
+    z = place_ref[0]
+    away = a - z
+    x = jnp.where(away == 0, own_ref[...].astype(jnp.float32), far_ref[...].astype(jnp.float32))
+    x = jnp.where(away == 1, down_ref[...].astype(jnp.float32), x)
+    x = jnp.where(away == -1, up_ref[...].astype(jnp.float32), x)
+    x = jnp.where(jnp.abs(away) == 3, last_ref[...].astype(jnp.float32), x)
+    line_ref[...] = x.astype(jnp.bfloat16)
+    unit, _ = norm_rows(x)
+    n1 = (unit * vec_ref[0:1] + vec_ref[1:2]).astype(jnp.bfloat16)
+    n1_ref[...] = n1
+    y = dot_nn(n1, wz_ref[...])
+    q_bias, v_bias = vec_ref[2:3, 0:GW], vec_ref[3:4, 0:GW]
+    for g in range(1, NZ):
+        q_bias = jnp.where(z == g, vec_ref[2:3, g * GW : (g + 1) * GW], q_bias)
+        v_bias = jnp.where(z == g, vec_ref[3:4, g * GW : (g + 1) * GW], v_bias)
+    q = (y[:, :GW] + q_bias).astype(jnp.bfloat16)
+    q_ref[...] = q * jnp.asarray(SCORE_SCALE, jnp.bfloat16)
+    kv_ref[:, :GW] = y[:, GW : 2 * GW].astype(jnp.bfloat16)
+    kv_ref[:, GW:] = (y[:, 2 * GW :] + v_bias).astype(jnp.bfloat16)
+
+
+def project(place, own, up, down, far, last, vec, wz):
+    rows, width = own.shape
+    low = jnp.bfloat16
+    tall = lambda w: pl.BlockSpec((rows, w), lambda a, *_: (a, 0))
+    return kernel_call(
+        project_kernel, place, (own, up, down, far, last, vec, wz),
+        [whole_spec((rows, width))] * 5 + [whole_spec(vec.shape), whole_spec(wz.shape)],
+        [((NZ * rows, width), low), ((NZ * rows, width), low), ((NZ * rows, GW), low), ((NZ * rows, 2 * GW), low)],
+        [tall(width), tall(width), tall(GW), tall(2 * GW)],
+        (NZ,), [], 8 * NZ * rows * width * 3 * GW, "project",
+    )
+
+
+def branch_kernel(place_ref, a0_ref, a1_ref, a2_ref, a3_ref, wo_ref, own_ref, vec_ref, hidden_ref, n2_ref):
+    z = place_ref[0]
+    total = own_ref[...].astype(jnp.float32) + vec_ref[4:5]
+    branch = None
+    for j, ref in enumerate((a0_ref, a1_ref, a2_ref, a3_ref)):
+        start = pl.multiple_of(lax.rem(z - j + NZ, NZ) * GW, GW)
+        part = dot_nn(ref[...], wo_ref[pl.ds(start, GW), :])
+        branch = part if branch is None else branch + part
+    hidden = total + branch
+    hidden_ref[...] = hidden
+    unit, _ = norm_rows(hidden)
+    n2_ref[...] = (unit * vec_ref[5:6] + vec_ref[6:7]).astype(jnp.bfloat16)
+
+
+def branch_call(place, pieces, wo, own, vec):
+    rows, width = own.shape
+    arrays = (*pieces, wo, own, vec)
+    return kernel_call(
+        branch_kernel, place, arrays, [whole_spec(a.shape) for a in arrays],
+        [((rows, width), jnp.float32), ((rows, width), jnp.bfloat16)],
+        [whole_spec((rows, width))] * 2, (1,), [], 8 * rows * width * width, "branch",
+    )
+
+
+FF_STEP = 512
+
+
+def feed_kernel(
+    place_ref, na_ref, nb_ref, ga_ref, gb_ref, up_ref, down_ref, bias_ref,
+    act_ref, grad_ref, out_ref, m_ref, sums_ref, bias_out_ref, n_s, g_s, out_s, m_s,
+):
+    k = pl.program_id(0)
+    rows = na_ref.shape[0]
+
+    @pl.when(k == 0)
+    def _():
+        n_s[:rows], n_s[rows:] = na_ref[...], nb_ref[...]
+        g_s[:rows], g_s[rows:] = ga_ref[...], gb_ref[...]
+        out_s[...] = jnp.zeros(out_s.shape, jnp.float32)
+        m_s[...] = jnp.zeros(m_s.shape, jnp.float32)
+
+    up, down = up_ref[...], down_ref[...]
+    v = dot_nn(n_s[...], up) + bias_ref[...]
+    cdf = 0.5 * (1.0 + lax.erf(v * 0.7071067811865476))
+    slope = cdf + v * (0.3989422804014327 * jnp.exp(-0.5 * v * v))
+    act = (v * cdf).astype(jnp.bfloat16)
+    act_ref[...] = act
+    grad = dot_nt(g_s[...], down) * slope
+    grad = grad.astype(jnp.bfloat16)
+    grad_ref[...] = grad
+    bias_out_ref[...] = jnp.sum(grad.astype(jnp.float32), axis=0, keepdims=True)
+    out_s[...] += dot_nn(act, down)
+    m_s[...] += dot_nt(grad, up)
+
+    @pl.when(k == pl.num_programs(0) - 1)
+    def _():
+        out_ref[...] = out_s[:rows]
+        m_ref[...] = m_s[:rows]
+        sums_ref[0] = m_s[rows:].astype(jnp.bfloat16)
+        sums_ref[1] = out_s[rows:].astype(jnp.bfloat16)
+
+
+def feed(place, na, nb, ga, gb, up, down, bias):
+    rows, width = na.shape
+    half = up.shape[1]
+    low, wide = jnp.bfloat16, jnp.float32
+    one = whole_spec((rows, width))
+    across = lambda r: pl.BlockSpec((r, FF_STEP), lambda k, *_: (0, k))
+    return kernel_call(
+        feed_kernel, place, (na, nb, ga, gb, up, down, bias),
+        [one] * 4 + [across(width), pl.BlockSpec((FF_STEP, width), lambda k, *_: (k, 0)), across(1)],
+        [
+            ((2 * rows, half), low), ((2 * rows, half), low), ((rows, width), wide), ((rows, width), wide),
+            ((2, rows, width), low), ((1, half), wide),
+        ],
+        [across(2 * rows), across(2 * rows), one, one, whole_spec((2, rows, width)), across(1)],
+        (half // FF_STEP,),
+        [
+            pltpu.VMEM((2 * rows, width), low), pltpu.VMEM((2 * rows, width), low),
+            pltpu.VMEM((2 * rows, width), wide), pltpu.VMEM((2 * rows, width), wide),
+        ],
+        32 * rows * width * half, "feed",
+    )
+
+
+def middle_kernel(
+    place_ref, m_ref, out_ref, sums_ref, hidden_ref, go_ref, vec_ref, wo_ref,
+    output_ref, gh_ref, branch_ref, d0_ref, d1_ref, d2_ref, d3_ref, cols_ref,
+):
+    z = place_ref[0]
+    hidden, go = hidden_ref[...], go_ref[...].astype(jnp.float32)
+    output_ref[...] = (hidden + out_ref[...] + sums_ref[1].astype(jnp.float32) + vec_ref[7:8]).astype(
+        jnp.bfloat16
+    )
+    m = m_ref[...] + sums_ref[0].astype(jnp.float32)
+    unit, scale = norm_rows(hidden)
+    grad_hidden = go + norm_back(m, vec_ref[5:6], unit, scale)
+    gh_ref[...] = grad_hidden
+    branch = grad_hidden.astype(jnp.bfloat16)
+    branch_ref[...] = branch
+    for j, ref in enumerate((d0_ref, d1_ref, d2_ref, d3_ref)):
+        start = pl.multiple_of(lax.rem(z + j, NZ) * GW, GW)
+        ref[...] = dot_nt(branch, wo_ref[pl.ds(start, GW), :]).astype(jnp.bfloat16)
+    cols_ref[...] = jnp.zeros(cols_ref.shape, jnp.float32)
+    cols_ref[0:1] = jnp.sum(m * unit, axis=0, keepdims=True)
+    cols_ref[1:2] = jnp.sum(m, axis=0, keepdims=True)
+    cols_ref[2:3] = jnp.sum(branch.astype(jnp.float32), axis=0, keepdims=True)
+    cols_ref[3:4] = jnp.sum(go, axis=0, keepdims=True)
+
+
+def middle(place, m, out, sums, hidden, go, vec, wo):
+    rows, width = m.shape
+    arrays = (m, out, sums, hidden, go, vec, wo)
+    low, wide = jnp.bfloat16, jnp.float32
+    outs = [((rows, width), low), ((rows, width), wide), ((rows, width), low)]
+    outs += [((rows, GW), low)] * NZ + [((8, width), wide)]
+    return kernel_call(
+        middle_kernel, place, arrays, [whole_spec(a.shape) for a in arrays], outs,
+        [whole_spec(shape) for shape, _ in outs], (1,), [], 8 * rows * width * width, "middle",
+    )
+
+
+def inward_kernel(
+    place_ref, dq_ref, mine_ref, theirs_ref, line_ref, wz_ref, dqkv_ref, keep_ref, sent_ref, cols_ref, sums_ref
+):
+    j = pl.program_id(0)
+    dq = dq_ref[...]
+    dkv = (mine_ref[...].astype(jnp.float32) + theirs_ref[...].astype(jnp.float32)).astype(jnp.bfloat16)
+    dqkv = jnp.concatenate([dq, dkv], axis=1)
+    dqkv_ref[...] = dqkv
+    m1 = dot_nt(dqkv, wz_ref[...])
+    sent_ref[0] = m1.astype(jnp.bfloat16)
+    unit, _ = norm_rows(line_ref[...].astype(jnp.float32))
+
+    @pl.when(j == 0)
+    def _():
+        cols_ref[...] = jnp.zeros(cols_ref.shape, jnp.float32)
+        sums_ref[...] = jnp.zeros(sums_ref.shape, jnp.float32)
+
+    cols_ref[0:1] += jnp.sum(m1 * unit, axis=0, keepdims=True)
+    cols_ref[1:2] += jnp.sum(m1, axis=0, keepdims=True)
+    sums_ref[0:1] += jnp.sum(dqkv.astype(jnp.float32), axis=0, keepdims=True)
+
+    @pl.when(j == pl.num_programs(0) - 1)
+    def _():
+        keep_ref[...] = m1
+
+
+def inward(place, dq, mine, theirs, line, wz):
+    total, width = line.shape
+    rows = total // NZ
+    low, wide = jnp.bfloat16, jnp.float32
+    turned = lambda w: pl.BlockSpec((rows, w), lambda j, p: (lax.rem(p[0] + 1 + j, NZ), 0))
+    return kernel_call(
+        inward_kernel, place, (dq, mine, theirs, line, wz),
+        [turned(GW), turned(2 * GW), turned(2 * GW), turned(width), whole_spec(wz.shape)],
+        [((total, 3 * GW), low), ((rows, width), wide), ((NZ, rows, width), low), ((8, width), wide), ((8, 3 * GW), wide)],
+        [
+            turned(3 * GW), whole_spec((rows, width)),
+            pl.BlockSpec((1, rows, width), lambda j, p: (j, 0, 0)),
+            whole_spec((8, width)), whole_spec((8, 3 * GW)),
+        ],
+        (NZ,), [], 8 * total * width * 3 * GW, "inward",
+    )
+
+
+def finish_kernel(place_ref, m_ref, r1_ref, r2_ref, r3_ref, own_ref, gh_ref, vec_ref, out_ref):
+    m = m_ref[...]
+    for ref in (r1_ref, r2_ref, r3_ref):
+        m = m + ref[...].astype(jnp.float32)
+    unit, scale = norm_rows(own_ref[...].astype(jnp.float32))
+    out_ref[...] = gh_ref[...] + norm_back(m, vec_ref[0:1], unit, scale)
+
+
+def finish(place, m, pieces, own, grad_hidden, vec):
+    rows, width = own.shape
+    arrays = (m, *pieces, own, grad_hidden, vec)
+    return kernel_call(
+        finish_kernel, place, arrays, [whole_spec(a.shape) for a in arrays],
+        [((rows, width), jnp.float32)], [whole_spec((rows, width))], (1,), [], 100 * rows * width, "finish",
+    )[0]
+
+
+def owners_kernel(
+    place_ref, a0_ref, a1_ref, a2_ref, a3_ref, branch_ref, n1_ref, dqkv_ref, cols_ref, mid_ref, sums_ref, up_ref,
+    mine_ref, theirs_ref, wo_s, wz_s, vec_s,
+):
+    z, c = place_ref[0], place_ref[1]
+    width = branch_ref.shape[1]
+    for j, ref in enumerate((a0_ref, a1_ref, a2_ref, a3_ref)):
+        start = pl.multiple_of(lax.rem(z - j + NZ, NZ) * GW, GW)
+        wo_s[pl.ds(start, GW), :] = dot_tn(ref[...], branch_ref[...]).astype(jnp.bfloat16)
+    wz_s[...] = dot_tn(n1_ref[...], dqkv_ref[...]).astype(jnp.bfloat16)
+    pack_kernel(place_ref, cols_ref, mid_ref, sums_ref, up_ref, vec_s)
+    chips, tall, span = mine_ref.shape
+    devices = 2 * chips
+    rows = width // devices
+    pad = jnp.zeros((tall - rows, span), jnp.bfloat16)
+    first_row = lax.broadcasted_iota(jnp.int32, (tall - rows, span), 0) == 0
+    for pair in range(chips):
+        blocks = []
+        for core in range(2):
+            at = slice((2 * pair + core) * rows, (2 * pair + core + 1) * rows)
+            vec = vec_s[2 * pair + core : 2 * pair + core + 1]
+            vec = jnp.where(first_row, jnp.broadcast_to(vec.astype(jnp.float32), pad.shape), 0.0)
+            top = jnp.concatenate([wo_s[at], wz_s[at]], axis=1)
+            blocks.append((top, vec.astype(jnp.bfloat16)))
+        mine_ref[pair, :rows] = jnp.where(c == 0, blocks[0][0], blocks[1][0])
+        mine_ref[pair, rows:] = jnp.where(c == 0, blocks[0][1], blocks[1][1])
+        theirs_ref[pair, :rows] = jnp.where(c == 0, blocks[1][0], blocks[0][0])
+        theirs_ref[pair, rows:] = jnp.where(c == 0, blocks[1][1], blocks[0][1])
+
+
+def owners(place, pieces, branch, n1, dqkv, cols, mid, sums, up, devices, tall):
+    width, span = n1.shape[1], n1.shape[1] + dqkv.shape[1]
+    low = jnp.bfloat16
+    arrays = (*pieces, branch, n1, dqkv, cols, mid, sums, up)
+    shape = (devices // 2, tall, span)
+    return kernel_call(
+        owners_kernel, place, arrays, [whole_spec(a.shape) for a in arrays], [(shape, low), (shape, low)],
+        [whole_spec(shape)] * 2, (1,),
+        [pltpu.VMEM((width, width), low), pltpu.VMEM((width, dqkv.shape[1]), low), pltpu.VMEM((devices, span), low)],
+        1 << 20, "owners",
+    )
+
+
 def attend_kernel(
-    act_ref, q_ref, kv_ref, qseg_ref, kseg_ref, o_ref, low_ref, lse_ref, k_s, v_s, m_s, l_s, acc_s
+    act_ref, may_ref, place_ref, q_ref, mine_ref, theirs_ref, qseg_ref, kseg_ref, o_ref, low_ref, lse_ref,
+    k_s, vt_s, col_s, m_s, l_s, acc_s,
 ):
     i = pl.program_id(0)
-    chunks = kv_ref.shape[0] // CHUNK
+    chunks = kseg_ref.shape[0]
 
     @pl.when(i == 0)
     def _():
-        for h in range(GROUP):
-            k_s[h] = kv_ref[:, HEAD_DIM * h : HEAD_DIM * (h + 1)]
-            v_s[h] = kv_ref[:, GW + HEAD_DIM * h : GW + HEAD_DIM * (h + 1)]
+        for line, ref in enumerate((mine_ref, theirs_ref)):
+            core = place_ref[1] if line == 0 else 1 - place_ref[1]
+            for a in range(chunks // 2):
+                rows = slice(a * CHUNK, (a + 1) * CHUNK)
+                at = pl.ds(pl.multiple_of((2 * a + core) * CHUNK, CHUNK), CHUNK)
+                for h in range(GROUP):
+                    k_s[h, at] = ref[rows, HEAD_DIM * h : HEAD_DIM * (h + 1)]
+                    vt_s[h, :, at] = jnp.transpose(ref[rows, GW + HEAD_DIM * h : GW + HEAD_DIM * (h + 1)])
+        for j in range(chunks):
+            col_s[j * CHUNK : (j + 1) * CHUNK] = column_of(kseg_ref[j : j + 1])
 
     m_s[...] = jnp.full(m_s.shape, NEG_FILL, jnp.float32)
     l_s[...] = jnp.zeros(l_s.shape, jnp.float32)
     acc_s[...] = jnp.zeros(acc_s.shape, jnp.float32)
     q_heads = [q_ref[:, HEAD_DIM * h : HEAD_DIM * (h + 1)] for h in range(GROUP)]
-    q_seg = qseg_ref[...]
+    q_seg = qseg_ref[pl.ds(i, 1)]
 
     def one_chunk(j, carry):
         @pl.when(act_ref[i, j] != 0)
         def _():
             at = pl.ds(pl.multiple_of(j * CHUNK, CHUNK), CHUNK)
-            permit = q_seg == kseg_ref[0, :, at]
+            permit = permit_of(may_ref, i, j, q_seg, col_s[at])
             for h in range(GROUP):
-                s = jnp.where(permit, dot_nt(q_heads[h], k_s[h, at]), NEG_FILL)
+                s = jnp.where(permit, dot_nt(k_s[h, at], q_heads[h]), NEG_FILL)
                 old = m_s[h]
-                new = jnp.maximum(old, jnp.max(s, axis=-1, keepdims=True))
+                new = jnp.maximum(old, jnp.max(s, axis=0, keepdims=True))
                 p = jnp.exp(s - new)
                 fade = jnp.exp(old - new)
-                l_s[h] = l_s[h] * fade + jnp.sum(p, axis=-1, keepdims=True)
-                acc_s[h] = acc_s[h] * fade + dot_nn(p.astype(jnp.bfloat16), v_s[h, at])
+                l_s[h] = l_s[h] * fade + jnp.sum(p, axis=0, keepdims=True)
+                acc_s[h] = acc_s[h] * fade + dot_nn(vt_s[h, :, at], p.astype(jnp.bfloat16))
                 m_s[h] = new
 
         return carry
 
     lax.fori_loop(0, chunks, one_chunk, 0)
-    rows = q_ref.shape[0]
-    outs, logs = [], []
-    for h in range(GROUP):
-        outs.append(acc_s[h] / l_s[h])
-        lse = m_s[h] + jnp.log(l_s[h])
-        logs.append(jnp.transpose(jnp.broadcast_to(lse, (rows, rows)))[0:1])
-    out = jnp.concatenate(outs, axis=1)
+    out = jnp.concatenate([jnp.transpose(acc_s[h] / l_s[h]) for h in range(GROUP)], axis=1)
     o_ref[...] = out
     low_ref[...] = out.astype(jnp.bfloat16)
+    logs = [m_s[h] + jnp.log(l_s[h]) for h in range(GROUP)]
     lse_ref[...] = jnp.concatenate(logs + [logs[0]] * (8 - GROUP), axis=0)
 
 
-def attend(active, q, kv, q_seg, k_seg):
-    rows, keys = q.shape[0], kv.shape[0]
-    grid = rows // BLOCK
+def attend(active, may, place, q, mine, theirs, q_seg, k_seg):
+    rows, keys = q.shape[0], 2 * mine.shape[0]
+    tall = pl.BlockSpec((CHUNK, GW), lambda i, *_: (i, 0))
     return pl.pallas_call(
         attend_kernel,
         out_shape=(
@@ -543,67 +953,70 @@
             jax.ShapeDtypeStruct((8, rows), jnp.float32),
         ),
         grid_spec=pltpu.PrefetchScalarGridSpec(
-            num_scalar_prefetch=1,
-            grid=(grid,),
+            num_scalar_prefetch=3,
+            grid=(rows // CHUNK,),
             in_specs=[
-                pl.BlockSpec((BLOCK, GW), lambda i, t: (i, 0)),
-                pl.BlockSpec((keys, 2 * GW), lambda i, t: (0, 0)),
-                pl.BlockSpec((BLOCK, 1), lambda i, t: (i, 0)),
-                pl.BlockSpec((1, 1, keys), lambda i, t: (i, 0, 0)),
+                tall, whole_spec(mine.shape), whole_spec(theirs.shape), whole_spec(q_seg.shape),
+                whole_spec(k_seg.shape),
             ],
-            out_specs=[
-                pl.BlockSpec((BLOCK, GW), lambda i, t: (i, 0)),
-                pl.BlockSpec((BLOCK, GW), lambda i, t: (i, 0)),
-                pl.BlockSpec((8, BLOCK), lambda i, t: (0, i)),
-            ],
+            out_specs=[tall, tall, pl.BlockSpec((8, CHUNK), lambda i, *_: (0, i))],
             scratch_shapes=[
                 pltpu.VMEM((GROUP, keys, HEAD_DIM), jnp.bfloat16),
-                pltpu.VMEM((GROUP, keys, HEAD_DIM), jnp.bfloat16),
-                pltpu.VMEM((GROUP, BLOCK, 1), jnp.float32),
-                pltpu.VMEM((GROUP, BLOCK, 1), jnp.float32),
-                pltpu.VMEM((GROUP, BLOCK, HEAD_DIM), jnp.float32),
+                pltpu.VMEM((GROUP, HEAD_DIM, keys), jnp.bfloat16),
+                pltpu.VMEM((keys, 1), jnp.float32),
+                pltpu.VMEM((GROUP, 1, CHUNK), jnp.float32),
+                pltpu.VMEM((GROUP, 1, CHUNK), jnp.float32),
+                pltpu.VMEM((GROUP, HEAD_DIM, CHUNK), jnp.float32),
             ],
         ),
         compiler_params=pltpu.CompilerParams(vmem_limit_bytes=32 << 20),
         cost_estimate=pl.CostEstimate(
-            flops=2 * rows * keys * GW, bytes_accessed=4 * keys * GW, transcendentals=rows * keys
+            flops=48 * rows * keys * GW, bytes_accessed=16 * keys * GW, transcendentals=4 * rows * keys
         ),
         name="attend",
-    )(active, q, kv, q_seg, k_seg)
+    )(active, may, place, q, mine, theirs, q_seg, k_seg)
 
 
 def attend_back_kernel(
-    act_ref, q_ref, do_ref, o_ref, kv_ref, lse_ref, qseg_ref, kseg_ref, dq_ref, dkv_ref,
-    q_s, do_s, dq_s, delta_s, dk_s, dv_s,
+    act_ref, may_ref, place_ref, q_ref, d0_ref, d1_ref, d2_ref, d3_ref, o_ref, mine_ref, theirs_ref, lse_ref,
+    qseg_ref, kseg_ref, dq_ref, dmine_ref, dtheirs_ref, q_s, do_s, dqt_s, delta_s, dk_s, dv_s,
 ):
-    kb = pl.program_id(0)
+    step = pl.program_id(0)
     rows = q_ref.shape[0]
-
-    @pl.when(kb == 0)
+    lines = rows // CHUNK
+    z, c = place_ref[0], place_ref[1]
+    j = jnp.where(step < lines, 2 * step + 1 - c, 2 * (step - lines) + c)
+
+    @pl.when(step == 0)
     def _():
+        for r, ref in enumerate((d0_ref, d1_ref, d2_ref, d3_ref)):
+            at = pl.ds(pl.multiple_of(lax.rem(z - r + NZ, NZ) * CHUNK, CHUNK), CHUNK)
+            for h in range(GROUP):
+                do_s[h, at] = ref[:, HEAD_DIM * h : HEAD_DIM * (h + 1)]
         ones = jnp.ones((8, HEAD_DIM), jnp.float32)
         for h in range(GROUP):
             lanes = slice(HEAD_DIM * h, HEAD_DIM * (h + 1))
             q_s[h] = q_ref[:, lanes]
-            do_s[h] = do_ref[:, lanes]
-            both = do_ref[:, lanes].astype(jnp.float32) * o_ref[:, lanes]
+            both = do_s[h].astype(jnp.float32) * o_ref[:, lanes]
             delta_s[h] = lax.dot_general(
                 ones, both, (((1,), (1,)), ((), ())), precision=lax.Precision.HIGHEST,
                 preferred_element_type=jnp.float32,
             )[0:1]
-        dq_s[...] = jnp.zeros(dq_s.shape, jnp.float32)
+        dqt_s[...] = jnp.zeros(dqt_s.shape, jnp.float32)
 
     dk_s[...] = jnp.zeros(dk_s.shape, jnp.float32)
     dv_s[...] = jnp.zeros(dv_s.shape, jnp.float32)
-    k_heads = [kv_ref[:, HEAD_DIM * h : HEAD_DIM * (h + 1)] for h in range(GROUP)]
-    v_heads = [kv_ref[:, GW + HEAD_DIM * h : GW + HEAD_DIM * (h + 1)] for h in range(GROUP)]
-    k_seg = kseg_ref[...]
-
-    def one_chunk(j, carry):
-        @pl.when(act_ref[kb, j] != 0)
+    kv = jnp.where(step < lines, theirs_ref[...], mine_ref[...])
+    k_heads = [kv[:, HEAD_DIM * h : HEAD_DIM * (h + 1)] for h in range(GROUP)]
+    v_heads = [kv[:, GW + HEAD_DIM * h : GW + HEAD_DIM * (h + 1)] for h in range(GROUP)]
+    k_turned = [jnp.transpose(k) for k in k_heads]
+    k_column = column_of(kseg_ref[pl.ds(j, 1)])
+
+    def one_tile(i, carry):
+        @pl.when(act_ref[i, j] != 0)
         def _():
-            at = pl.ds(pl.multiple_of(j * CHUNK, CHUNK), CHUNK)
-            permit = k_seg == qseg_ref[0, :, at]
+            at = pl.ds(pl.multiple_of(i * CHUNK, CHUNK), CHUNK)
+            permit = permit_of(may_ref, i, j, qseg_ref[pl.ds(i, 1)], k_column)
             for h in range(GROUP):
                 q, do = q_s[h, at], do_s[h, at]
                 s = dot_nt(k_heads[h], q)
@@ -612,62 +1025,65 @@
                 ds = (p * (dp - delta_s[h, :, at])).astype(jnp.bfloat16)
                 dv_s[h] += dot_nn(p.astype(jnp.bfloat16), do)
                 dk_s[h] += dot_nn(ds, q)
-                dq_s[h, at] += dot_tn(ds, k_heads[h])
+                dqt_s[h, :, at] += dot_nn(k_turned[h], ds)
 
         return carry
 
-    lax.fori_loop(0, rows // CHUNK, one_chunk, 0)
-    dkv_ref[...] = jnp.concatenate(
+    lax.fori_loop(0, lines, one_tile, 0)
+    dkv = jnp.concatenate(
         [dk_s[h] for h in range(GROUP)] + [dv_s[h] for h in range(GROUP)], axis=1
     ).astype(jnp.bfloat16)
 
-    @pl.when(kb == pl.num_programs(0) - 1)
+    @pl.when(step < lines)
+    def _():
+        dtheirs_ref[...] = dkv
+
+    @pl.when(step >= lines)
+    def _():
+        dmine_ref[...] = dkv
+
+    @pl.when(step == pl.num_programs(0) - 1)
     def _():
         dq_ref[...] = jnp.concatenate(
-            [dq_s[h] * SCORE_SCALE for h in range(GROUP)], axis=1
+            [jnp.transpose(dqt_s[h] * SCORE_SCALE) for h in range(GROUP)], axis=1
         ).astype(jnp.bfloat16)
 
 
-def attend_back(active, q, dout, out, kv, lse, q_seg, k_seg):
-    rows, keys = q.shape[0], kv.shape[0]
-    whole = lambda shape: pl.BlockSpec(shape, lambda i, t: (0,) * len(shape))
+def attend_back(active, may, place, q, pieces, out, mine, theirs, lse, q_seg, k_seg):
+    rows, keys = q.shape[0], 2 * mine.shape[0]
+    lines = rows // CHUNK
+    late = pl.BlockSpec((CHUNK, 2 * GW), lambda s, *_: (jnp.maximum(s - lines, 0), 0))
+    early = pl.BlockSpec((CHUNK, 2 * GW), lambda s, *_: (jnp.minimum(s, lines - 1), 0))
     return pl.pallas_call(
         attend_back_kernel,
         out_shape=(
             jax.ShapeDtypeStruct((rows, GW), jnp.bfloat16),
-            jax.ShapeDtypeStruct((keys, 2 * GW), jnp.bfloat16),
+            jax.ShapeDtypeStruct((rows, 2 * GW), jnp.bfloat16),
+            jax.ShapeDtypeStruct((rows, 2 * GW), jnp.bfloat16),
         ),
         grid_spec=pltpu.PrefetchScalarGridSpec(
-            num_scalar_prefetch=1,
-            grid=(keys // BLOCK,),
+            num_scalar_prefetch=3,
+            grid=(keys // CHUNK,),
             in_specs=[
-                whole((rows, GW)),
-                whole((rows, GW)),
-                whole((rows, GW)),
-                pl.BlockSpec((BLOCK, 2 * GW), lambda i, t: (i, 0)),
-                whole((8, rows)),
-                pl.BlockSpec((1, 1, rows), lambda i, t: (i, 0, 0)),
-                pl.BlockSpec((BLOCK, 1), lambda i, t: (i, 0)),
+                whole_spec((rows, GW)), *[whole_spec(p.shape) for p in pieces], whole_spec((rows, GW)),
+                late, early, whole_spec((8, rows)), whole_spec(q_seg.shape), whole_spec(k_seg.shape),
             ],
-            out_specs=[
-                whole((rows, GW)),
-                pl.BlockSpec((BLOCK, 2 * GW), lambda i, t: (i, 0)),
-            ],
+            out_specs=[whole_spec((rows, GW)), late, early],
             scratch_shapes=[
                 pltpu.VMEM((GROUP, rows, HEAD_DIM), jnp.bfloat16),
                 pltpu.VMEM((GROUP, rows, HEAD_DIM), jnp.bfloat16),
-                pltpu.VMEM((GROUP, rows, HEAD_DIM), jnp.float32),
+                pltpu.VMEM((GROUP, HEAD_DIM, rows), jnp.float32),
                 pltpu.VMEM((GROUP, 1, rows), jnp.float32),
-                pltpu.VMEM((GROUP, BLOCK, HEAD_DIM), jnp.float32),
-                pltpu.VMEM((GROUP, BLOCK, HEAD_DIM), jnp.float32),
+                pltpu.VMEM((GROUP, CHUNK, HEAD_DIM), jnp.float32),
+                pltpu.VMEM((GROUP, CHUNK, HEAD_DIM), jnp.float32),
             ],
         ),
         compiler_params=pltpu.CompilerParams(vmem_limit_bytes=32 << 20),
         cost_estimate=pl.CostEstimate(
-            flops=5 * rows * keys * GW, bytes_accessed=8 * keys * GW, transcendentals=rows * keys
+            flops=56 * rows * keys * GW, bytes_accessed=32 * keys * GW, transcendentals=4 * rows * keys
         ),
         name="attend_back",
-    )(active, q, dout, out, kv, lse, q_seg, k_seg)
+    )(active, may, place, q, *pieces, out, mine, theirs, lse, q_seg, k_seg)
 
 
 def fast_local(
@@ -675,160 +1091,123 @@
     norm2_gain, norm2_bias, up_weight, up_bias, down_weight, down_bias, grad_out,
 ):
     y, x, z, c = (lax.axis_index(name) for name in ("y", "x", "z", "c"))
+    place = jnp.stack([z, c]).astype(jnp.int32)
     wide, low = jnp.float32, jnp.bfloat16
     _, rows, width = tokens.shape
     own_rows, units = qkv_weight.shape[0], down_weight.shape[0]
     ff = up_weight.shape[1]
-    half = ff // 2
+    half, pairs = ff // 2, ff // (2 * units)
     devices = width // own_rows
     seq_rows = rows * NZ
     keys = 2 * seq_rows
     blocks = keys // BLOCK
-
-    own_tokens = tokens[0]
-    line_tokens = z_spread(own_tokens, z).reshape(seq_rows, width)
-    own_seg = z_spread(segment_ids, z).reshape(NZ, rows)
-    seg = in_order(own_seg, swap(own_seg, "c"), c, 1).reshape(keys)
+    per = CHUNK // BLOCK
+
+    own = tokens[0]
+    line_pieces = z_pieces(own)
+
     vectors = (norm1_gain, norm1_bias, qv_bias, out_bias, norm2_gain, norm2_bias, up_bias, down_bias)
     sizes = [v.shape[0] for v in vectors]
-    packed = xy_gather(z_spread(jnp.concatenate(vectors)[None], z), y, x)
-    packed = in_order(packed, swap(packed, "c"), c, 3).reshape(devices, sum(sizes)).astype(wide)
     cuts = [sum(sizes[:i]) for i in range(len(sizes) + 1)]
-    gain1, shift1, bias_qv, bias_out, gain2, shift2, bias_up, bias_down = (
-        packed[:, cuts[i] : cuts[i + 1]].reshape(-1) for i in range(len(sizes))
-    )
+    extra = jnp.concatenate(vectors + (segment_ids[0].astype(low),))[None]
+    span = width + 3 * GW
+    tall = own_rows + 8
+    extra = jnp.pad(extra, ((0, 7), (0, span - extra.shape[1])))
     wz = qkv_weight.reshape(own_rows, 3, NZ, GW).transpose(2, 0, 1, 3).reshape(NZ, own_rows, 3 * GW)
-    wz = xy_gather(z_order(z_exchange(wz, z), z), y, x)
-    wz = in_order(wz, swap(wz, "c"), c, 3).reshape(width, 3 * GW)
-
-    up_sets = up_weight.reshape(own_rows, ff // (2 * units), 2, units).transpose(2, 0, 1, 3)
+    group1 = jnp.concatenate(
+        [jnp.broadcast_to(out_weight[None], (NZ, own_rows, width)), wz], axis=2
+    )
+    group1 = jnp.concatenate([group1, jnp.broadcast_to(extra[None], (NZ, 8, span))], axis=1)
+    group1 = group1
+    group1 = z_order(z_exchange(group1, z), z)
+    own_seg = group1[:, own_rows, cuts[-1] : cuts[-1] + rows].astype(wide)
+    seg = in_order(own_seg, swap(own_seg, "c"), c, 1).reshape(keys // CHUNK, CHUNK)
+    group1 = xy_gather(group1, y, x)
+    group1 = in_order(group1, swap(group1, "c"), c, 3)
+    wo = group1[..., :own_rows, :width].reshape(width, width)
+    wz = group1[..., :own_rows, width:].reshape(width, 3 * GW)
+    packed = group1[..., own_rows, : cuts[-1]].reshape(devices, cuts[-1])
+    vec = kernel_call(
+        unpack_kernel, place, (packed,), [whole_spec(packed.shape)], [((VEC_ROWS, width), wide)],
+        [whole_spec((VEC_ROWS, width))], (1,), [], 1 << 20, "unpack",
+    )[0]
+
+    up_sets = up_weight.reshape(own_rows, pairs, 2, units).transpose(2, 0, 1, 3)
     up_sets = up_sets.reshape(2, own_rows, half)
     up_chip = in_order(pick(up_sets, c), swap(pick(up_sets, 1 - c), "c"), c, 0)
-    up_half = xy_gather(z_spread(up_chip.reshape(2 * own_rows, half), z), y, x).reshape(width, half)
-    wo = xy_gather(z_spread(out_weight, z), y, x)
-    wo = in_order(wo, swap(wo, "c"), c, 3).reshape(NZ, GW, width)
-    down_half = xy_gather(z_spread(down_weight, z), y, x).reshape(half, width)
-    up_bias_half = pick(bias_up.reshape(ff // (2 * units), 2, units), c, 1).reshape(half)
-
+    up_chip = up_chip.reshape(2 * own_rows, half)
+    up_pieces = z_pieces(up_chip)
+    down_chip = after(down_weight, line_pieces[2])
+    up_line = z_select(up_chip, up_pieces, z)
+    down_line = z_select(down_chip, z_pieces(down_chip), z)
     own_blocks = seq_rows // BLOCK
-    per = rows // BLOCK
     ids = jnp.arange(blocks, dtype=jnp.int32)
-    own_ids = pick(ids.reshape(NZ, 2, per), c, 1).reshape(own_blocks)
-    own_live = pick(live_blocks[0].reshape(NZ, 2, per, blocks), c, 1).reshape(own_blocks, blocks)
+    own_ids = pick(ids.reshape(NZ, 2, rows // BLOCK), c, 1).reshape(own_blocks)
+    own_live = pick(live_blocks[0].reshape(NZ, 2, rows // BLOCK, blocks), c, 1)
+    own_live = own_live.reshape(own_blocks, blocks)
     seg_blocks = seg.reshape(blocks, BLOCK)
-    first, last = seg_blocks[:, 0], seg_blocks[:, -1]
     own_seg_blocks = own_seg.reshape(own_blocks, BLOCK)
-    own_first, own_last = own_seg_blocks[:, 0], own_seg_blocks[:, -1]
     may = (own_live > 0) | (own_ids[:, None] == ids[None, :])
-    meet = may & (own_first[:, None] <= last[None, :]) & (first[None, :] <= own_last[:, None])
-    per_chunk = CHUNK // BLOCK
-    active = jnp.any(meet.reshape(own_blocks, blocks // per_chunk, per_chunk), axis=2).astype(jnp.int32)
-    active_back = jnp.any(
-        meet.reshape(own_blocks // per_chunk, per_chunk, blocks), axis=1
-    ).T.astype(jnp.int32)
-    key_seg = jnp.where(may[:, :, None], seg_blocks[None], -1).reshape(own_blocks, 1, keys)
-    query_seg = jnp.where(may.T[:, :, None], own_seg_blocks[None], -1).reshape(blocks, 1, seq_rows)
-
-    tokens_wide = line_tokens.astype(wide)
-    unit1, scale1 = norm_stats(tokens_wide)
-    n1 = (unit1 * gain1 + shift1).astype(low)
-    projected = matmul_low(n1, wz)
-    q_bias = pick(bias_qv[:width].reshape(NZ, GW), z)
-    v_bias = pick(bias_qv[width:].reshape(NZ, GW), z)
-    q = (projected[:, :GW] + q_bias).astype(low) * jnp.asarray(SCORE_SCALE, low)
-    kv = jnp.concatenate(
-        [projected[:, GW : 2 * GW].astype(low), (projected[:, 2 * GW :] + v_bias).astype(low)], axis=1
-    )
-    kv_line = kv.reshape(NZ, rows, 2 * GW)
-    kv_all = in_order(kv_line, swap(kv_line, "c"), c, 1).reshape(keys, 2 * GW)
-    att_wide, att_low, lse = attend(active, q, kv_all, own_seg.reshape(seq_rows, 1), key_seg)
-    att = z_order(z_exchange(att_low.reshape(NZ, rows, GW), z), z)
-
-    own_wide = own_tokens.astype(wide)
-    branch = sum(matmul_low(att[g], wo[g]) for g in range(NZ))
-    hidden = own_wide + branch + bias_out
-    unit2, scale2 = norm_stats(hidden)
-    n2 = (unit2 * gain2 + shift2).astype(low)
-
+    meet = (
+        may
+        & (own_seg_blocks[:, :1] <= seg_blocks[:, -1][None])
+        & (seg_blocks[:, 0][None] <= own_seg_blocks[:, -1:])
+    )
+    active = jnp.any(meet.reshape(own_blocks // per, per, blocks // per, per), axis=(1, 3))
+    active, may = active.astype(jnp.int32), may.astype(jnp.int32)
+
+    line, n1, q, kv = project(place, own, *line_pieces, vec, wz)
+    kv_theirs = swap(kv, "c")
+    up_half = xy_gather(up_line, y, x, q).reshape(width, half)
+    att_wide, att_low, lse = attend(active, may, place, q, kv, kv_theirs, own_seg, seg)
+    att = z_exchange(att_low.reshape(NZ, rows, GW), z)
+    down_half = xy_gather(after(down_line, q), y, x, att_low).reshape(half, width)
+
+    hidden, n2 = branch_call(place, att, wo, own, vec)
     go = grad_out[0]
-    n2_both = jnp.concatenate([n2, swap(n2, "c")], axis=0)
-    go_both = jnp.concatenate([go, swap(go, "c")], axis=0)
-    before = matmul_low(n2_both, up_half) + up_bias_half
-    cdf = 0.5 * (1.0 + lax.erf(before * 0.7071067811865476))
-    slope = cdf + before * (0.3989422804014327 * jnp.exp(-0.5 * before * before))
-    activated = (before * cdf).astype(low)
-    out_part = matmul_low(activated, down_half)
-    out_sum = out_part[:rows] + swap(out_part[rows:].astype(low), "c").astype(wide)
-    output = (hidden + out_sum + bias_down).astype(low)
-    grad_before = (dot_nt(go_both, down_half) * slope).astype(low)
-    m_part = dot_nt(grad_before, up_half)
-    m = m_part[:rows] + swap(m_part[rows:].astype(low), "c").astype(wide)
+    n2_theirs, go_theirs = swap(n2, "c"), swap(go, "c")
+    up_bias_half = vec[8:10].reshape(1, half)
+    activated, grad_before, out_part, m_part, sums, up_bias_part = feed(
+        place, n2, n2_theirs, go, go_theirs, up_half, down_half, up_bias_half
+    )
+    sums = swap(sums, "c")
+    output, grad_hidden, grad_branch, *grad_att, mid = middle(
+        place, m_part, out_part, sums, hidden, go, vec, wo
+    )
+    dout = [grad_att[0]] + [shift(grad_att[j], "z", NZ, j) for j in range(1, NZ)]
+    n2_both = jnp.concatenate([n2, n2_theirs], axis=0)
+    go_both = jnp.concatenate([go, go_theirs], axis=0)
+    grad_down = dot_tn(activated, go_both).astype(low)
     grad_up = dot_tn(n2_both, grad_before).astype(low)
-    grad_down = dot_tn(activated, go_both).astype(low)
-    up_bias_part = jnp.sum(grad_before.astype(wide), axis=0)
-
-    go_wide = go.astype(wide)
-    grad_hidden = go_wide + norm_back(m, gain2, unit2, scale2)
-    grad_branch = grad_hidden.astype(low)
-    grad_att = jnp.stack([dot_nt(grad_branch, wo[g]).astype(low) for g in range(NZ)])
-    dout = z_order(z_exchange(grad_att, z), z).reshape(seq_rows, GW)
-    grad_wo = jnp.stack([dot_tn(att[g], grad_branch) for g in range(NZ)]).astype(low)
-
-    dq, dkv = attend_back(
-        active_back, q, dout, att_wide, kv_all, lse, query_seg, seg.reshape(keys, 1)
-    )
-    dkv = dkv.reshape(NZ, 2, rows, 2 * GW)
-    dkv_sum = pick(dkv, c, 1).astype(wide) + swap(pick(dkv, 1 - c, 1), "c").astype(wide)
-    dkv_low = dkv_sum.reshape(seq_rows, 2 * GW).astype(low)
-    dqkv = jnp.concatenate([dq, dkv_low], axis=1)
-    m1 = dot_nt(dqkv, wz)
-    m1_line = m1.reshape(NZ, rows, width)
-    m1_own = z_collect(m1_line, z, low)
-    grad_wz = dot_tn(n1, dqkv).astype(low)
-    own_unit1, own_scale1 = norm_stats(own_wide)
-    grad_tokens = grad_hidden + norm_back(m1_own, gain1, own_unit1, own_scale1)
-
-    grad_down = z_collect(xy_scatter(grad_down.reshape(2, 2, NZ, units, width), y, x, low), z, low)
-    grad_up = z_collect(xy_scatter(grad_up.reshape(2, 2, NZ, 2 * own_rows, half), y, x, low), z, low)
-    grad_up = grad_up.reshape(2, own_rows, half)
+    down_line = xy_scatter(grad_down.reshape(2, 2, NZ, units, width), y, x, low, grad_branch)
+    up_line = xy_scatter(grad_up.reshape(2, 2, NZ, 2 * own_rows, half), y, x, low, dout[3])
+
+    dq, dkv_mine, dkv_theirs = attend_back(
+        active, may, place, q, dout, att_wide, kv, kv_theirs, lse, own_seg, seg
+    )
+    dqkv, m1_own, m1_sent, cols, dqkv_sum = inward(place, dq, dkv_mine, swap(dkv_theirs, "c"), line, wz)
+    m1_pieces = [shift(m1_sent[j - 1], "z", NZ, j) for j in range(1, NZ)]
+
+    grad_down = z_collect(down_line, z, low)
+    grad_up = z_collect(up_line, z, low).reshape(2, own_rows, half)
     up_other = swap(pick(grad_up, 1 - c).astype(low), "c").astype(wide)
-    up_shape = (own_rows, ff // (2 * units), units)
+    up_shape = (own_rows, pairs, units)
     grad_up = in_order(pick(grad_up, c).reshape(up_shape), up_other.reshape(up_shape), c, 2)
     grad_up = grad_up.reshape(own_rows, ff)
 
-    def over_cores(array, wire):
-        return pick(array, c, 3).astype(wide) + swap(pick(array, 1 - c, 3).astype(wire), "c").astype(wide)
-
-    grad_wo = over_cores(grad_wo.reshape(2, 2, NZ, 2, own_rows, width), low)
-    grad_wo = z_collect(xy_scatter(grad_wo, y, x, low), z, low)
-    grad_wz = over_cores(grad_wz.reshape(2, 2, NZ, 2, own_rows, 3 * GW), low)
-    grad_wz = z_order(z_exchange(xy_scatter(grad_wz, y, x, low).astype(low), z), z)
+    mine, theirs = owners(
+        place, att, grad_branch, n1, dqkv, cols, mid, dqkv_sum, up_bias_part, devices, tall
+    )
+    group1 = mine.astype(wide) + swap(theirs, "c").astype(wide)
+    group1 = group1.reshape(2, 2, NZ, tall, span)
+    group1 = xy_scatter(group1, y, x, low)
+    pieces = z_exchange(group1.astype(low), z)
+    grad_wz = z_order([p[:own_rows, width:] for p in pieces], z)
     grad_qkv = grad_wz.reshape(NZ, own_rows, 3, GW).transpose(1, 2, 0, 3).reshape(own_rows, 3 * width)
-
-    dqkv_sum = jnp.sum(dqkv.astype(wide), axis=0)
-    at_group = (jnp.arange(NZ) == z)[:, None]
-    qv_part = jnp.concatenate(
-        [
-            jnp.where(at_group, dqkv_sum[None, :GW], 0.0).reshape(width),
-            jnp.where(at_group, dqkv_sum[None, 2 * GW :], 0.0).reshape(width),
-        ]
-    )
-    at_core = (jnp.arange(2) == c)[None, :, None]
-    up_bias_part = jnp.where(at_core, up_bias_part.reshape(ff // (2 * units), 1, units), 0.0)
-    parts = (
-        jnp.sum(m1 * unit1, axis=0),
-        jnp.sum(m1, axis=0),
-        qv_part,
-        jnp.sum(grad_branch.astype(wide), axis=0),
-        jnp.sum(m * unit2, axis=0),
-        jnp.sum(m, axis=0),
-        up_bias_part,
-        jnp.sum(go_wide, axis=0),
-    )
-    vec = jnp.concatenate([p.reshape(devices, s) for p, s in zip(parts, sizes)], axis=1)
-    vec = over_cores(vec.reshape(2, 2, NZ, 2, 1, sum(sizes)), wide)
-    vec = z_collect(xy_scatter(vec, y, x, wide), z, wide)[0]
-    v = [vec[cuts[i] : cuts[i + 1]] for i in range(len(sizes))]
+    total = sum([p.astype(wide) for p in pieces[1:]], pick(group1, z))
+    grad_wo = total[:own_rows, :width]
+    v = [total[own_rows, cuts[i] : cuts[i + 1]] for i in range(len(sizes))]
+    grad_tokens = finish(place, m1_own, m1_pieces, own, grad_hidden, vec)
     return (
         output[None], grad_tokens[None], v[0], v[1], grad_qkv.astype(wide), v[2], grad_wo, v[3],
         v[4], v[5], grad_up, v[6], grad_down, v[7],

time: 489 us -> 327 us (0.67); the launches traced: 479 us -> 326 us
  starting transfers between devices: 166 us -> 88.9 us
  matrix products: 29.4 us -> 2.85 us
  other arithmetic: 46.6 us -> 20.8 us
  local copies, waits for them, and re-layouts: 56.1 us -> 32.4 us
  waiting for transfers between devices: 121 us -> 106 us
  Pallas kernels: 56.7 us -> 65.8 us
  between operations: 3.84 us -> 9.39 us
    ppermute x88 -> x58, starting transfers between devices: 131 us -> 71.9 us  [shift(): lax.ppermute(array, axis, [(i, (i + hop) % size) for i in range(size)])]
    pallas_call x0 -> x8, Pallas kernels: none -> 26 us  [kernel_call(): pl.pallas_call(body, out_shape=tuple((jax.ShapeDtypeStruct(shape, dtype)...]
    dot_general x14 -> x0, matrix products: 17.7 us -> none  [the longest x7 10.3 us: dot_nt(): lax.dot_general(a, b, (((1,), (1,)), ((), ())), preferred_element_type=jn...]
    ppermute x18 -> x9, starting transfers between devices: 34.3 us -> 17 us  [the longest x3 9.15 us: z_pieces(): up = lax.ppermute(block, 'z', [(0, 1), (1, 2), (2, 3)])]
    ppermute x88 -> x58, waiting for transfers between devices: 106 us -> 93.1 us  [shift(): lax.ppermute(array, axis, [(i, (i + hop) % size) for i in range(size)])]
    unnamed x219 -> x63, local copies, waits for them, and re-layouts: 12.3 us -> 3.35 us
    dot_general x7 -> x2, matrix products: 11.7 us -> 2.85 us  [dot_tn(): lax.dot_general(a, b, (((0,), (0,)), ((), ())), preferred_element_type=jn...]
    pallas_call x1, Pallas kernels: 27.9 us -> 19.3 us  [attend(): pl.pallas_call(attend_kernel, out_shape=(jax.ShapeDtypeStruct((rows, GW),...]
  transfers between devices with their start and end apart: 106 -> 67, of which waited for: 45 -> 28; matrix products, arithmetic and copies ran while one was open for 22% -> 13% of each run, Pallas kernels for 12% -> 11%
where the time goes in v3:
time: 327 us; the launch traced here: 326 us
  waiting for transfers between devices  106 us (32%)
  starting transfers between devices  88.9 us (27%)
  Pallas kernels  65.8 us (20%)
  local copies, waits for them, and re-layouts  32.4 us (10%)
  other arithmetic  20.8 us (6%)
  between operations  9.39 us (3%)
    ppermute x58, waiting for transfers between devices, shift(): lax.ppermute(array, axis, [(i, (i + hop) % size) for i in range(size)])  93.1 us
    ppermute x58, starting transfers between devices, shift(): lax.ppermute(array, axis, [(i, (i + hop) % size) for i in range(size)])  71.9 us
    pallas_call x8, Pallas kernels, kernel_call(): pl.pallas_call(body, out_shape=tuple((jax.ShapeDtypeStruct(shape, dtype)...  26 us
    pallas_call x1, Pallas kernels, attend_back(): pl.pallas_call(attend_back_kernel, out_shape=(jax.ShapeDtypeStruct((rows,...  20.5 us
    pallas_call x1, Pallas kernels, attend(): pl.pallas_call(attend_kernel, out_shape=(jax.ShapeDtypeStruct((rows, GW),...  19.3 us
    ppermute x3, waiting for transfers between devices, z_pieces(): last = lax.ppermute(after(far, up, down), 'z', [(2, 3), (1, 0)])  12 us
    ppermute x3, starting transfers between devices, z_pieces(): up = lax.ppermute(block, 'z', [(0, 1), (1, 2), (2, 3)])  9.15 us
  transfers between devices with their start and end apart: 67, of which 28 were waited for; matrix products, arithmetic and copies ran while one was open for 13% of the time, Pallas kernels for 11%

profile of v3, /device:TPU:0, one launch (start us, length us, event | category | flops | bytes accessed | tf_op | source)
XLA Modules:
  0.0 326.5 jit_solution(7505169616003197813)
XLA Ops:
  0.7 5.1 %collective-permute-start.4 = (bf16[256,768]{1,0:T(8,128)(2,1)}, bf16[256,768]{1,0:T(8,128)(2,1)S(1)}, u32[]{:S(2)}, u32[]{:S(2)}) collective-permute-start(bf16[256,768]{1,0:T(8,128)(2,1)} %bitcast.336), channel_id=1, source_target_pairs={{0,2},{2,4},{4,6},{1,3},{3,5},{5,7},{8,10},{10,12},{12,14},{9,11},... | collective-permute-start | bytes 1179656 | tf_op jit(solution)/shard_map/ppermute | solution.py:404
  9.1 5.4 %concatenate.39 = bf16[544]{0:T(1024)(128)(2,1)S(1)} concatenate(bf16[24]{0:T(256)(128)(2,1)} %param.19, bf16[24]{0:T(256)(128)(2,1)} %param.20, bf16[48]{0:T(256)(128)(2,1)} %param.22, bf16[24]{0:T(256)(128)(2,1)} %param.24, bf16[24]{0:T(256)(128)(2,1)} %param.25, bf16[24]{0:T(256)(128)(2,1)} %param.26, bf16[96]{0:T(256)(128)(2,1)} %param.28, bf16[24]{0:T(256)(128)(2,1)} %param.30, ...), dimensions={0} | concatenate | bytes 2176 | tf_op jit(solution)/shard_map/concatenate | solution.py:1112
  15.4 2.7 collective-permute-start
  18.1 2.6 collective-permute-start.1
  23.9 2.6 collective-permute-start.20
  30.2 2.7 collective-permute-start.21
  37.8 11.6 %collective-permute-done.21 = bf16[48,1536]{1,0:T(8,128)(2,1)S(1)} collective-permute-done((bf16[48,1536]{1,0:T(8,128)(2,1)S(1)}, bf16[48,1536]{1,0:T(8,128)(2,1)S(1)}, u32[]{:S(2)}, u32[]{:S(2)}) %collective-permute-start.21) | collective-permute-done | bytes 147488 | tf_op jit(solution)/shard_map/ppermute | solution.py:390
  52.4 2.5 collective-permute-done.8
  56.7 3.6 %collective-permute-done.23 = bf16[48,1536]{1,0:T(8,128)(2,1)S(1)} collective-permute-done((bf16[48,1536]{1,0:T(8,128)(2,1)S(1)}, bf16[48,1536]{1,0:T(8,128)(2,1)S(1)}, u32[]{:S(2)}, u32[]{:S(2)}) %collective-permute-start.23) | collective-permute-done | bytes 147488 | tf_op jit(solution)/shard_map/ppermute | solution.py:407
  73.7 3.7 %collective-permute-start.29 = (bf16[96,768]{1,0:T(8,128)(2,1)S(1)}, bf16[96,768]{1,0:T(8,128)(2,1)S(1)}, u32[]{:S(2)}, u32[]{:S(2)}) collective-permute-start(bf16[96,768]{1,0:T(8,128)(2,1)S(1)} %broadcast_select_fusion.4), channel_id=1, source_target_pairs={{0,4},{2,6},{4,0},{6,2},{1,5},{3,7},{5,1},{7,3},{8,12},{10,14},{12... | collective-permute-start | bytes 442376 | tf_op jit(solution)/shard_map/ppermute | solution.py:390
  81.0 2.1 collective-permute-done.29
  86.2 8.4 %collective-permute-done.31 = bf16[96,768]{1,0:T(8,128)(2,1)S(1)} collective-permute-done((bf16[96,768]{1,0:T(8,128)(2,1)S(1)}, bf16[96,768]{1,0:T(8,128)(2,1)S(1)}, u32[]{:S(2)}, u32[]{:S(2)}) %collective-permute-start.31) | collective-permute-done | bytes 147488 | tf_op jit(solution)/shard_map/ppermute | solution.py:407
  101.5 4.3 %project.1 = (bf16[1024,768]{1,0:T(8,128)(2,1)S(1)}, bf16[1024,768]{1,0:T(8,128)(2,1)S(1)}, bf16[1024,192]{1,0:T(8,128)(2,1)S(1)}, bf16[1024,384]{1,0:T(8,128)(2,1)S(1)}) custom-call(s32[2]{0:T(128)S(1)} %pad_add_fusion.place_ref, bf16[256,768]{1,0:T(8,128)(2,1)S(1)} %bitcast.339, bf16[256,768]{1,0:T(8,128)(2,1)S(1)} %collective-permute-done.4.up_ref, ...), custom_call_target="tpu_custom_call" | custom-call | flops 3623878656 | bytes 2899968 | tf_op jit(solution)/shard_map/project/pallas_call | solution.py:527
  111.7 3.0 collective-permute-done.32
  114.7 2.9 collective-permute-done.34
  117.7 10.5 %collective-permute-done.25 = bf16[2,2,48,1536]{3,2,1,0:T(8,128)(2,1)S(1)} collective-permute-done((bf16[2,2,48,1536]{3,2,1,0:T(8,128)(2,1)S(1)}, bf16[2,2,48,1536]{3,2,1,0:T(8,128)(2,1)S(1)}, u32[]{:S(2)}, u32[]{:S(2)}) %collective-permute-start.25) | collective-permute-done | bytes 589856 | tf_op jit(solution)/shard_map/ppermute | solution.py:390
  128.4 19.3 %attend.1 = (f32[1024,192]{1,0:T(8,128)S(1)}, bf16[1024,192]{1,0:T(8,128)(2,1)S(1)}, f32[8,1024]{1,0:T(8,128)S(1)}) custom-call(s32[4,8]{1,0:T(4,128)S(1)} %convert_element_type.280.act_ref, s32[8,16]{1,0:T(8,128)S(1)} %fusion.66.may_ref, s32[2]{0:T(128)S(1)} %pad_add_fusion.place_ref, bf16[1024,192]{1,0:T(8,128)(2,1)S(1)} %get-tuple-element.47.q_ref, ...), custom_call_target="tpu_custom_call" | custom-call | flops 19327352832 | bytes 6291456 | tf_op jit(solution)/shard_map/attend/pallas_call | solution.py:948
  149.0 4.2 %collective-permute-start.33 = (bf16[2,2,96,768]{3,2,1,0:T(8,128)(2,1)S(1)}, bf16[2,2,96,768]{3,2,1,0:T(8,128)(2,1)S(1)}, u32[]{:S(2)}, u32[]{:S(2)}) collective-permute-start(bf16[2,2,96,768]{3,2,1,0:T(8,128)(2,1)S(1)} %maximum_select_fusion.3), channel_id=1, source_target_pairs={{0,16},{16,0},{1,17},{17,1},{2,18},{18,2},{3,19},{19,3},{4,20},{20... | collective-permute-start | bytes 1769480 | tf_op jit(solution)/shard_map/ppermute | solution.py:390
  154.5 4.0 %collective-permute-start.15 = (bf16[256,192]{1,0:T(8,128)(2,1)S(1)}, bf16[256,192]{1,0:T(8,128)(2,1)S(1)}, u32[]{:S(2)}, u32[]{:S(2)}) collective-permute-start(bf16[256,192]{1,0:T(8,128)(2,1)S(1)} %get-tuple-element.136), channel_id=1, source_target_pairs={{0,4},{2,6},{4,0},{6,2},{1,5},{3,7},{5,1},{7,3},{8,12},{10,14},{12... | collective-permute-start | bytes 294920 | tf_op jit(solution)/shard_map/ppermute | solution.py:390
  161.4 2.8 collective-permute-done.15.a2_ref
  168.0 7.2 %feed.1 = (bf16[512,1536]{1,0:T(8,128)(2,1)S(1)}, bf16[512,1536]{1,0:T(8,128)(2,1)S(1)}, f32[256,768]{1,0:T(8,128)S(1)}, f32[256,768]{1,0:T(8,128)S(1)}, bf16[2,...) custom-call(s32[2]{0:T(128)S(1)} %pad_add_fusion.place_ref, bf16[256,768]{1,0:T(8,128)(2,1)S(1)} %get-tuple-element.50.na_ref, ...), custom_call_target="tpu_custom_call" | custom-call | flops 9663676416 | bytes 6297600 | tf_op jit(solution)/shard_map/feed/pallas_call | solution.py:527
  177.2 2.1 collective-permute-start.60
  183.0 2.4 middle.1
  186.5 6.7 %collective-permute-done.62 = bf16[2,2,96,768]{3,2,1,0:T(8,128)(2,1)} collective-permute-done((bf16[2,2,96,768]{3,2,1,0:T(8,128)(2,1)S(1)}, bf16[2,2,96,768]{3,2,1,0:T(8,128)(2,1)}, u32[]{:S(2)}, u32[]{:S(2)}) %collective-permute-start.62) | collective-permute-done | bytes 589856 | tf_op jit(solution)/shard_map/ppermute | solution.py:390
  194.5 2.1 collective-permute-start.63
  196.6 2.2 collective-permute-start.39
  200.2 2.2 collective-permute-done.39.d3_ref
  205.8 2.7 collective-permute-start.38
  210.8 4.0 %collective-permute-done.38.d2_ref = bf16[256,192]{1,0:T(8,128)(2,1)S(1)} collective-permute-done((bf16[256,192]{1,0:T(8,128)(2,1)S(1)}, bf16[256,192]{1,0:T(8,128)(2,1)S(1)}, u32[]{:S(2)}, u32[]{:S(2)}) %collective-permute-start.38) | collective-permute-done | bytes 98336 | tf_op jit(solution)/shard_map/ppermute | solution.py:390
  214.8 20.5 %attend_back.1 = (bf16[1024,192]{1,0:T(8,128)(2,1)S(1)}, bf16[1024,384]{1,0:T(8,128)(2,1)S(1)}, bf16[1024,384]{1,0:T(8,128)(2,1)S(1)}) custom-call(s32[4,8]{1,0:T(4,128)S(1)} %convert_element_type.280.act_ref, s32[8,16]{1,0:T(8,128)S(1)} %fusion.66.may_ref, s32[2]{0:T(128)S(1)} %pad_add_fusion.place_ref, bf16[1024,192]{1,0:T(8,128)(2,1)S(1)} %get-tuple-element.47.q_ref, ...), custom_call_target="tpu_custom_call" | custom-call | flops 22548578304 | bytes 12582912 | tf_op jit(solution)/shard_map/attend_back/pallas_call | solution.py:1057
  235.9 3.7 %collective-permute-start.66 = (bf16[96,768]{1,0:T(8,128)(2,1)S(1)}, bf16[96,768]{1,0:T(8,128)(2,1)S(1)}, u32[]{:S(2)}, u32[]{:S(2)}) collective-permute-start(bf16[96,768]{1,0:T(8,128)(2,1)S(1)} %get-tuple-element.99), channel_id=1, source_target_pairs={{0,6},{2,0},{4,2},{6,4},{1,7},{3,1},{5,3},{7,5},{8,14},{10,8},{12,... | collective-permute-start | bytes 442376 | tf_op jit(solution)/shard_map/ppermute | solution.py:390
  242.1 3.8 %inward.1 = (bf16[1024,576]{1,0:T(8,128)(2,1)S(1)}, f32[256,768]{1,0:T(8,128)S(1)}, bf16[4,256,768]{2,1,0:T(8,128)(2,1)S(1)}, f32[8,768]{1,0:T(8,128)S(1)}, f32[8,576]{1,0:T(8,128)S(1)}) custom-call(s32[2]{0:T(128)S(1)} %pad_add_fusion.place_ref, bf16[1024,192]{1,0:T(8,128)(2,1)S(1)} %get-tuple-element.62.dq_ref, ...), custom_call_target="tpu_custom_call" | custom-call | flops 3623878656 | bytes 4423680 | tf_op jit(solution)/shard_map/inward/pallas_call | solution.py:527
  245.9 4.1 %owners.1 = (bf16[16,32,1344]{2,1,0:T(8,128)(2,1)S(1)}, bf16[16,32,1344]{2,1,0:T(8,128)(2,1)}) custom-call(s32[2]{0:T(128)S(1)} %pad_add_fusion.place_ref, bf16[256,192]{1,0:T(8,128)(2,1)S(1)} %get-tuple-element.138.a0_ref, bf16[256,192]{1,0:T(8,128)(2,1)S(1)} %collective-permute-done.14.a1_ref, bf16[256,192]{1,0:T(8,128)(2,1)S(1)} %collective-permute-done.15.a2_ref, ...), custom_call_target="tpu_custom_call" | custom-call | flops 1048576 | bytes 3612672 | tf_op jit(solution)/shard_map/owners/pallas_call | solution.py:527
  249.9 2.8 collective-permute-start.58
  253.9 8.5 %collective-permute-done.57 = bf16[48,1536]{1,0:T(8,128)(2,1)S(1)} collective-permute-done((bf16[48,1536]{1,0:T(8,128)(2,1)S(1)}, bf16[48,1536]{1,0:T(8,128)(2,1)S(1)}, u32[]{:S(2)}, u32[]{:S(2)}) %collective-permute-start.57) | collective-permute-done | bytes 147488 | tf_op jit(solution)/shard_map/ppermute | solution.py:390
  263.3 2.0 reshape.341
  265.3 2.0 reshape.352
  270.4 4.3 %collective-permute-start.47 = (bf16[2,2,32,1344]{3,2,1,0:T(8,128)(2,1)S(1)}, bf16[2,2,32,1344]{3,2,1,0:T(8,128)(2,1)S(1)}, u32[]{:S(2)}, u32[]{:S(2)}) collective-permute-start(bf16[2,2,32,1344]{3,2,1,0:T(8,128)(2,1)S(1)} %fusion.12), channel_id=1, source_target_pairs={{0,8},{8,0},{1,9},{9,1},{2,10},{10,2},{3,11},{11,3},{4,12},{12,4},... | collective-permute-start | bytes 1032200 | tf_op jit(solution)/shard_map/ppermute | solution.py:390
  275.6 3.3 %collective-permute-start.41 = (bf16[256,768]{1,0:T(8,128)(2,1)S(1)}, bf16[256,768]{1,0:T(8,128)(2,1)S(1)}, u32[]{:S(2)}, u32[]{:S(2)}) collective-permute-start(bf16[256,768]{1,0:T(8,128)(2,1)S(1)} %get-tuple-element.96), channel_id=1, source_target_pairs={{0,2},{2,4},{4,6},{6,0},{1,3},{3,5},{5,7},{7,1},{8,10},{10,12},{12... | collective-permute-start | bytes 1179656 | tf_op jit(solution)/shard_map/ppermute | solution.py:390
  279.3 2.1 collective-permute-start.43
  281.4 2.3 collective-permute-done.47
  284.7 8.0 %collective-permute-done.45 = bf16[2,2,32,1344]{3,2,1,0:T(8,128)(2,1)S(1)} collective-permute-done((bf16[2,2,32,1344]{3,2,1,0:T(8,128)(2,1)S(1)}, bf16[2,2,32,1344]{3,2,1,0:T(8,128)(2,1)S(1)}, u32[]{:S(2)}, u32[]{:S(2)}) %collective-permute-start.45) | collective-permute-done | bytes 344096 | tf_op jit(solution)/shard_map/ppermute | solution.py:390
  292.9 2.3 collective-permute-done.48
  295.3 3.1 collective-permute-done.46
  299.3 2.6 collective-permute-start.50
  304.6 2.2 reshape.344
  306.9 2.1 finish.1
  309.0 10.9 %collective-permute-done.50 = bf16[32,1344]{1,0:T(8,128)(2,1)S(1)} collective-permute-done((bf16[32,1344]{1,0:T(8,128)(2,1)}, bf16[32,1344]{1,0:T(8,128)(2,1)S(1)}, u32[]{:S(2)}, u32[]{:S(2)}) %collective-permute-start.50) | collective-permute-done | bytes 86048 | tf_op jit(solution)/shard_map/ppermute | solution.py:390
  (314 shorter events, 90.7 us)
Async XLA Ops:
  0.7 64.0 %collective-permute-start.4 = (bf16[256,768]{1,0:T(8,128)(2,1)}, bf16[256,768]{1,0:T(8,128)(2,1)S(1)}, u32[]{:S(2)}, u32[]{:S(2)}) collective-permute-start(bf16[256,768]{1,0:T(8,128)(2,1)} %bitcast.336), channel_id=1, source_target_pairs={{0,2},{2,4},{4,6},{1,3},{3,5},{5,7},{8,10},{10,12},{12,14},{9,11},... | collective-permute-start | bytes 1179656 | tf_op jit(solution)/shard_map/ppermute | solution.py:404
  5.7 60.9 %collective-permute-start.5 = (bf16[256,768]{1,0:T(8,128)(2,1)}, bf16[256,768]{1,0:T(8,128)(2,1)S(1)}, u32[]{:S(2)}, u32[]{:S(2)}) collective-permute-start(bf16[256,768]{1,0:T(8,128)(2,1)} %bitcast.337), channel_id=1, source_target_pairs={{2,0},{4,2},{6,4},{3,1},{5,3},{7,5},{10,8},{12,10},{14,12},{11,9},... | collective-permute-start | bytes 1179656 | tf_op jit(solution)/shard_map/ppermute | solution.py:405
  15.4 8.5 %collective-permute-start = (bf16[32,1344]{1,0:T(8,128)(2,1)S(1)}, bf16[32,1344]{1,0:T(8,128)(2,1)S(1)}, u32[]{:S(2)}, u32[]{:S(2)}) collective-permute-start(bf16[32,1344]{1,0:T(8,128)(2,1)S(1)} %get-tuple-element.163), channel_id=1, source_target_pairs={{0,2},{2,4},{4,6},{6,0},{1,3},{3,5},{5,7},{7,1},{8,10},{10,12},{12... | collective-permute-start | bytes 258056 | tf_op jit(solution)/shard_map/ppermute | solution.py:390
  23.9 9.7 %collective-permute-start.20 = (bf16[48,1536]{1,0:T(8,128)(2,1)S(1)}, bf16[48,1536]{1,0:T(8,128)(2,1)S(1)}, u32[]{:S(2)}, u32[]{:S(2)}) collective-permute-start(bf16[48,1536]{1,0:T(8,128)(2,1)S(1)} %bitcast.358), channel_id=1, source_target_pairs={{0,2},{2,4},{4,6},{1,3},{3,5},{5,7},{8,10},{10,12},{12,14},{9,11},... | collective-permute-start | bytes 442376 | tf_op jit(solution)/shard_map/ppermute | solution.py:404
  30.2 19.2 %collective-permute-start.21 = (bf16[48,1536]{1,0:T(8,128)(2,1)S(1)}, bf16[48,1536]{1,0:T(8,128)(2,1)S(1)}, u32[]{:S(2)}, u32[]{:S(2)}) collective-permute-start(bf16[48,1536]{1,0:T(8,128)(2,1)S(1)} %bitcast.360), channel_id=1, source_target_pairs={{0,4},{2,6},{4,0},{6,2},{1,5},{3,7},{5,1},{7,3},{8,12},{10,14},{12... | collective-permute-start | bytes 442376 | tf_op jit(solution)/shard_map/ppermute | solution.py:390
  33.7 29.2 %collective-permute-start.6 = (bf16[256,768]{1,0:T(8,128)(2,1)S(1)}, bf16[256,768]{1,0:T(8,128)(2,1)S(1)}, u32[]{:S(2)}, u32[]{:S(2)}) collective-permute-start(bf16[256,768]{1,0:T(8,128)(2,1)S(1)} %bitcast.338), channel_id=1, source_target_pairs={{0,4},{2,6},{4,0},{6,2},{1,5},{3,7},{5,1},{7,3},{8,12},{10,14},{12... | collective-permute-start | bytes 1179656 | tf_op jit(solution)/shard_map/ppermute | solution.py:390
  34.4 16.5 %collective-permute-start.10 = (bf16[2,32,1344]{2,1,0:T(8,128)(2,1)S(1)}, bf16[2,32,1344]{2,1,0:T(8,128)(2,1)S(1)}, u32[]{:S(2)}, u32[]{:S(2)}) collective-permute-start(bf16[2,32,1344]{2,1,0:T(8,128)(2,1)S(1)} %pad_maximum_fusion.10), channel_id=1, source_target_pairs={{0,16},{16,0},{1,17},{17,1},{2,18},{18,2},{3,19},{19,3},{4,20},{20... | collective-permute-start | bytes 516104 | tf_op jit(solution)/shard_map/ppermute | solution.py:390
  50.9 9.4 %collective-permute-start.23 = (bf16[48,1536]{1,0:T(8,128)(2,1)S(1)}, bf16[48,1536]{1,0:T(8,128)(2,1)S(1)}, u32[]{:S(2)}, u32[]{:S(2)}) collective-permute-start(bf16[48,1536]{1,0:T(8,128)(2,1)S(1)} %broadcast_select_fusion.5), channel_id=1, source_target_pairs={{4,6},{2,0},{5,7},{3,1},{12,14},{10,8},{13,15},{11,9},{20,22},{18,... | collective-permute-start | bytes 442376 | tf_op jit(solution)/shard_map/ppermute | solution.py:407
  55.0 24.2 %collective-permute-start.9 = (bf16[2,2,32,1344]{3,2,1,0:T(8,128)(2,1)S(1)}, bf16[2,2,32,1344]{3,2,1,0:T(8,128)(2,1)S(1)}, u32[]{:S(2)}, u32[]{:S(2)}) collective-permute-start(bf16[2,2,32,1344]{3,2,1,0:T(8,128)(2,1)S(1)} %pad_maximum_fusion.5), channel_id=1, source_target_pairs={{0,16},{16,0},{1,17},{17,1},{2,18},{18,2},{3,19},{19,3},{4,20},{20... | collective-permute-start | bytes 1032200 | tf_op jit(solution)/shard_map/ppermute | solution.py:390
  60.3 20.3 %collective-permute-start.11 = (bf16[2,2,32,1344]{3,2,1,0:T(8,128)(2,1)S(1)}, bf16[2,2,32,1344]{3,2,1,0:T(8,128)(2,1)S(1)}, u32[]{:S(2)}, u32[]{:S(2)}) collective-permute-start(bf16[2,2,32,1344]{3,2,1,0:T(8,128)(2,1)S(1)} %pad_maximum_fusion.6), channel_id=1, source_target_pairs={{0,8},{8,0},{1,9},{9,1},{2,10},{10,2},{3,11},{11,3},{4,12},{12,4},... | collective-permute-start | bytes 1032200 | tf_op jit(solution)/shard_map/ppermute | solution.py:390
  62.9 21.5 %collective-permute-start.24 = (bf16[2,48,1536]{2,1,0:T(8,128)(2,1)S(1)}, bf16[2,48,1536]{2,1,0:T(8,128)(2,1)S(1)}, u32[]{:S(2)}, u32[]{:S(2)}) collective-permute-start(bf16[2,48,1536]{2,1,0:T(8,128)(2,1)S(1)} %pad_maximum_fusion.7), channel_id=1, source_target_pairs={{0,8},{8,0},{1,9},{9,1},{2,10},{10,2},{3,11},{11,3},{4,12},{12,4},... | collective-permute-start | bytes 884744 | tf_op jit(solution)/shard_map/ppermute | solution.py:390
  70.6 14.7 %collective-permute-start.26 = (bf16[2,48,1536]{2,1,0:T(8,128)(2,1)S(1)}, bf16[2,48,1536]{2,1,0:T(8,128)(2,1)S(1)}, u32[]{:S(2)}, u32[]{:S(2)}) collective-permute-start(bf16[2,48,1536]{2,1,0:T(8,128)(2,1)S(1)} %pad_maximum_fusion.8), channel_id=1, source_target_pairs={{0,16},{16,0},{1,17},{17,1},{2,18},{18,2},{3,19},{19,3},{4,20},{20... | collective-permute-start | bytes 884744 | tf_op jit(solution)/shard_map/ppermute | solution.py:390
  73.7 9.4 %collective-permute-start.29 = (bf16[96,768]{1,0:T(8,128)(2,1)S(1)}, bf16[96,768]{1,0:T(8,128)(2,1)S(1)}, u32[]{:S(2)}, u32[]{:S(2)}) collective-permute-start(bf16[96,768]{1,0:T(8,128)(2,1)S(1)} %broadcast_select_fusion.4), channel_id=1, source_target_pairs={{0,4},{2,6},{4,0},{6,2},{1,5},{3,7},{5,1},{7,3},{8,12},{10,14},{12... | collective-permute-start | bytes 442376 | tf_op jit(solution)/shard_map/ppermute | solution.py:390
  79.2 20.5 %collective-permute-start.7 = (bf16[256,768]{1,0:T(8,128)(2,1)}, bf16[256,768]{1,0:T(8,128)(2,1)S(1)}, u32[]{:S(2)}, u32[]{:S(2)}) collective-permute-start(bf16[256,768]{1,0:T(8,128)(2,1)} %broadcast_select_fusion.2), channel_id=1, source_target_pairs={{4,6},{2,0},{5,7},{3,1},{12,14},{10,8},{13,15},{11,9},{20,22},{18,... | collective-permute-start | bytes 1179656 | tf_op jit(solution)/shard_map/ppermute | solution.py:407
  80.9 14.5 %collective-permute-start.12 = (bf16[2,2,4,32,1344]{4,3,2,1,0:T(8,128)(2,1)S(1)}, bf16[2,2,4,32,1344]{4,3,2,1,0:T(8,128)(2,1)S(1)}, u32[]{:S(2)}, u32[]{:S(2)}) collective-permute-start(bf16[2,2,4,32,1344]{4,3,2,1,0:T(8,128)(2,1)S(1)} %maximum_maximum_fusion.2), channel_id=1, source_target_pairs={{0,1},{1,0},{2,3},{3,2},{4,5},{5,4},{6,7},{7,6},{8,9},{9,8},{10,11... | collective-permute-start | bytes 4128776 | tf_op jit(solution)/shard_map/ppermute | solution.py:390
  83.1 11.5 %collective-permute-start.31 = (bf16[96,768]{1,0:T(8,128)(2,1)S(1)}, bf16[96,768]{1,0:T(8,128)(2,1)S(1)}, u32[]{:S(2)}, u32[]{:S(2)}) collective-permute-start(bf16[96,768]{1,0:T(8,128)(2,1)S(1)} %broadcast_select_fusion.3), channel_id=1, source_target_pairs={{4,6},{2,0},{5,7},{3,1},{12,14},{10,8},{13,15},{11,9},{20,22},{18,... | collective-permute-start | bytes 442376 | tf_op jit(solution)/shard_map/ppermute | solution.py:407
  108.8 8.9 %collective-permute-start.34 = (bf16[2,96,768]{2,1,0:T(8,128)(2,1)S(1)}, bf16[2,96,768]{2,1,0:T(8,128)(2,1)S(1)}, u32[]{:S(2)}, u32[]{:S(2)}) collective-permute-start(bf16[2,96,768]{2,1,0:T(8,128)(2,1)S(1)} %get-tuple-element.126), channel_id=1, source_target_pairs={{0,16},{16,0},{1,17},{17,1},{2,18},{18,2},{3,19},{19,3},{4,20},{20... | collective-permute-start | bytes 884744 | tf_op jit(solution)/shard_map/ppermute | solution.py:390
  110.2 18.2 %collective-permute-start.13 = (bf16[1024,384]{1,0:T(8,128)(2,1)S(1)}, bf16[1024,384]{1,0:T(8,128)(2,1)S(1)}, u32[]{:S(2)}, u32[]{:S(2)}) collective-permute-start(bf16[1024,384]{1,0:T(8,128)(2,1)S(1)} %get-tuple-element.48.mine_ref), channel_id=1, source_target_pairs={{0,1},{1,0},{2,3},{3,2},{4,5},{5,4},{6,7},{7,6},{8,9},{9,8},{10,11... | collective-permute-start | bytes 2359304 | tf_op jit(solution)/shard_map/ppermute | solution.py:390
  110.3 17.9 %collective-permute-start.25 = (bf16[2,2,48,1536]{3,2,1,0:T(8,128)(2,1)S(1)}, bf16[2,2,48,1536]{3,2,1,0:T(8,128)(2,1)S(1)}, u32[]{:S(2)}, u32[]{:S(2)}) collective-permute-start(bf16[2,2,48,1536]{3,2,1,0:T(8,128)(2,1)S(1)} %maximum_select_fusion), channel_id=1, source_target_pairs={{0,16},{16,0},{1,17},{17,1},{2,18},{18,2},{3,19},{19,3},{4,20},{20... | collective-permute-start | bytes 1769480 | tf_op jit(solution)/shard_map/ppermute | solution.py:390
  111.0 17.3 %collective-permute-start.27 = (bf16[2,2,48,1536]{3,2,1,0:T(8,128)(2,1)S(1)}, bf16[2,2,48,1536]{3,2,1,0:T(8,128)(2,1)S(1)}, u32[]{:S(2)}, u32[]{:S(2)}) collective-permute-start(bf16[2,2,48,1536]{3,2,1,0:T(8,128)(2,1)S(1)} %maximum_select_fusion.1), channel_id=1, source_target_pairs={{0,8},{8,0},{1,9},{9,1},{2,10},{10,2},{3,11},{11,3},{4,12},{12,4},... | collective-permute-start | bytes 1769480 | tf_op jit(solution)/shard_map/ppermute | solution.py:390
  149.0 17.3 %collective-permute-start.33 = (bf16[2,2,96,768]{3,2,1,0:T(8,128)(2,1)S(1)}, bf16[2,2,96,768]{3,2,1,0:T(8,128)(2,1)S(1)}, u32[]{:S(2)}, u32[]{:S(2)}) collective-permute-start(bf16[2,2,96,768]{3,2,1,0:T(8,128)(2,1)S(1)} %maximum_select_fusion.3), channel_id=1, source_target_pairs={{0,16},{16,0},{1,17},{17,1},{2,18},{18,2},{3,19},{19,3},{4,20},{20... | collective-permute-start | bytes 1769480 | tf_op jit(solution)/shard_map/ppermute | solution.py:390
  153.3 13.1 %collective-permute-start.35 = (bf16[2,2,96,768]{3,2,1,0:T(8,128)(2,1)S(1)}, bf16[2,2,96,768]{3,2,1,0:T(8,128)(2,1)S(1)}, u32[]{:S(2)}, u32[]{:S(2)}) collective-permute-start(bf16[2,2,96,768]{3,2,1,0:T(8,128)(2,1)S(1)} %maximum_select_fusion.4), channel_id=1, source_target_pairs={{0,8},{8,0},{1,9},{9,1},{2,10},{10,2},{3,11},{11,3},{4,12},{12,4},... | collective-permute-start | bytes 1769480 | tf_op jit(solution)/shard_map/ppermute | solution.py:390
  154.5 9.7 %collective-permute-start.15 = (bf16[256,192]{1,0:T(8,128)(2,1)S(1)}, bf16[256,192]{1,0:T(8,128)(2,1)S(1)}, u32[]{:S(2)}, u32[]{:S(2)}) collective-permute-start(bf16[256,192]{1,0:T(8,128)(2,1)S(1)} %get-tuple-element.136), channel_id=1, source_target_pairs={{0,4},{2,6},{4,0},{6,2},{1,5},{3,7},{5,1},{7,3},{8,12},{10,14},{12... | collective-permute-start | bytes 294920 | tf_op jit(solution)/shard_map/ppermute | solution.py:390
  176.9 16.3 %collective-permute-start.62 = (bf16[2,2,96,768]{3,2,1,0:T(8,128)(2,1)S(1)}, bf16[2,2,96,768]{3,2,1,0:T(8,128)(2,1)}, u32[]{:S(2)}, u32[]{:S(2)}) collective-permute-start(bf16[2,2,96,768]{3,2,1,0:T(8,128)(2,1)S(1)} %dynamic-slice_bitcast_fusion), channel_id=1, source_target_pairs={{0,8},{8,0},{1,9},{9,1},{2,10},{10,2},{3,11},{11,3},{4,12},{12,4},... | collective-permute-start | bytes 1769480 | tf_op jit(solution)/shard_map/ppermute | solution.py:390
  177.2 21.6 %collective-permute-start.60 = (bf16[2,2,96,768]{3,2,1,0:T(8,128)(2,1)S(1)}, bf16[2,2,96,768]{3,2,1,0:T(8,128)(2,1)}, u32[]{:S(2)}, u32[]{:S(2)}) collective-permute-start(bf16[2,2,96,768]{3,2,1,0:T(8,128)(2,1)S(1)} %dynamic-slice_bitcast_fusion.1), channel_id=1, source_target_pairs={{0,16},{16,0},{1,17},{17,1},{2,18},{18,2},{3,19},{19,3},{4,20},{20... | collective-permute-start | bytes 1769480 | tf_op jit(solution)/shard_map/ppermute | solution.py:390
  181.0 24.8 %collective-permute-start.54 = (bf16[2,2,48,1536]{3,2,1,0:T(8,128)(2,1)S(1)}, bf16[2,2,48,1536]{3,2,1,0:T(8,128)(2,1)S(1)}, u32[]{:S(2)}, u32[]{:S(2)}) collective-permute-start(bf16[2,2,48,1536]{3,2,1,0:T(8,128)(2,1)S(1)} %dynamic-slice_bitcast_fusion.2), channel_id=1, source_target_pairs={{0,8},{8,0},{1,9},{9,1},{2,10},{10,2},{3,11},{11,3},{4,12},{12,4},... | collective-permute-start | bytes 1769480 | tf_op jit(solution)/shard_map/ppermute | solution.py:390
  182.9 25.9 %collective-permute-start.52 = (bf16[2,2,48,1536]{3,2,1,0:T(8,128)(2,1)S(1)}, bf16[2,2,48,1536]{3,2,1,0:T(8,128)(2,1)S(1)}, u32[]{:S(2)}, u32[]{:S(2)}) collective-permute-start(bf16[2,2,48,1536]{3,2,1,0:T(8,128)(2,1)S(1)} %dynamic-slice_bitcast_fusion.3), channel_id=1, source_target_pairs={{0,16},{16,0},{1,17},{17,1},{2,18},{18,2},{3,19},{19,3},{4,20},{20... | collective-permute-start | bytes 1769480 | tf_op jit(solution)/shard_map/ppermute | solution.py:390
  194.5 40.9 %collective-permute-start.63 = (bf16[2,96,768]{2,1,0:T(8,128)(2,1)S(1)}, bf16[2,96,768]{2,1,0:T(8,128)(2,1)S(1)}, u32[]{:S(2)}, u32[]{:S(2)}) collective-permute-start(bf16[2,96,768]{2,1,0:T(8,128)(2,1)S(1)} %fusion.16), channel_id=1, source_target_pairs={{0,16},{16,0},{1,17},{17,1},{2,18},{18,2},{3,19},{19,3},{4,20},{20... | collective-permute-start | bytes 884744 | tf_op jit(solution)/shard_map/ppermute | solution.py:390
  200.1 35.4 %collective-permute-start.61 = (bf16[2,96,768]{2,1,0:T(8,128)(2,1)S(1)}, bf16[2,96,768]{2,1,0:T(8,128)(2,1)S(1)}, u32[]{:S(2)}, u32[]{:S(2)}) collective-permute-start(bf16[2,96,768]{2,1,0:T(8,128)(2,1)S(1)} %fusion.15), channel_id=1, source_target_pairs={{0,8},{8,0},{1,9},{9,1},{2,10},{10,2},{3,11},{11,3},{4,12},{12,4},... | collective-permute-start | bytes 884744 | tf_op jit(solution)/shard_map/ppermute | solution.py:390
  205.8 9.0 %collective-permute-start.38 = (bf16[256,192]{1,0:T(8,128)(2,1)S(1)}, bf16[256,192]{1,0:T(8,128)(2,1)S(1)}, u32[]{:S(2)}, u32[]{:S(2)}) collective-permute-start(bf16[256,192]{1,0:T(8,128)(2,1)S(1)} %get-tuple-element.58), channel_id=1, source_target_pairs={{0,4},{2,6},{4,0},{6,2},{1,5},{3,7},{5,1},{7,3},{8,12},{10,14},{12... | collective-permute-start | bytes 294920 | tf_op jit(solution)/shard_map/ppermute | solution.py:390
  208.7 27.1 %collective-permute-start.55 = (bf16[2,48,1536]{2,1,0:T(8,128)(2,1)S(1)}, bf16[2,48,1536]{2,1,0:T(8,128)(2,1)S(1)}, u32[]{:S(2)}, u32[]{:S(2)}) collective-permute-start(bf16[2,48,1536]{2,1,0:T(8,128)(2,1)S(1)} %fusion.14), channel_id=1, source_target_pairs={{0,16},{16,0},{1,17},{17,1},{2,18},{18,2},{3,19},{19,3},{4,20},{20... | collective-permute-start | bytes 884744 | tf_op jit(solution)/shard_map/ppermute | solution.py:390
  210.8 28.8 %collective-permute-start.53 = (bf16[2,48,1536]{2,1,0:T(8,128)(2,1)S(1)}, bf16[2,48,1536]{2,1,0:T(8,128)(2,1)S(1)}, u32[]{:S(2)}, u32[]{:S(2)}) collective-permute-start(bf16[2,48,1536]{2,1,0:T(8,128)(2,1)S(1)} %fusion.13), channel_id=1, source_target_pairs={{0,8},{8,0},{1,9},{9,1},{2,10},{10,2},{3,11},{11,3},{4,12},{12,4},... | collective-permute-start | bytes 884744 | tf_op jit(solution)/shard_map/ppermute | solution.py:390
  235.7 14.2 %collective-permute-start.64 = (bf16[96,768]{1,0:T(8,128)(2,1)S(1)}, bf16[96,768]{1,0:T(8,128)(2,1)S(1)}, u32[]{:S(2)}, u32[]{:S(2)}) collective-permute-start(bf16[96,768]{1,0:T(8,128)(2,1)S(1)} %get-tuple-element.97), channel_id=1, source_target_pairs={{0,2},{2,4},{4,6},{6,0},{1,3},{3,5},{5,7},{7,1},{8,10},{10,12},{12... | collective-permute-start | bytes 442376 | tf_op jit(solution)/shard_map/ppermute | solution.py:390
  235.8 17.0 %collective-permute-start.65 = (bf16[96,768]{1,0:T(8,128)(2,1)S(1)}, bf16[96,768]{1,0:T(8,128)(2,1)S(1)}, u32[]{:S(2)}, u32[]{:S(2)}) collective-permute-start(bf16[96,768]{1,0:T(8,128)(2,1)S(1)} %get-tuple-element.98), channel_id=1, source_target_pairs={{0,4},{2,6},{4,0},{6,2},{1,5},{3,7},{5,1},{7,3},{8,12},{10,14},{12... | collective-permute-start | bytes 442376 | tf_op jit(solution)/shard_map/ppermute | solution.py:390
  235.9 16.9 %collective-permute-start.66 = (bf16[96,768]{1,0:T(8,128)(2,1)S(1)}, bf16[96,768]{1,0:T(8,128)(2,1)S(1)}, u32[]{:S(2)}, u32[]{:S(2)}) collective-permute-start(bf16[96,768]{1,0:T(8,128)(2,1)S(1)} %get-tuple-element.99), channel_id=1, source_target_pairs={{0,6},{2,0},{4,2},{6,4},{1,7},{3,1},{5,3},{7,5},{8,14},{10,8},{12,... | collective-permute-start | bytes 442376 | tf_op jit(solution)/shard_map/ppermute | solution.py:390
  239.9 14.0 %collective-permute-start.56 = (bf16[48,1536]{1,0:T(8,128)(2,1)S(1)}, bf16[48,1536]{1,0:T(8,128)(2,1)S(1)}, u32[]{:S(2)}, u32[]{:S(2)}) collective-permute-start(bf16[48,1536]{1,0:T(8,128)(2,1)S(1)} %get-tuple-element.100), channel_id=1, source_target_pairs={{0,2},{2,4},{4,6},{6,0},{1,3},{3,5},{5,7},{7,1},{8,10},{10,12},{12... | collective-permute-start | bytes 442376 | tf_op jit(solution)/shard_map/ppermute | solution.py:390
  240.5 21.9 %collective-permute-start.57 = (bf16[48,1536]{1,0:T(8,128)(2,1)S(1)}, bf16[48,1536]{1,0:T(8,128)(2,1)S(1)}, u32[]{:S(2)}, u32[]{:S(2)}) collective-permute-start(bf16[48,1536]{1,0:T(8,128)(2,1)S(1)} %get-tuple-element.101), channel_id=1, source_target_pairs={{0,4},{2,6},{4,0},{6,2},{1,5},{3,7},{5,1},{7,3},{8,12},{10,14},{12... | collective-permute-start | bytes 442376 | tf_op jit(solution)/shard_map/ppermute | solution.py:390
  249.9 12.5 %collective-permute-start.58 = (bf16[48,1536]{1,0:T(8,128)(2,1)S(1)}, bf16[48,1536]{1,0:T(8,128)(2,1)S(1)}, u32[]{:S(2)}, u32[]{:S(2)}) collective-permute-start(bf16[48,1536]{1,0:T(8,128)(2,1)S(1)} %get-tuple-element.102), channel_id=1, source_target_pairs={{0,6},{2,0},{4,2},{6,4},{1,7},{3,1},{5,3},{7,5},{8,14},{10,8},{12,... | collective-permute-start | bytes 442376 | tf_op jit(solution)/shard_map/ppermute | solution.py:390
  252.8 15.6 %collective-permute-start.44 = (bf16[16,32,1344]{2,1,0:T(8,128)(2,1)}, bf16[16,32,1344]{2,1,0:T(8,128)(2,1)}, u32[]{:S(2)}, u32[]{:S(2)}) collective-permute-start(bf16[16,32,1344]{2,1,0:T(8,128)(2,1)} %get-tuple-element.77), channel_id=1, source_target_pairs={{0,1},{1,0},{2,3},{3,2},{4,5},{5,4},{6,7},{7,6},{8,9},{9,8},{10,11... | collective-permute-start | bytes 4128776 | tf_op jit(solution)/shard_map/ppermute | solution.py:390
  270.4 13.3 %collective-permute-start.47 = (bf16[2,2,32,1344]{3,2,1,0:T(8,128)(2,1)S(1)}, bf16[2,2,32,1344]{3,2,1,0:T(8,128)(2,1)S(1)}, u32[]{:S(2)}, u32[]{:S(2)}) collective-permute-start(bf16[2,2,32,1344]{3,2,1,0:T(8,128)(2,1)S(1)} %fusion.12), channel_id=1, source_target_pairs={{0,8},{8,0},{1,9},{9,1},{2,10},{10,2},{3,11},{11,3},{4,12},{12,4},... | collective-permute-start | bytes 1032200 | tf_op jit(solution)/shard_map/ppermute | solution.py:390
  275.6 26.3 %collective-permute-start.41 = (bf16[256,768]{1,0:T(8,128)(2,1)S(1)}, bf16[256,768]{1,0:T(8,128)(2,1)S(1)}, u32[]{:S(2)}, u32[]{:S(2)}) collective-permute-start(bf16[256,768]{1,0:T(8,128)(2,1)S(1)} %get-tuple-element.96), channel_id=1, source_target_pairs={{0,2},{2,4},{4,6},{6,0},{1,3},{3,5},{5,7},{7,1},{8,10},{10,12},{12... | collective-permute-start | bytes 1179656 | tf_op jit(solution)/shard_map/ppermute | solution.py:390
  278.9 27.9 %collective-permute-start.42 = (bf16[256,768]{1,0:T(8,128)(2,1)}, bf16[256,768]{1,0:T(8,128)(2,1)S(1)}, u32[]{:S(2)}, u32[]{:S(2)}) collective-permute-start(bf16[256,768]{1,0:T(8,128)(2,1)} %get-tuple-element.95), channel_id=1, source_target_pairs={{0,4},{2,6},{4,0},{6,2},{1,5},{3,7},{5,1},{7,3},{8,12},{10,14},{12... | collective-permute-start | bytes 1179656 | tf_op jit(solution)/shard_map/ppermute | solution.py:390
  279.3 27.6 %collective-permute-start.43 = (bf16[256,768]{1,0:T(8,128)(2,1)}, bf16[256,768]{1,0:T(8,128)(2,1)S(1)}, u32[]{:S(2)}, u32[]{:S(2)}) collective-permute-start(bf16[256,768]{1,0:T(8,128)(2,1)} %get-tuple-element.94), channel_id=1, source_target_pairs={{0,6},{2,0},{4,2},{6,4},{1,7},{3,1},{5,3},{7,5},{8,14},{10,8},{12,... | collective-permute-start | bytes 1179656 | tf_op jit(solution)/shard_map/ppermute | solution.py:390
  281.3 11.4 %collective-permute-start.45 = (bf16[2,2,32,1344]{3,2,1,0:T(8,128)(2,1)S(1)}, bf16[2,2,32,1344]{3,2,1,0:T(8,128)(2,1)S(1)}, u32[]{:S(2)}, u32[]{:S(2)}) collective-permute-start(bf16[2,2,32,1344]{3,2,1,0:T(8,128)(2,1)S(1)} %fusion.11), channel_id=1, source_target_pairs={{0,16},{16,0},{1,17},{17,1},{2,18},{18,2},{3,19},{19,3},{4,20},{20... | collective-permute-start | bytes 1032200 | tf_op jit(solution)/shard_map/ppermute | solution.py:390
  283.9 11.4 %collective-permute-start.48 = (bf16[2,32,1344]{2,1,0:T(8,128)(2,1)S(1)}, bf16[2,32,1344]{2,1,0:T(8,128)(2,1)S(1)}, u32[]{:S(2)}, u32[]{:S(2)}) collective-permute-start(bf16[2,32,1344]{2,1,0:T(8,128)(2,1)S(1)} %fusion.40), channel_id=1, source_target_pairs={{0,16},{16,0},{1,17},{17,1},{2,18},{18,2},{3,19},{19,3},{4,20},{20... | collective-permute-start | bytes 516104 | tf_op jit(solution)/shard_map/ppermute | solution.py:390
  299.3 9.7 %collective-permute-start.49 = (bf16[32,1344]{1,0:T(8,128)(2,1)}, bf16[32,1344]{1,0:T(8,128)(2,1)S(1)}, u32[]{:S(2)}, u32[]{:S(2)}) collective-permute-start(bf16[32,1344]{1,0:T(8,128)(2,1)} %get-tuple-element.156), channel_id=1, source_target_pairs={{0,2},{2,4},{4,6},{6,0},{1,3},{3,5},{5,7},{7,1},{8,10},{10,12},{12... | collective-permute-start | bytes 258056 | tf_op jit(solution)/shard_map/ppermute | solution.py:390
  299.3 20.6 %collective-permute-start.50 = (bf16[32,1344]{1,0:T(8,128)(2,1)}, bf16[32,1344]{1,0:T(8,128)(2,1)S(1)}, u32[]{:S(2)}, u32[]{:S(2)}) collective-permute-start(bf16[32,1344]{1,0:T(8,128)(2,1)} %get-tuple-element.155), channel_id=1, source_target_pairs={{0,4},{2,6},{4,0},{6,2},{1,5},{3,7},{5,1},{7,3},{8,12},{10,14},{12... | collective-permute-start | bytes 258056 | tf_op jit(solution)/shard_map/ppermute | solution.py:390
  301.9 18.0 %collective-permute-start.51 = (bf16[32,1344]{1,0:T(8,128)(2,1)}, bf16[32,1344]{1,0:T(8,128)(2,1)}, u32[]{:S(2)}, u32[]{:S(2)}) collective-permute-start(bf16[32,1344]{1,0:T(8,128)(2,1)} %get-tuple-element.154), channel_id=1, source_target_pairs={{0,6},{2,0},{4,2},{6,4},{1,7},{3,1},{5,3},{7,5},{8,14},{10,8},{12,... | collective-permute-start | bytes 258056 | tf_op jit(solution)/shard_map/ppermute | solution.py:390
  (49 other events, 302.8 us)
